TPU v7x, 32 devices: a whole 2x2x4 slice. The times are simulated.
32 devices in a mesh: groups: 2 (over x), seq: 16 (over z, y, core).
Axes of the slice: x: 2, y: 2, z: 4, core: 2. Of those that a mesh axis runs over, the one named last changes fastest.
Arguments:
- inputs: bfloat16 [4096, 2048], P(('groups', 'seq')), parts along dimension 0, may hold values from -0.015625 to 0.015625
- grad_out: bfloat16 [4096, 2048], P(('groups', 'seq')), parts along dimension 0, may hold values from -6 to 6
- filter_weight: float32 [32, 2048], replicated, may hold values from -0.0625 to 0.0625
- filter_rates: float32 [32], replicated, may hold values from 9.765625e-05 to 0.03
- filter_freqs: float32 [32], replicated, may hold values from 0 to 3
- skip_gain: float32 [2048], replicated, may hold values from 0.1 to 1.9
- span_of_slot: int32 [64], P('groups'), parts along dimension 0, may hold values from 0 to 31, as said below
Outputs:
- input_grad: bfloat16 [4096, 2048], P(('groups', 'seq')), parts along dimension 0
- filter_weight_grad: float32 [64, 2048], P('groups', 'seq'), parts along dimension 0
There are 2 independent parts, one for each index of `groups`. A program takes and returns all parts, laid end to end along the dimension named above; an argument that names none is the same for every part. Nothing has to cross between parts.
Inputs may be any that keep to these rules, and one draw needn't show every extreme that they name: `span_of_slot`: each span number appears once; the two row blocks of one device (slots 2 i and 2 i + 1) hold spans c and 31 - c for some c, in either order.
All inputs are finite; a program needn't handle non-finite values.
Results may differ from a plain program's by a relative error of at most 0.001.
Values may be sent and summed in bfloat16 or wider, within the bound.
No kernel may reach another device: no remote copies, remote signals or barrier semaphores. Data moves between devices by JAX's collectives and lax.ppermute only.
A program may use at most 64 MiB of HBM per device.

v0:
```python
import math

import jax
import jax.numpy as jnp
from jax import lax
from jax.sharding import PartitionSpec as P

HIGHEST_PRECISION = lax.Precision.HIGHEST


def shifted(value, axis, by):
    peers = lax.axis_size(axis)
    return lax.ppermute(value, axis, [(i, (i + by) % peers) for i in range(peers)])


def matmul(left, right):
    return jnp.dot(left, right, precision=HIGHEST_PRECISION, preferred_element_type=jnp.float32)


def left_transposed(left, right):
    return lax.dot_general(
        left,
        right,
        (((0,), (0,)), ((), ())),
        precision=HIGHEST_PRECISION,
        preferred_element_type=jnp.float32,
    )


def forward_tables(half_rows):
    spectrum_len = 2 * half_rows
    row_index = lax.broadcasted_iota(jnp.int32, (half_rows, spectrum_len), 0)
    col_index = lax.broadcasted_iota(jnp.int32, (half_rows, spectrum_len), 1)
    angles = (row_index * col_index % spectrum_len).astype(jnp.float32) * (
        2.0 * math.pi / spectrum_len
    )
    parity = jnp.where(col_index % 2 == 0, 1.0, -1.0).astype(jnp.float32)
    cosine = jnp.cos(angles)
    sine_part = jnp.where(row_index == 0, parity, -jnp.sin(angles))
    return (cosine, sine_part)


def inverse_tables(half_rows):
    spectrum_len = 2 * half_rows
    row_index = lax.broadcasted_iota(jnp.int32, (half_rows, half_rows), 0)
    col_index = lax.broadcasted_iota(jnp.int32, (half_rows, half_rows), 1)
    angles = (row_index * col_index % spectrum_len).astype(jnp.float32) * (
        2.0 * math.pi / spectrum_len
    )
    parity = jnp.where(row_index % 2 == 0, 1.0, -1.0).astype(jnp.float32)
    real_back = jnp.where(col_index == 0, 1.0, 2.0 * jnp.cos(angles)) / spectrum_len
    imag_back = jnp.where(col_index == 0, parity, -2.0 * jnp.sin(angles)) / spectrum_len
    return (real_back, imag_back)


def conj_product(left_real, left_imag, right_real, right_imag, first_row):
    product_ii = left_imag * right_imag
    real_part = left_real * right_real + jnp.where(first_row, 0.0, product_ii)
    imag_part = jnp.where(first_row, product_ii, left_real * right_imag - left_imag * right_real)
    return (real_part, imag_part)


def filter_window(span_gap, half_rows, length, filter_rates, filter_freqs):
    offsets = lax.broadcasted_iota(jnp.int32, (2 * half_rows, 1), 0)
    lag_steps = (span_gap - 1) * half_rows + offsets
    inside = (lag_steps >= 0) & (lag_steps < length)
    lag_float = jnp.maximum(lag_steps, 0).astype(jnp.float32)
    values = jnp.exp(-lag_float * filter_rates[None, :]) * jnp.cos(
        lag_float * filter_freqs[None, :]
    )
    return jnp.where(inside, values, 0.0)


def on_device(inputs, grad_out, filter_weight, filter_rates, filter_freqs, skip_gain, span_of_slot):
    rows_dev = inputs.shape[0]
    half_rows = rows_dev // 2
    devices = lax.axis_size("seq")
    length = rows_dev * devices
    position = lax.axis_index("seq")
    cosine, sine_part = forward_tables(half_rows)
    real_back, imag_back = inverse_tables(half_rows)
    first_row = lax.broadcasted_iota(jnp.int32, (half_rows, 1), 0) == 0
    freq_weight = jnp.where(first_row, 1.0, 2.0) / (2 * half_rows)
    own_spans = [span_of_slot[2 * position], span_of_slot[2 * position + 1]]
    own_values = inputs.astype(jnp.float32)
    own_spectra = []
    for slot_index in range(2):
        block_rows = own_values[slot_index * half_rows : (slot_index + 1) * half_rows]
        own_spectra.append(
            (
                matmul(cosine[:, :half_rows], block_rows),
                matmul(sine_part[:, :half_rows], block_rows),
            )
        )

    def absorb(running, block, source):
        values = block.astype(jnp.float32)
        totals = list(running[:4])
        weight_grad = running[4]
        for incoming in range(2):
            block_rows = values[incoming * half_rows : (incoming + 1) * half_rows]
            grad_real = matmul(cosine[:, half_rows:], block_rows)
            grad_imag = matmul(sine_part[:, half_rows:], block_rows)
            span_later = span_of_slot[2 * source + incoming]
            for slot_index in range(2):
                span_gap = span_later - own_spans[slot_index]
                own_real, own_imag = own_spectra[slot_index]

                def update(partial_value):
                    sum_real, sum_imag, grad_sum = partial_value
                    window = filter_window(span_gap, half_rows, length, filter_rates, filter_freqs)
                    basis_real = matmul(cosine, window)
                    basis_imag = matmul(sine_part, window)
                    filter_real = matmul(basis_real, filter_weight)
                    filter_imag = matmul(basis_imag, filter_weight)
                    add_real, add_imag = conj_product(
                        filter_real, filter_imag, grad_real, grad_imag, first_row
                    )
                    cross_real, cross_imag = conj_product(
                        own_real, own_imag, grad_real, grad_imag, first_row
                    )
                    grad_sum = (
                        grad_sum
                        + left_transposed(basis_real * freq_weight, cross_real)
                        + left_transposed(basis_imag * freq_weight, cross_imag)
                    )
                    return (sum_real + add_real, sum_imag + add_imag, grad_sum)

                partial_value = (totals[2 * slot_index], totals[2 * slot_index + 1], weight_grad)
                partial_value = lax.cond(
                    span_gap >= 0, update, lambda unchanged: unchanged, partial_value
                )
                totals[2 * slot_index], totals[2 * slot_index + 1], weight_grad = partial_value
        return (totals[0], totals[1], totals[2], totals[3], weight_grad)

    empty_block = jnp.zeros((half_rows, filter_weight.shape[1]), jnp.float32)
    running = (
        empty_block,
        empty_block,
        empty_block,
        empty_block,
        jnp.zeros(filter_weight.shape, jnp.float32),
    )
    running = absorb(running, grad_out, position)

    def cycle_turn(cycle_step, carried):
        block, partial_value = carried
        block = shifted(block, "seq", 1)
        return (block, absorb(partial_value, block, (position - cycle_step) % devices))

    running = lax.fori_loop(1, devices, cycle_turn, (grad_out, running))[1]
    grad_values = grad_out.astype(jnp.float32)
    restored = []
    for slot_index in range(2):
        spatial = matmul(real_back, running[2 * slot_index]) + matmul(
            imag_back, running[2 * slot_index + 1]
        )
        restored.append(
            spatial
            + skip_gain[None, :]
            * grad_values[slot_index * half_rows : (slot_index + 1) * half_rows]
        )
    input_grad = jnp.concatenate(restored, axis=0).astype(jnp.bfloat16)
    weight_grad = lax.psum_scatter(running[4], "seq", scatter_dimension=1, tiled=True)
    return (input_grad, weight_grad)


def solution(mesh):
    placed = (
        P(("groups", "seq"), None),
        P(("groups", "seq"), None),
        P(),
        P(),
        P(),
        P(),
        P("groups"),
    )
    return jax.shard_map(
        on_device,
        mesh=mesh,
        in_specs=placed,
        out_specs=(P(("groups", "seq"), None), P("groups", "seq")),
        check_vma=False,
    )
```

profile of v0, /device:TPU:8, one launch (start us, length us, event | category | flops | bytes accessed | tf_op | source)
XLA Modules:
  0.0 595.1 jit_solution(11698199382936403795)
XLA Ops:
  22.9 6.1 %conditional.6 = (f32[64,2048]{1,0:T(8,128)}, f32[64,2048]{1,0:T(8,128)}, f32[32,2048]{1,0:T(8,128)}) conditional(s32[]{:T(128)} %convert_element_type.210, f32[32,2048]{1,0:T(8,128)} %convolution_add_fusion.16, (s32[]{:T(128)}, f32[32]{0:T(128)S(1)}, f32[32]{0:T(128)S(1)}, f32[64,128]{1,0:T(8,128)S(1)}, f32[32,2048]{1,0:T(8,128)S(1)}, ...), branch_computations={%region_0.1_spmd, %region_1.2_spmd} | conditional | flops 210015616 | bytes 9032380 | solution.py:130
  29.1 3.9 select_add_fusion.6
  38.0 469.7 %while.27 = (s32[]{:T(128)}, bf16[128,2048]{1,0:T(8,128)(2,1)}, f32[64,2048]{1,0:T(8,128)S(1)}, f32[64,2048]{1,0:T(8,128)S(1)}, f32[64,2048]{1,0:T(8,128)}, /*in...) while((s32[]{:T(128)}, bf16[128,2048]{1,0:T(8,128)(2,1)}, ...), condition=%wide.region_13.14_spmd.clone.clone, body=%wide.region_4.13_spmd.clone.clone.sunk | while | flops 1243764480 | bytes 92885984 | solution.py:151
  45.6 2.9 collective-permute-done
  50.7 7.3 %conditional.21 = ((f32[64,2048]{1,0:T(8,128)}, f32[64,2048]{1,0:T(8,128)}, f32[32,2048]{1,0:T(8,128)})) conditional(s32[]{:T(128)} %convert_element_type.271, (f32[64,2048]{1,0:T(8,128)}, f32[64,2048]{1,0:T(8,128)}, f32[32,2048]{1,0:T(8,128)}) %tuple.142, (s32[]{:T(128)}, f32[32]{0:T(128)S(1)}, f32[32]{0:T(128)S(1)}, f32[64,128]{1,0:T(8,128)S(1)}, ...), branch_computations={%region_7.7_spmd, %region_8.8_spmd} | conditional | flops 210277760 | bytes 18469684 | solution.py:130
  60.0 7.3 %conditional.23 = ((f32[64,2048]{1,0:T(8,128)}, f32[64,2048]{1,0:T(8,128)}, f32[32,2048]{1,0:T(8,128)})) conditional(s32[]{:T(128)} %convert_element_type.272, (f32[64,2048]{1,0:T(8,128)}, f32[64,2048]{1,0:T(8,128)}, f32[32,2048]{1,0:T(8,128)}) %tuple.146, (s32[]{:T(128)}, f32[32]{0:T(128)S(1)}, f32[32]{0:T(128)S(1)}, f32[64,128]{1,0:T(8,128)S(1)}, ...), branch_computations={%region_11.11_spmd, %region_12.12_spmd} | conditional | flops 210277760 | bytes 18469684 | solution.py:130
  67.3 2.0 copy.60
  75.8 4.0 collective-permute-done
  83.9 7.4 %conditional.22 = ((f32[64,2048]{1,0:T(8,128)}, f32[64,2048]{1,0:T(8,128)}, f32[32,2048]{1,0:T(8,128)})) conditional(s32[]{:T(128)} %convert_element_type.269, (f32[64,2048]{1,0:T(8,128)}, f32[64,2048]{1,0:T(8,128)}, f32[32,2048]{1,0:T(8,128)}) %tuple.144, (s32[]{:T(128)}, f32[32]{0:T(128)S(1)}, f32[32]{0:T(128)S(1)}, f32[64,128]{1,0:T(8,128)S(1)}, ...), branch_computations={%region_9.9_spmd, %region_10.10_spmd} | conditional | flops 210277760 | bytes 18469684 | solution.py:130
  91.3 7.3 %conditional.23 = ((f32[64,2048]{1,0:T(8,128)}, f32[64,2048]{1,0:T(8,128)}, f32[32,2048]{1,0:T(8,128)})) conditional(s32[]{:T(128)} %convert_element_type.272, (f32[64,2048]{1,0:T(8,128)}, f32[64,2048]{1,0:T(8,128)}, f32[32,2048]{1,0:T(8,128)}) %tuple.146, (s32[]{:T(128)}, f32[32]{0:T(128)S(1)}, f32[32]{0:T(128)S(1)}, f32[64,128]{1,0:T(8,128)S(1)}, ...), branch_computations={%region_11.11_spmd, %region_12.12_spmd} | conditional | flops 210277760 | bytes 18469684 | solution.py:130
  98.6 2.0 copy.60
  107.1 4.0 collective-permute-done
  113.3 7.4 %conditional.21 = ((f32[64,2048]{1,0:T(8,128)}, f32[64,2048]{1,0:T(8,128)}, f32[32,2048]{1,0:T(8,128)})) conditional(s32[]{:T(128)} %convert_element_type.271, (f32[64,2048]{1,0:T(8,128)}, f32[64,2048]{1,0:T(8,128)}, f32[32,2048]{1,0:T(8,128)}) %tuple.142, (s32[]{:T(128)}, f32[32]{0:T(128)S(1)}, f32[32]{0:T(128)S(1)}, f32[64,128]{1,0:T(8,128)S(1)}, ...), branch_computations={%region_7.7_spmd, %region_8.8_spmd} | conditional | flops 210277760 | bytes 18469684 | solution.py:130
  122.6 7.3 %conditional.23 = ((f32[64,2048]{1,0:T(8,128)}, f32[64,2048]{1,0:T(8,128)}, f32[32,2048]{1,0:T(8,128)})) conditional(s32[]{:T(128)} %convert_element_type.272, (f32[64,2048]{1,0:T(8,128)}, f32[64,2048]{1,0:T(8,128)}, f32[32,2048]{1,0:T(8,128)}) %tuple.146, (s32[]{:T(128)}, f32[32]{0:T(128)S(1)}, f32[32]{0:T(128)S(1)}, f32[64,128]{1,0:T(8,128)S(1)}, ...), branch_computations={%region_11.11_spmd, %region_12.12_spmd} | conditional | flops 210277760 | bytes 18469684 | solution.py:130
  129.9 2.0 copy.60
  138.4 4.0 collective-permute-done
  146.5 7.4 %conditional.22 = ((f32[64,2048]{1,0:T(8,128)}, f32[64,2048]{1,0:T(8,128)}, f32[32,2048]{1,0:T(8,128)})) conditional(s32[]{:T(128)} %convert_element_type.269, (f32[64,2048]{1,0:T(8,128)}, f32[64,2048]{1,0:T(8,128)}, f32[32,2048]{1,0:T(8,128)}) %tuple.144, (s32[]{:T(128)}, f32[32]{0:T(128)S(1)}, f32[32]{0:T(128)S(1)}, f32[64,128]{1,0:T(8,128)S(1)}, ...), branch_computations={%region_9.9_spmd, %region_10.10_spmd} | conditional | flops 210277760 | bytes 18469684 | solution.py:130
  153.9 7.3 %conditional.23 = ((f32[64,2048]{1,0:T(8,128)}, f32[64,2048]{1,0:T(8,128)}, f32[32,2048]{1,0:T(8,128)})) conditional(s32[]{:T(128)} %convert_element_type.272, (f32[64,2048]{1,0:T(8,128)}, f32[64,2048]{1,0:T(8,128)}, f32[32,2048]{1,0:T(8,128)}) %tuple.146, (s32[]{:T(128)}, f32[32]{0:T(128)S(1)}, f32[32]{0:T(128)S(1)}, f32[64,128]{1,0:T(8,128)S(1)}, ...), branch_computations={%region_11.11_spmd, %region_12.12_spmd} | conditional | flops 210277760 | bytes 18469684 | solution.py:130
  161.2 2.0 copy.60
  169.7 4.0 collective-permute-done
  175.9 7.4 %conditional.20 = ((f32[64,2048]{1,0:T(8,128)}, f32[64,2048]{1,0:T(8,128)}, f32[32,2048]{1,0:T(8,128)})) conditional(s32[]{:T(128)} %convert_element_type.270, (f32[64,2048]{1,0:T(8,128)}, f32[64,2048]{1,0:T(8,128)}, f32[32,2048]{1,0:T(8,128)}) %tuple.182, (s32[]{:T(128)}, f32[32]{0:T(128)S(1)}, f32[32]{0:T(128)S(1)}, f32[64,128]{1,0:T(8,128)S(1)}, ...), branch_computations={%region_5.5_spmd, %region_6.6_spmd} | conditional | flops 210277760 | bytes 18469684 | solution.py:130
  183.2 7.3 %conditional.21 = ((f32[64,2048]{1,0:T(8,128)}, f32[64,2048]{1,0:T(8,128)}, f32[32,2048]{1,0:T(8,128)})) conditional(s32[]{:T(128)} %convert_element_type.271, (f32[64,2048]{1,0:T(8,128)}, f32[64,2048]{1,0:T(8,128)}, f32[32,2048]{1,0:T(8,128)}) %tuple.142, (s32[]{:T(128)}, f32[32]{0:T(128)S(1)}, f32[32]{0:T(128)S(1)}, f32[64,128]{1,0:T(8,128)S(1)}, ...), branch_computations={%region_7.7_spmd, %region_8.8_spmd} | conditional | flops 210277760 | bytes 18469684 | solution.py:130
  192.5 2.0 copy.60
  201.0 4.0 collective-permute-done
  207.2 7.4 %conditional.21 = ((f32[64,2048]{1,0:T(8,128)}, f32[64,2048]{1,0:T(8,128)}, f32[32,2048]{1,0:T(8,128)})) conditional(s32[]{:T(128)} %convert_element_type.271, (f32[64,2048]{1,0:T(8,128)}, f32[64,2048]{1,0:T(8,128)}, f32[32,2048]{1,0:T(8,128)}) %tuple.142, (s32[]{:T(128)}, f32[32]{0:T(128)S(1)}, f32[32]{0:T(128)S(1)}, f32[64,128]{1,0:T(8,128)S(1)}, ...), branch_computations={%region_7.7_spmd, %region_8.8_spmd} | conditional | flops 210277760 | bytes 18469684 | solution.py:130
  216.4 7.3 %conditional.23 = ((f32[64,2048]{1,0:T(8,128)}, f32[64,2048]{1,0:T(8,128)}, f32[32,2048]{1,0:T(8,128)})) conditional(s32[]{:T(128)} %convert_element_type.272, (f32[64,2048]{1,0:T(8,128)}, f32[64,2048]{1,0:T(8,128)}, f32[32,2048]{1,0:T(8,128)}) %tuple.146, (s32[]{:T(128)}, f32[32]{0:T(128)S(1)}, f32[32]{0:T(128)S(1)}, f32[64,128]{1,0:T(8,128)S(1)}, ...), branch_computations={%region_11.11_spmd, %region_12.12_spmd} | conditional | flops 210277760 | bytes 18469684 | solution.py:130
  223.8 2.0 copy.60
  232.3 4.0 collective-permute-done
  240.4 7.4 %conditional.22 = ((f32[64,2048]{1,0:T(8,128)}, f32[64,2048]{1,0:T(8,128)}, f32[32,2048]{1,0:T(8,128)})) conditional(s32[]{:T(128)} %convert_element_type.269, (f32[64,2048]{1,0:T(8,128)}, f32[64,2048]{1,0:T(8,128)}, f32[32,2048]{1,0:T(8,128)}) %tuple.144, (s32[]{:T(128)}, f32[32]{0:T(128)S(1)}, f32[32]{0:T(128)S(1)}, f32[64,128]{1,0:T(8,128)S(1)}, ...), branch_computations={%region_9.9_spmd, %region_10.10_spmd} | conditional | flops 210277760 | bytes 18469684 | solution.py:130
  247.7 7.3 %conditional.23 = ((f32[64,2048]{1,0:T(8,128)}, f32[64,2048]{1,0:T(8,128)}, f32[32,2048]{1,0:T(8,128)})) conditional(s32[]{:T(128)} %convert_element_type.272, (f32[64,2048]{1,0:T(8,128)}, f32[64,2048]{1,0:T(8,128)}, f32[32,2048]{1,0:T(8,128)}) %tuple.146, (s32[]{:T(128)}, f32[32]{0:T(128)S(1)}, f32[32]{0:T(128)S(1)}, f32[64,128]{1,0:T(8,128)S(1)}, ...), branch_computations={%region_11.11_spmd, %region_12.12_spmd} | conditional | flops 210277760 | bytes 18469684 | solution.py:130
  255.1 2.0 copy.60
  263.6 4.0 collective-permute-done
  271.7 7.4 %conditional.22 = ((f32[64,2048]{1,0:T(8,128)}, f32[64,2048]{1,0:T(8,128)}, f32[32,2048]{1,0:T(8,128)})) conditional(s32[]{:T(128)} %convert_element_type.269, (f32[64,2048]{1,0:T(8,128)}, f32[64,2048]{1,0:T(8,128)}, f32[32,2048]{1,0:T(8,128)}) %tuple.144, (s32[]{:T(128)}, f32[32]{0:T(128)S(1)}, f32[32]{0:T(128)S(1)}, f32[64,128]{1,0:T(8,128)S(1)}, ...), branch_computations={%region_9.9_spmd, %region_10.10_spmd} | conditional | flops 210277760 | bytes 18469684 | solution.py:130
  279.0 7.3 %conditional.23 = ((f32[64,2048]{1,0:T(8,128)}, f32[64,2048]{1,0:T(8,128)}, f32[32,2048]{1,0:T(8,128)})) conditional(s32[]{:T(128)} %convert_element_type.272, (f32[64,2048]{1,0:T(8,128)}, f32[64,2048]{1,0:T(8,128)}, f32[32,2048]{1,0:T(8,128)}) %tuple.146, (s32[]{:T(128)}, f32[32]{0:T(128)S(1)}, f32[32]{0:T(128)S(1)}, f32[64,128]{1,0:T(8,128)S(1)}, ...), branch_computations={%region_11.11_spmd, %region_12.12_spmd} | conditional | flops 210277760 | bytes 18469684 | solution.py:130
  286.4 2.0 copy.60
  294.9 4.0 collective-permute-done
  301.1 7.4 %conditional.21 = ((f32[64,2048]{1,0:T(8,128)}, f32[64,2048]{1,0:T(8,128)}, f32[32,2048]{1,0:T(8,128)})) conditional(s32[]{:T(128)} %convert_element_type.271, (f32[64,2048]{1,0:T(8,128)}, f32[64,2048]{1,0:T(8,128)}, f32[32,2048]{1,0:T(8,128)}) %tuple.142, (s32[]{:T(128)}, f32[32]{0:T(128)S(1)}, f32[32]{0:T(128)S(1)}, f32[64,128]{1,0:T(8,128)S(1)}, ...), branch_computations={%region_7.7_spmd, %region_8.8_spmd} | conditional | flops 210277760 | bytes 18469684 | solution.py:130
  310.3 7.3 %conditional.23 = ((f32[64,2048]{1,0:T(8,128)}, f32[64,2048]{1,0:T(8,128)}, f32[32,2048]{1,0:T(8,128)})) conditional(s32[]{:T(128)} %convert_element_type.272, (f32[64,2048]{1,0:T(8,128)}, f32[64,2048]{1,0:T(8,128)}, f32[32,2048]{1,0:T(8,128)}) %tuple.146, (s32[]{:T(128)}, f32[32]{0:T(128)S(1)}, f32[32]{0:T(128)S(1)}, f32[64,128]{1,0:T(8,128)S(1)}, ...), branch_computations={%region_11.11_spmd, %region_12.12_spmd} | conditional | flops 210277760 | bytes 18469684 | solution.py:130
  317.7 2.0 copy.60
  326.2 4.0 collective-permute-done
  332.3 7.4 %conditional.20 = ((f32[64,2048]{1,0:T(8,128)}, f32[64,2048]{1,0:T(8,128)}, f32[32,2048]{1,0:T(8,128)})) conditional(s32[]{:T(128)} %convert_element_type.270, (f32[64,2048]{1,0:T(8,128)}, f32[64,2048]{1,0:T(8,128)}, f32[32,2048]{1,0:T(8,128)}) %tuple.182, (s32[]{:T(128)}, f32[32]{0:T(128)S(1)}, f32[32]{0:T(128)S(1)}, f32[64,128]{1,0:T(8,128)S(1)}, ...), branch_computations={%region_5.5_spmd, %region_6.6_spmd} | conditional | flops 210277760 | bytes 18469684 | solution.py:130
  339.7 7.3 %conditional.21 = ((f32[64,2048]{1,0:T(8,128)}, f32[64,2048]{1,0:T(8,128)}, f32[32,2048]{1,0:T(8,128)})) conditional(s32[]{:T(128)} %convert_element_type.271, (f32[64,2048]{1,0:T(8,128)}, f32[64,2048]{1,0:T(8,128)}, f32[32,2048]{1,0:T(8,128)}) %tuple.142, (s32[]{:T(128)}, f32[32]{0:T(128)S(1)}, f32[32]{0:T(128)S(1)}, f32[64,128]{1,0:T(8,128)S(1)}, ...), branch_computations={%region_7.7_spmd, %region_8.8_spmd} | conditional | flops 210277760 | bytes 18469684 | solution.py:130
  348.9 2.0 copy.60
  357.5 4.0 collective-permute-done
  365.6 7.4 %conditional.22 = ((f32[64,2048]{1,0:T(8,128)}, f32[64,2048]{1,0:T(8,128)}, f32[32,2048]{1,0:T(8,128)})) conditional(s32[]{:T(128)} %convert_element_type.269, (f32[64,2048]{1,0:T(8,128)}, f32[64,2048]{1,0:T(8,128)}, f32[32,2048]{1,0:T(8,128)}) %tuple.144, (s32[]{:T(128)}, f32[32]{0:T(128)S(1)}, f32[32]{0:T(128)S(1)}, f32[64,128]{1,0:T(8,128)S(1)}, ...), branch_computations={%region_9.9_spmd, %region_10.10_spmd} | conditional | flops 210277760 | bytes 18469684 | solution.py:130
  372.9 7.3 %conditional.23 = ((f32[64,2048]{1,0:T(8,128)}, f32[64,2048]{1,0:T(8,128)}, f32[32,2048]{1,0:T(8,128)})) conditional(s32[]{:T(128)} %convert_element_type.272, (f32[64,2048]{1,0:T(8,128)}, f32[64,2048]{1,0:T(8,128)}, f32[32,2048]{1,0:T(8,128)}) %tuple.146, (s32[]{:T(128)}, f32[32]{0:T(128)S(1)}, f32[32]{0:T(128)S(1)}, f32[64,128]{1,0:T(8,128)S(1)}, ...), branch_computations={%region_11.11_spmd, %region_12.12_spmd} | conditional | flops 210277760 | bytes 18469684 | solution.py:130
  380.2 2.0 copy.60
  388.8 4.0 collective-permute-done
  394.9 7.4 %conditional.21 = ((f32[64,2048]{1,0:T(8,128)}, f32[64,2048]{1,0:T(8,128)}, f32[32,2048]{1,0:T(8,128)})) conditional(s32[]{:T(128)} %convert_element_type.271, (f32[64,2048]{1,0:T(8,128)}, f32[64,2048]{1,0:T(8,128)}, f32[32,2048]{1,0:T(8,128)}) %tuple.142, (s32[]{:T(128)}, f32[32]{0:T(128)S(1)}, f32[32]{0:T(128)S(1)}, f32[64,128]{1,0:T(8,128)S(1)}, ...), branch_computations={%region_7.7_spmd, %region_8.8_spmd} | conditional | flops 210277760 | bytes 18469684 | solution.py:130
  404.2 7.3 %conditional.23 = ((f32[64,2048]{1,0:T(8,128)}, f32[64,2048]{1,0:T(8,128)}, f32[32,2048]{1,0:T(8,128)})) conditional(s32[]{:T(128)} %convert_element_type.272, (f32[64,2048]{1,0:T(8,128)}, f32[64,2048]{1,0:T(8,128)}, f32[32,2048]{1,0:T(8,128)}) %tuple.146, (s32[]{:T(128)}, f32[32]{0:T(128)S(1)}, f32[32]{0:T(128)S(1)}, f32[64,128]{1,0:T(8,128)S(1)}, ...), branch_computations={%region_11.11_spmd, %region_12.12_spmd} | conditional | flops 210277760 | bytes 18469684 | solution.py:130
  411.5 2.0 copy.60
  420.1 4.0 collective-permute-done
  426.2 7.4 %conditional.21 = ((f32[64,2048]{1,0:T(8,128)}, f32[64,2048]{1,0:T(8,128)}, f32[32,2048]{1,0:T(8,128)})) conditional(s32[]{:T(128)} %convert_element_type.271, (f32[64,2048]{1,0:T(8,128)}, f32[64,2048]{1,0:T(8,128)}, f32[32,2048]{1,0:T(8,128)}) %tuple.142, (s32[]{:T(128)}, f32[32]{0:T(128)S(1)}, f32[32]{0:T(128)S(1)}, f32[64,128]{1,0:T(8,128)S(1)}, ...), branch_computations={%region_7.7_spmd, %region_8.8_spmd} | conditional | flops 210277760 | bytes 18469684 | solution.py:130
  435.5 7.3 %conditional.23 = ((f32[64,2048]{1,0:T(8,128)}, f32[64,2048]{1,0:T(8,128)}, f32[32,2048]{1,0:T(8,128)})) conditional(s32[]{:T(128)} %convert_element_type.272, (f32[64,2048]{1,0:T(8,128)}, f32[64,2048]{1,0:T(8,128)}, f32[32,2048]{1,0:T(8,128)}) %tuple.146, (s32[]{:T(128)}, f32[32]{0:T(128)S(1)}, f32[32]{0:T(128)S(1)}, f32[64,128]{1,0:T(8,128)S(1)}, ...), branch_computations={%region_11.11_spmd, %region_12.12_spmd} | conditional | flops 210277760 | bytes 18469684 | solution.py:130
  442.8 2.0 copy.60
  451.4 4.0 collective-permute-done
  457.5 7.3 %conditional.21 = ((f32[64,2048]{1,0:T(8,128)}, f32[64,2048]{1,0:T(8,128)}, f32[32,2048]{1,0:T(8,128)})) conditional(s32[]{:T(128)} %convert_element_type.271, (f32[64,2048]{1,0:T(8,128)}, f32[64,2048]{1,0:T(8,128)}, f32[32,2048]{1,0:T(8,128)}) %tuple.142, (s32[]{:T(128)}, f32[32]{0:T(128)S(1)}, f32[32]{0:T(128)S(1)}, f32[64,128]{1,0:T(8,128)S(1)}, ...), branch_computations={%region_7.7_spmd, %region_8.8_spmd} | conditional | flops 210277760 | bytes 18469684 | solution.py:130
  466.8 7.3 %conditional.23 = ((f32[64,2048]{1,0:T(8,128)}, f32[64,2048]{1,0:T(8,128)}, f32[32,2048]{1,0:T(8,128)})) conditional(s32[]{:T(128)} %convert_element_type.272, (f32[64,2048]{1,0:T(8,128)}, f32[64,2048]{1,0:T(8,128)}, f32[32,2048]{1,0:T(8,128)}) %tuple.146, (s32[]{:T(128)}, f32[32]{0:T(128)S(1)}, f32[32]{0:T(128)S(1)}, f32[64,128]{1,0:T(8,128)S(1)}, ...), branch_computations={%region_11.11_spmd, %region_12.12_spmd} | conditional | flops 210277760 | bytes 18469684 | solution.py:130
  474.1 2.0 copy.60
  482.7 4.2 collective-permute-done
  491.0 7.4 %conditional.22 = ((f32[64,2048]{1,0:T(8,128)}, f32[64,2048]{1,0:T(8,128)}, f32[32,2048]{1,0:T(8,128)})) conditional(s32[]{:T(128)} %convert_element_type.269, (f32[64,2048]{1,0:T(8,128)}, f32[64,2048]{1,0:T(8,128)}, f32[32,2048]{1,0:T(8,128)}) %tuple.144, (s32[]{:T(128)}, f32[32]{0:T(128)S(1)}, f32[32]{0:T(128)S(1)}, f32[64,128]{1,0:T(8,128)S(1)}, ...), branch_computations={%region_9.9_spmd, %region_10.10_spmd} | conditional | flops 210277760 | bytes 18469684 | solution.py:130
  498.4 7.3 %conditional.23 = ((f32[64,2048]{1,0:T(8,128)}, f32[64,2048]{1,0:T(8,128)}, f32[32,2048]{1,0:T(8,128)})) conditional(s32[]{:T(128)} %convert_element_type.272, (f32[64,2048]{1,0:T(8,128)}, f32[64,2048]{1,0:T(8,128)}, f32[32,2048]{1,0:T(8,128)}) %tuple.146, (s32[]{:T(128)}, f32[32]{0:T(128)S(1)}, f32[32]{0:T(128)S(1)}, f32[64,128]{1,0:T(8,128)S(1)}, ...), branch_computations={%region_11.11_spmd, %region_12.12_spmd} | conditional | flops 210277760 | bytes 18469684 | solution.py:130
  505.7 2.0 copy.60
  513.3 75.0 %reduce-scatter.2.cloned.1.call-done = f32[32,128]{1,0:T(8,128)} async-done(((f32[32,2048]{1,0:T(8,128)}), f32[32,128]{1,0:T(8,128)}) %reduce-scatter.2.cloned.1.call-update) | async-done | bytes 16400 | tf_op jit(solution)/shard_map/reduce_scatter | solution.py:164
  (914 shorter events, 331.8 us)
Async XLA Ops:
  7.2 581.1 %reduce-scatter.2.cloned.1.call-start = ((), (), s32[]{:S(2)}) async-start(), calls=%async_computation.1 | async-start | bytes 278528 | tf_op jit(solution)/shard_map/reduce_scatter | solution.py:164
  9.9 13.0 %copy-start.29 = (f32[64,2048]{1,0:T(8,128)}, f32[64,2048]{1,0:T(8,128)S(1)}, u32[]{:S(2)}) copy-start(f32[64,2048]{1,0:T(8,128)S(1)} %fusion.261) | copy-start | bytes 1572868
  10.7 12.2 %copy-start.30 = (f32[64,2048]{1,0:T(8,128)}, f32[64,2048]{1,0:T(8,128)S(1)}, u32[]{:S(2)}) copy-start(f32[64,2048]{1,0:T(8,128)S(1)} %fusion.263) | copy-start | bytes 1572868
  15.3 4.4 copy-start
  38.8 9.7 %copy-start.3 = (f32[64,2048]{1,0:T(8,128)}, f32[64,2048]{1,0:T(8,128)S(1)}, u32[]{:S(2)}) copy-start(f32[64,2048]{1,0:T(8,128)S(1)} %get-tuple-element.1500) | copy-start | bytes 1572868 | tf_op jit(solution)/shard_map/while
  38.8 9.7 %collective-permute-start = (bf16[128,2048]{1,0:T(8,128)(2,1)}, bf16[128,2048]{1,0:T(8,128)(2,1)S(1)}, u32[]{:S(2)}, u32[]{:S(2)}) collective-permute-start(bf16[128,2048]{1,0:T(8,128)(2,1)} %get-tuple-element.1499), channel_id=1, source_target_pairs={{0,1},{1,2},{2,3},{3,4},{4,5},{5,6},{6,7},{7,8},{8,9},{9,10},{10,1... | collective-permute-start | bytes 1572872 | tf_op jit(solution)/shard_map/while/body/eval_jaxpr/ppermute | solution.py:13
  67.3 2.0 copy-start.8
  67.3 2.0 copy-start.14
  70.1 9.7 %copy-start.3 = (f32[64,2048]{1,0:T(8,128)}, f32[64,2048]{1,0:T(8,128)S(1)}, u32[]{:S(2)}) copy-start(f32[64,2048]{1,0:T(8,128)S(1)} %get-tuple-element.1500) | copy-start | bytes 1572868 | tf_op jit(solution)/shard_map/while
  70.1 9.7 %collective-permute-start = (bf16[128,2048]{1,0:T(8,128)(2,1)}, bf16[128,2048]{1,0:T(8,128)(2,1)S(1)}, u32[]{:S(2)}, u32[]{:S(2)}) collective-permute-start(bf16[128,2048]{1,0:T(8,128)(2,1)} %get-tuple-element.1499), channel_id=1, source_target_pairs={{0,1},{1,2},{2,3},{3,4},{4,5},{5,6},{6,7},{7,8},{8,9},{9,10},{10,1... | collective-permute-start | bytes 1572872 | tf_op jit(solution)/shard_map/while/body/eval_jaxpr/ppermute | solution.py:13
  98.6 2.0 copy-start.8
  98.6 2.0 copy-start.14
  101.4 9.7 %copy-start.3 = (f32[64,2048]{1,0:T(8,128)}, f32[64,2048]{1,0:T(8,128)S(1)}, u32[]{:S(2)}) copy-start(f32[64,2048]{1,0:T(8,128)S(1)} %get-tuple-element.1500) | copy-start | bytes 1572868 | tf_op jit(solution)/shard_map/while
  101.4 9.7 %collective-permute-start = (bf16[128,2048]{1,0:T(8,128)(2,1)}, bf16[128,2048]{1,0:T(8,128)(2,1)S(1)}, u32[]{:S(2)}, u32[]{:S(2)}) collective-permute-start(bf16[128,2048]{1,0:T(8,128)(2,1)} %get-tuple-element.1499), channel_id=1, source_target_pairs={{0,1},{1,2},{2,3},{3,4},{4,5},{5,6},{6,7},{7,8},{8,9},{9,10},{10,1... | collective-permute-start | bytes 1572872 | tf_op jit(solution)/shard_map/while/body/eval_jaxpr/ppermute | solution.py:13
  129.9 2.0 copy-start.8
  129.9 2.0 copy-start.14
  132.7 9.7 %copy-start.3 = (f32[64,2048]{1,0:T(8,128)}, f32[64,2048]{1,0:T(8,128)S(1)}, u32[]{:S(2)}) copy-start(f32[64,2048]{1,0:T(8,128)S(1)} %get-tuple-element.1500) | copy-start | bytes 1572868 | tf_op jit(solution)/shard_map/while
  132.7 9.7 %collective-permute-start = (bf16[128,2048]{1,0:T(8,128)(2,1)}, bf16[128,2048]{1,0:T(8,128)(2,1)S(1)}, u32[]{:S(2)}, u32[]{:S(2)}) collective-permute-start(bf16[128,2048]{1,0:T(8,128)(2,1)} %get-tuple-element.1499), channel_id=1, source_target_pairs={{0,1},{1,2},{2,3},{3,4},{4,5},{5,6},{6,7},{7,8},{8,9},{9,10},{10,1... | collective-permute-start | bytes 1572872 | tf_op jit(solution)/shard_map/while/body/eval_jaxpr/ppermute | solution.py:13
  161.2 2.0 copy-start.8
  161.2 2.0 copy-start.14
  164.0 9.7 %copy-start.3 = (f32[64,2048]{1,0:T(8,128)}, f32[64,2048]{1,0:T(8,128)S(1)}, u32[]{:S(2)}) copy-start(f32[64,2048]{1,0:T(8,128)S(1)} %get-tuple-element.1500) | copy-start | bytes 1572868 | tf_op jit(solution)/shard_map/while
  164.0 9.7 %collective-permute-start = (bf16[128,2048]{1,0:T(8,128)(2,1)}, bf16[128,2048]{1,0:T(8,128)(2,1)S(1)}, u32[]{:S(2)}, u32[]{:S(2)}) collective-permute-start(bf16[128,2048]{1,0:T(8,128)(2,1)} %get-tuple-element.1499), channel_id=1, source_target_pairs={{0,1},{1,2},{2,3},{3,4},{4,5},{5,6},{6,7},{7,8},{8,9},{9,10},{10,1... | collective-permute-start | bytes 1572872 | tf_op jit(solution)/shard_map/while/body/eval_jaxpr/ppermute | solution.py:13
  192.5 2.0 copy-start.8
  192.5 2.0 copy-start.14
  195.3 9.7 %copy-start.3 = (f32[64,2048]{1,0:T(8,128)}, f32[64,2048]{1,0:T(8,128)S(1)}, u32[]{:S(2)}) copy-start(f32[64,2048]{1,0:T(8,128)S(1)} %get-tuple-element.1500) | copy-start | bytes 1572868 | tf_op jit(solution)/shard_map/while
  195.3 9.7 %collective-permute-start = (bf16[128,2048]{1,0:T(8,128)(2,1)}, bf16[128,2048]{1,0:T(8,128)(2,1)S(1)}, u32[]{:S(2)}, u32[]{:S(2)}) collective-permute-start(bf16[128,2048]{1,0:T(8,128)(2,1)} %get-tuple-element.1499), channel_id=1, source_target_pairs={{0,1},{1,2},{2,3},{3,4},{4,5},{5,6},{6,7},{7,8},{8,9},{9,10},{10,1... | collective-permute-start | bytes 1572872 | tf_op jit(solution)/shard_map/while/body/eval_jaxpr/ppermute | solution.py:13
  223.8 2.0 copy-start.8
  223.8 2.0 copy-start.14
  226.6 9.7 %copy-start.3 = (f32[64,2048]{1,0:T(8,128)}, f32[64,2048]{1,0:T(8,128)S(1)}, u32[]{:S(2)}) copy-start(f32[64,2048]{1,0:T(8,128)S(1)} %get-tuple-element.1500) | copy-start | bytes 1572868 | tf_op jit(solution)/shard_map/while
  226.6 9.7 %collective-permute-start = (bf16[128,2048]{1,0:T(8,128)(2,1)}, bf16[128,2048]{1,0:T(8,128)(2,1)S(1)}, u32[]{:S(2)}, u32[]{:S(2)}) collective-permute-start(bf16[128,2048]{1,0:T(8,128)(2,1)} %get-tuple-element.1499), channel_id=1, source_target_pairs={{0,1},{1,2},{2,3},{3,4},{4,5},{5,6},{6,7},{7,8},{8,9},{9,10},{10,1... | collective-permute-start | bytes 1572872 | tf_op jit(solution)/shard_map/while/body/eval_jaxpr/ppermute | solution.py:13
  255.1 2.0 copy-start.8
  255.1 2.0 copy-start.14
  257.8 9.7 %copy-start.3 = (f32[64,2048]{1,0:T(8,128)}, f32[64,2048]{1,0:T(8,128)S(1)}, u32[]{:S(2)}) copy-start(f32[64,2048]{1,0:T(8,128)S(1)} %get-tuple-element.1500) | copy-start | bytes 1572868 | tf_op jit(solution)/shard_map/while
  257.8 9.7 %collective-permute-start = (bf16[128,2048]{1,0:T(8,128)(2,1)}, bf16[128,2048]{1,0:T(8,128)(2,1)S(1)}, u32[]{:S(2)}, u32[]{:S(2)}) collective-permute-start(bf16[128,2048]{1,0:T(8,128)(2,1)} %get-tuple-element.1499), channel_id=1, source_target_pairs={{0,1},{1,2},{2,3},{3,4},{4,5},{5,6},{6,7},{7,8},{8,9},{9,10},{10,1... | collective-permute-start | bytes 1572872 | tf_op jit(solution)/shard_map/while/body/eval_jaxpr/ppermute | solution.py:13
  286.4 2.0 copy-start.8
  286.4 2.0 copy-start.14
  289.1 9.7 %copy-start.3 = (f32[64,2048]{1,0:T(8,128)}, f32[64,2048]{1,0:T(8,128)S(1)}, u32[]{:S(2)}) copy-start(f32[64,2048]{1,0:T(8,128)S(1)} %get-tuple-element.1500) | copy-start | bytes 1572868 | tf_op jit(solution)/shard_map/while
  289.1 9.7 %collective-permute-start = (bf16[128,2048]{1,0:T(8,128)(2,1)}, bf16[128,2048]{1,0:T(8,128)(2,1)S(1)}, u32[]{:S(2)}, u32[]{:S(2)}) collective-permute-start(bf16[128,2048]{1,0:T(8,128)(2,1)} %get-tuple-element.1499), channel_id=1, source_target_pairs={{0,1},{1,2},{2,3},{3,4},{4,5},{5,6},{6,7},{7,8},{8,9},{9,10},{10,1... | collective-permute-start | bytes 1572872 | tf_op jit(solution)/shard_map/while/body/eval_jaxpr/ppermute | solution.py:13
  317.6 2.0 copy-start.8
  317.7 2.0 copy-start.14
  320.4 9.7 %copy-start.3 = (f32[64,2048]{1,0:T(8,128)}, f32[64,2048]{1,0:T(8,128)S(1)}, u32[]{:S(2)}) copy-start(f32[64,2048]{1,0:T(8,128)S(1)} %get-tuple-element.1500) | copy-start | bytes 1572868 | tf_op jit(solution)/shard_map/while
  320.4 9.7 %collective-permute-start = (bf16[128,2048]{1,0:T(8,128)(2,1)}, bf16[128,2048]{1,0:T(8,128)(2,1)S(1)}, u32[]{:S(2)}, u32[]{:S(2)}) collective-permute-start(bf16[128,2048]{1,0:T(8,128)(2,1)} %get-tuple-element.1499), channel_id=1, source_target_pairs={{0,1},{1,2},{2,3},{3,4},{4,5},{5,6},{6,7},{7,8},{8,9},{9,10},{10,1... | collective-permute-start | bytes 1572872 | tf_op jit(solution)/shard_map/while/body/eval_jaxpr/ppermute | solution.py:13
  348.9 2.0 copy-start.8
  348.9 2.0 copy-start.14
  351.7 9.7 %copy-start.3 = (f32[64,2048]{1,0:T(8,128)}, f32[64,2048]{1,0:T(8,128)S(1)}, u32[]{:S(2)}) copy-start(f32[64,2048]{1,0:T(8,128)S(1)} %get-tuple-element.1500) | copy-start | bytes 1572868 | tf_op jit(solution)/shard_map/while
  351.7 9.7 %collective-permute-start = (bf16[128,2048]{1,0:T(8,128)(2,1)}, bf16[128,2048]{1,0:T(8,128)(2,1)S(1)}, u32[]{:S(2)}, u32[]{:S(2)}) collective-permute-start(bf16[128,2048]{1,0:T(8,128)(2,1)} %get-tuple-element.1499), channel_id=1, source_target_pairs={{0,1},{1,2},{2,3},{3,4},{4,5},{5,6},{6,7},{7,8},{8,9},{9,10},{10,1... | collective-permute-start | bytes 1572872 | tf_op jit(solution)/shard_map/while/body/eval_jaxpr/ppermute | solution.py:13
  380.2 2.0 copy-start.8
  380.2 2.0 copy-start.14
  383.0 9.7 %copy-start.3 = (f32[64,2048]{1,0:T(8,128)}, f32[64,2048]{1,0:T(8,128)S(1)}, u32[]{:S(2)}) copy-start(f32[64,2048]{1,0:T(8,128)S(1)} %get-tuple-element.1500) | copy-start | bytes 1572868 | tf_op jit(solution)/shard_map/while
  383.0 9.7 %collective-permute-start = (bf16[128,2048]{1,0:T(8,128)(2,1)}, bf16[128,2048]{1,0:T(8,128)(2,1)S(1)}, u32[]{:S(2)}, u32[]{:S(2)}) collective-permute-start(bf16[128,2048]{1,0:T(8,128)(2,1)} %get-tuple-element.1499), channel_id=1, source_target_pairs={{0,1},{1,2},{2,3},{3,4},{4,5},{5,6},{6,7},{7,8},{8,9},{9,10},{10,1... | collective-permute-start | bytes 1572872 | tf_op jit(solution)/shard_map/while/body/eval_jaxpr/ppermute | solution.py:13
  411.5 2.0 copy-start.8
  411.5 2.0 copy-start.14
  414.3 9.7 %copy-start.3 = (f32[64,2048]{1,0:T(8,128)}, f32[64,2048]{1,0:T(8,128)S(1)}, u32[]{:S(2)}) copy-start(f32[64,2048]{1,0:T(8,128)S(1)} %get-tuple-element.1500) | copy-start | bytes 1572868 | tf_op jit(solution)/shard_map/while
  414.3 9.7 %collective-permute-start = (bf16[128,2048]{1,0:T(8,128)(2,1)}, bf16[128,2048]{1,0:T(8,128)(2,1)S(1)}, u32[]{:S(2)}, u32[]{:S(2)}) collective-permute-start(bf16[128,2048]{1,0:T(8,128)(2,1)} %get-tuple-element.1499), channel_id=1, source_target_pairs={{0,1},{1,2},{2,3},{3,4},{4,5},{5,6},{6,7},{7,8},{8,9},{9,10},{10,1... | collective-permute-start | bytes 1572872 | tf_op jit(solution)/shard_map/while/body/eval_jaxpr/ppermute | solution.py:13
  442.8 2.0 copy-start.8
  442.8 2.0 copy-start.14
  445.6 9.7 %copy-start.3 = (f32[64,2048]{1,0:T(8,128)}, f32[64,2048]{1,0:T(8,128)S(1)}, u32[]{:S(2)}) copy-start(f32[64,2048]{1,0:T(8,128)S(1)} %get-tuple-element.1500) | copy-start | bytes 1572868 | tf_op jit(solution)/shard_map/while
  445.6 9.7 %collective-permute-start = (bf16[128,2048]{1,0:T(8,128)(2,1)}, bf16[128,2048]{1,0:T(8,128)(2,1)S(1)}, u32[]{:S(2)}, u32[]{:S(2)}) collective-permute-start(bf16[128,2048]{1,0:T(8,128)(2,1)} %get-tuple-element.1499), channel_id=1, source_target_pairs={{0,1},{1,2},{2,3},{3,4},{4,5},{5,6},{6,7},{7,8},{8,9},{9,10},{10,1... | collective-permute-start | bytes 1572872 | tf_op jit(solution)/shard_map/while/body/eval_jaxpr/ppermute | solution.py:13
  474.1 2.0 copy-start.8
  474.1 2.0 copy-start.14
  476.9 10.0 %copy-start.3 = (f32[64,2048]{1,0:T(8,128)}, f32[64,2048]{1,0:T(8,128)S(1)}, u32[]{:S(2)}) copy-start(f32[64,2048]{1,0:T(8,128)S(1)} %get-tuple-element.1500) | copy-start | bytes 1572868 | tf_op jit(solution)/shard_map/while
  476.9 10.0 %collective-permute-start = (bf16[128,2048]{1,0:T(8,128)(2,1)}, bf16[128,2048]{1,0:T(8,128)(2,1)S(1)}, u32[]{:S(2)}, u32[]{:S(2)}) collective-permute-start(bf16[128,2048]{1,0:T(8,128)(2,1)} %get-tuple-element.1499), channel_id=1, source_target_pairs={{0,1},{1,2},{2,3},{3,4},{4,5},{5,6},{6,7},{7,8},{8,9},{9,10},{10,1... | collective-permute-start | bytes 1572872 | tf_op jit(solution)/shard_map/while/body/eval_jaxpr/ppermute | solution.py:13
  505.7 2.0 copy-start.8
  505.7 2.0 copy-start.14
  (176 other events, 194.6 us)
Sparse Core Ops, SparseCore 0:
  507.8 80.3 reduce-scatter.1
where the time goes:
time: 602 us; the launch traced here: 595 us
  matrix products  237 us (39%)
  waiting for transfers between devices  134 us (22%)
  local copies, waits for them, and re-layouts  124 us (21%)
  loops' own time  79.8 us (13%)
  between operations  16.8 us (3%)
    dot_general x200, matrix products, matmul(): jnp.dot(left, right, precision=HIGHEST_PRECISION, preferred_element_type=...  148 us
    dot_general x66, matrix products, left_transposed(): lax.dot_general(left, right, (((0,), (0,)), ((), ())), precision=HIGHEST_...  88.7 us
    another operation x1, loops' own time, on_device(): running = lax.fori_loop(1, devices, cycle_turn, (grad_out, running))[1]  76.2 us
    reduce_scatter x1, waiting for transfers between devices, on_device(): lax.psum_scatter(running[4], 'seq', scatter_dimension=1, tiled=True)  75 us
    cond x240, local copies, waits for them, and re-layouts  60.4 us
    ppermute x15, waiting for transfers between devices, shifted(): lax.ppermute(value, axis, [(i, (i + by) % peers) for i in range(peers)])  58.8 us
    while x195, local copies, waits for them, and re-layouts  47.4 us
  transfers between devices with their start and end apart: 16, of which 16 were waited for; matrix products, arithmetic and copies ran while one was open for 3% of the time, Pallas kernels for 0%

commit v1 on v0

v1 whole, which is shorter than its diff:
```python
import functools
import math

import jax
import jax.numpy as jnp
import numpy as np
from jax import lax
from jax.experimental import pallas as pl
from jax.experimental.pallas import tpu as pltpu
from jax.sharding import PartitionSpec as P

HIGHEST = lax.Precision.HIGHEST
F32 = jnp.float32
BF16 = jnp.bfloat16
LANES = 128


def halves(value):
    high = value.astype(BF16)
    return high, (value - high.astype(F32)).astype(BF16)


def table_halves(value):
    high = lax.reduce_precision(value, 8, 7)
    return high.astype(BF16), (value - high).astype(BF16)


def odd_frequencies(rows):
    angles = np.pi * np.outer(2 * np.arange(rows) + 1, np.arange(rows)) / (2 * rows)
    return np.cos(angles), -np.sin(angles)


def tables(rows, rates, freqs):
    cos_part, sin_part = odd_frequencies(rows)
    forward = jnp.asarray(np.concatenate([cos_part, sin_part], 0), F32)
    inverse = jnp.asarray(np.concatenate([cos_part, sin_part], 0).T / rows, F32)
    lags = jnp.arange(rows + 1).astype(F32)[None, :]
    decay = jnp.exp(-lags * rates[:, None])
    power_real = decay * jnp.cos(lags * freqs[:, None])
    power_imag = decay * jnp.sin(lags * freqs[:, None])
    to_start = jnp.concatenate([power_real[:, :rows], power_imag[:, :rows]], 0)
    to_end = jnp.concatenate([power_real[:, :0:-1], power_imag[:, :0:-1]], 0)
    left_g = jnp.concatenate(table_halves(jnp.concatenate([forward, to_start], 0)), 1)
    left_x = jnp.concatenate(table_halves(jnp.concatenate([forward, to_end], 0)), 1)
    back = jnp.concatenate(
        [inverse, power_real[:, :0:-1].T, -power_imag[:, :0:-1].T], 1
    )
    back_high, back_low = table_halves(back)
    basis_spectrum = jnp.dot(
        forward, power_real[:, :rows].T, precision=HIGHEST, preferred_element_type=F32
    )
    step = jnp.stack([power_real[:, rows], power_imag[:, rows]], 0)[:, :, None]
    return left_g, left_x, back_high, back_low, basis_spectrum, step


def kernel(
    spans_ref,
    gx_ref,
    weight_ref,
    gain_ref,
    left_g_ref,
    left_x_ref,
    back_high_ref,
    back_low_ref,
    spectrum_ref,
    step_ref,
    y_ref,
    wgrad_ref,
    slot_of,
    sums_g,
    sums_x,
    high,
    low,
):
    n_src, _, rows_dev, width = gx_ref.shape
    rows = rows_dev // 2
    n_basis = weight_ref.shape[0]
    n_spans = 2 * n_src

    def invert(slot, carry):
        slot_of[spans_ref[slot]] = slot
        return carry

    lax.fori_loop(0, n_spans, invert, 0)
    weight = weight_ref[...]
    spectrum = spectrum_ref[...]
    taps = jnp.dot(spectrum, weight, precision=HIGHEST, preferred_element_type=F32)
    taps_real, taps_imag = taps[:rows], taps[rows:]

    def pair(source, which):
        first = gx_ref[source, which, :rows, :]
        second = gx_ref[source, which, rows:, :]
        both = jnp.concatenate([first, second], 1)
        return jnp.concatenate([both, both], 0)

    def analyse(source, carry):
        cross_real, cross_imag = carry
        of_g = jnp.dot(left_g_ref[...], pair(source, 0), preferred_element_type=F32)
        of_x = jnp.dot(left_x_ref[...], pair(source, 1), preferred_element_type=F32)
        for half in range(2):
            at = slice(half * width, (half + 1) * width)
            slot = 2 * source + half
            sums_g[slot] = of_g[2 * rows :, at]
            sums_x[slot] = of_x[2 * rows :, at]
            g_real, g_imag = of_g[:rows, at], of_g[rows : 2 * rows, at]
            x_real, x_imag = of_x[:rows, at], of_x[rows : 2 * rows, at]
            cross_real = cross_real + (x_real * g_real + x_imag * g_imag)
            cross_imag = cross_imag + (x_real * g_imag - x_imag * g_real)
            y_real = halves(taps_real * g_real + taps_imag * g_imag)
            y_imag = halves(taps_real * g_imag - taps_imag * g_real)
            high[slot, :rows] = y_real[0]
            high[slot, rows : 2 * rows] = y_imag[0]
            low[slot, :rows] = y_real[1]
            low[slot, rows : 2 * rows] = y_imag[1]
        return cross_real, cross_imag

    zero = jnp.zeros((rows, width), F32)
    cross_real, cross_imag = lax.fori_loop(0, n_src, analyse, (zero, zero))
    near = lax.dot_general(
        spectrum,
        jnp.concatenate([cross_real, cross_imag], 0) * (1.0 / rows),
        (((0,), (0,)), ((), ())),
        precision=HIGHEST,
        preferred_element_type=F32,
    )
    step_real = jnp.broadcast_to(step_ref[0], (n_basis, width))
    step_imag = jnp.broadcast_to(step_ref[1], (n_basis, width))

    def descend(index, carry):
        state_real, state_imag, total = carry
        slot = slot_of[n_spans - 1 - index]
        total = total + (
            state_real * sums_x[slot, :n_basis] - state_imag * sums_x[slot, n_basis:]
        )
        far_real, far_imag = halves(weight * state_real), halves(weight * state_imag)
        high[slot, 2 * rows : 2 * rows + n_basis] = far_real[0]
        high[slot, 2 * rows + n_basis :] = far_imag[0]
        low[slot, 2 * rows : 2 * rows + n_basis] = far_real[1]
        low[slot, 2 * rows + n_basis :] = far_imag[1]
        next_real = sums_g[slot, :n_basis] + step_real * state_real - step_imag * state_imag
        next_imag = sums_g[slot, n_basis:] + step_real * state_imag + step_imag * state_real
        return next_real, next_imag, total

    empty = jnp.zeros((n_basis, width), F32)
    total = lax.fori_loop(0, n_spans, descend, (empty, empty, near))[2]
    wgrad_ref[...] = total
    gain = gain_ref[...]

    def restore(source, carry):
        both_high = jnp.concatenate([high[2 * source], high[2 * source + 1]], 1)
        both_low = jnp.concatenate([low[2 * source], low[2 * source + 1]], 1)
        value = (
            jnp.dot(back_high_ref[...], both_high, preferred_element_type=F32)
            + jnp.dot(back_high_ref[...], both_low, preferred_element_type=F32)
            + jnp.dot(back_low_ref[...], both_high, preferred_element_type=F32)
        )
        for half in range(2):
            at = slice(half * rows, (half + 1) * rows)
            own = gx_ref[source, 0, at, :].astype(F32)
            y_ref[source, at, :] = (
                value[:, half * width : (half + 1) * width] + gain * own
            ).astype(BF16)
        return carry

    lax.fori_loop(0, n_src, restore, 0)


def on_device(inputs, grad_out, filter_weight, filter_rates, filter_freqs, skip_gain, span_of_slot):
    rows_dev, channels = inputs.shape
    rows = rows_dev // 2
    n_basis = filter_weight.shape[0]
    devices = lax.axis_size("seq")
    position = lax.axis_index("seq")
    own = channels // devices
    width = -(-own // LANES) * LANES
    widen = ((0, 0), (0, width - own))
    both = jnp.stack([grad_out, inputs], 0).reshape(2, rows_dev, devices, own)
    gx = lax.all_to_all(both.transpose(2, 0, 1, 3), "seq", 0, 0, tiled=True)
    gx = jnp.pad(gx, ((0, 0), (0, 0)) + widen)
    weight = jnp.pad(lax.dynamic_slice_in_dim(filter_weight, position * own, own, 1), widen)
    gain = jnp.pad(lax.dynamic_slice_in_dim(skip_gain[None, :], position * own, own, 1), widen)
    n_spans = 2 * devices
    vmem = pl.BlockSpec(memory_space=pltpu.VMEM)
    y, wgrad = pl.pallas_call(
        kernel,
        out_shape=(
            jax.ShapeDtypeStruct((devices, rows_dev, width), BF16),
            jax.ShapeDtypeStruct((n_basis, width), F32),
        ),
        in_specs=[pl.BlockSpec(memory_space=pltpu.SMEM)] + [vmem] * 9,
        out_specs=(vmem, vmem),
        scratch_shapes=[
            pltpu.SMEM((n_spans,), jnp.int32),
            pltpu.VMEM((n_spans, 2 * n_basis, width), F32),
            pltpu.VMEM((n_spans, 2 * n_basis, width), F32),
            pltpu.VMEM((n_spans, 2 * rows + 2 * n_basis, width), BF16),
            pltpu.VMEM((n_spans, 2 * rows + 2 * n_basis, width), BF16),
        ],
        name="spans",
    )(span_of_slot, gx, weight, gain, *tables(rows, filter_rates, filter_freqs))
    y = lax.all_to_all(y[:, :, :own], "seq", 0, 0, tiled=True)
    input_grad = y.transpose(1, 0, 2).reshape(rows_dev, channels)
    return input_grad, wgrad[:, :own]


def solution(mesh):
    placed = (
        P(("groups", "seq"), None),
        P(("groups", "seq"), None),
        P(),
        P(),
        P(),
        P(),
        P("groups"),
    )
    return jax.shard_map(
        on_device,
        mesh=mesh,
        in_specs=placed,
        out_specs=(P(("groups", "seq"), None), P("groups", "seq")),
        check_vma=False,
    )
```

time: 602 us -> 68.8 us (0.11)
  the two profiles are of different devices: /device:TPU:8 before, /device:TPU:0 now
where the time goes in v1:
time: 68.8 us; the launch traced here: 68.3 us
  blocking collectives  21.3 us (31%)
  waiting for transfers between devices  15.3 us (22%)
  Pallas kernels  9.69 us (14%)
  local copies, waits for them, and re-layouts  9.56 us (14%)
  starting transfers between devices  7.39 us (11%)
  other arithmetic  3.45 us (5%)
  matrix products  0.81 us (1%)
  between operations  0.77 us (1%)
    all_to_all x1, blocking collectives, on_device(): y = lax.all_to_all(y[:, :, :own], 'seq', 0, 0, tiled=True)  21.3 us
    all_to_all x1, waiting for transfers between devices, on_device(): gx = lax.all_to_all(both.transpose(2, 0, 1, 3), 'seq', 0, 0, tiled=True)  15.3 us
    pallas_call x1, Pallas kernels, on_device(): pl.pallas_call(kernel, out_shape=(jax.ShapeDtypeStruct((devices, rows_dev...  9.69 us
    all_to_all x1, starting transfers between devices, on_device(): gx = lax.all_to_all(both.transpose(2, 0, 1, 3), 'seq', 0, 0, tiled=True)  7.39 us
    unnamed x17, local copies, waits for them, and re-layouts  5.79 us
  transfers between devices with their start and end apart: 1, of which 1 were waited for; matrix products, arithmetic and copies ran while one was open for 9% of the time, Pallas kernels for 0%

profile of v1, /device:TPU:0, one launch (start us, length us, event | category | flops | bytes accessed | tf_op | source)
XLA Modules:
  0.0 68.3 jit_solution(1196762118262106612)
XLA Ops:
  0.6 0.0 copy-start
  0.6 1.4 %copy.18 = bf16[128,2048]{0,1:T(8,128)(2,1)S(1)} copy(bf16[128,2048]{1,0:T(8,128)(2,1)} %param.9) | data formatting | bytes 1048576 | tf_op args[0]
  2.0 0.0 copy-start.2
  2.0 0.3 copy.20
  2.3 0.8 %copy-done.2 = bf16[128,2048]{1,0:T(8,128)(2,1)S(1)} copy-done((bf16[128,2048]{1,0:T(8,128)(2,1)S(1)}, bf16[128,2048]{1,0:T(8,128)(2,1)}, u32[]{:S(2)}) %copy-start.2) | copy-done | bytes 524312
  3.1 0.3 copy.17
  3.3 0.3 copy.19
  3.6 1.1 %maximum_bitcast_fusion = bf16[16,2,128,128]{3,2,1,0:T(8,128)(2,1)} fusion(bf16[1,128,16,128]{3,1,0,2:T(8,128)(2,1)S(1)} %copy.20, bf16[1,128,16,128]{3,1,0,2:T(8,128)(2,1)S(1)} %copy.19), kind=kLoop, calls=%fused_computation | loop fusion | flops 524288 | bytes 2097152 | tf_op jit(solution)/shard_map/transpose | solution.py:178
  4.7 7.4 %all-to-all-start = ((bf16[16,2,128,128]{3,2,1,0:T(8,128)(2,1)}), bf16[16,2,128,128]{3,2,1,0:T(8,128)(2,1)S(1)}, u32[]{:S(2)}, u32[]{:S(2)}) async-start(bf16[16,2,128,128]{3,2,1,0:T(8,128)(2,1)} %maximum_bitcast_fusion), calls=%async_computation | async-start | bytes 2097152 | tf_op jit(solution)/shard_map/all_to_all | solution.py:178
  12.1 0.0 copy-start.5
  12.1 0.0 copy-start.6
  12.1 0.6 copy-done.5
  12.8 0.0 copy-done.6
  12.8 0.2 fusion.5
  13.0 0.1 copy.24
  13.1 0.1 copy.23
  13.2 0.1 copy.22
  13.3 0.0 copy-start.3
  13.3 0.1 copy.21
  13.4 0.7 %copy.26.step_ref = f32[2,32,1]{2,1,0:T(8,128)} copy(f32[2,32,1]{1,0,2:T(2,128)S(1)} %maximum_bitcast_fusion.1) | data formatting | bytes 512 | tf_op jit(solution)/shard_map/broadcast_in_dim | solution.py:52
  14.1 1.3 %dynamic-slice_bitcast_fusion.gain_ref = f32[1,128]{1,0:T(1,128)} fusion(f32[2048]{0:T(1024)} %param.14, s32[]{:T(128)S(6)} %select_n.4), kind=kLoop, calls=%fused_computation.27 | loop fusion | bytes 1028 | tf_op jit(solution)/shard_map/dynamic_slice | solution.py:181
  15.4 0.0 copy-done
  15.4 0.6 constant_dynamic-slice_fusion.weight_ref
  16.0 0.0 copy-done.3
  16.0 0.7 %pad_maximum_fusion.3.left_g_ref = bf16[192,128]{1,0:T(8,128)(2,1)} fusion(bf16[192,64]{1,0:T(8,128)(2,1)S(1)} %get-tuple-element.14, bf16[192,64]{1,0:T(8,128)(2,1)S(1)} %get-tuple-element.15), kind=kLoop, calls=%fused_computation.17 | loop fusion | flops 98304 | bytes 98304 | tf_op jit(solution)/shard_map/concatenate | solution.py:43
  16.7 0.7 %pad_maximum_fusion.4.left_x_ref = bf16[192,128]{1,0:T(8,128)(2,1)} fusion(bf16[192,64]{1,0:T(8,128)(2,1)S(1)} %get-tuple-element.11, bf16[192,64]{1,0:T(8,128)(2,1)S(1)} %get-tuple-element.10), kind=kLoop, calls=%fused_computation.18 | loop fusion | flops 98304 | bytes 98304 | tf_op jit(solution)/shard_map/concatenate | solution.py:44
  17.4 0.0 copy-start.4
  17.4 0.8 %copy-done.4 = f32[64,128]{1,0:T(8,128)S(1)} copy-done((f32[64,128]{1,0:T(8,128)S(1)}, f32[64,128]{1,0:T(8,128)}, u32[]{:S(2)}) %copy-start.4) | copy-done | bytes 32792
  18.2 0.7 %fusion.4 = (bf16[64,192]{1,0:T(8,128)(2,1)}, bf16[64,192]{1,0:T(8,128)(2,1)}) fusion(f32[64,32]{1,0:T(8,128)S(1)} %negate_bitcast_fusion, f32[64,32]{1,0:T(8,128)S(1)} %bitcast.22, f32[64,128]{1,0:T(8,128)S(1)} %copy-done.4), kind=kLoop, calls=%fused_computation.13 | loop fusion | flops 73728 | bytes 98304 | tf_op jit(solution)/shard_map/convert_element_type | solution.py:25
  18.9 0.8 %fusion.8.spectrum_ref = f32[128,32]{1,0:T(8,128)} fusion(f32[128,64]{1,0:T(8,128)S(1)} %copy-done.3, f32[32,65]{0,1:T(8,128)S(1)} %get-tuple-element.20), kind=kOutput, calls=%fused_computation.30 | convolution fusion | flops 3145728 | bytes 114688 | tf_op jit(solution)/shard_map/dot_general | solution.py:49
  19.7 15.3 %all-to-all-done.gx_ref = bf16[16,2,128,128]{3,2,1,0:T(8,128)(2,1)S(1)} async-done(((bf16[16,2,128,128]{3,2,1,0:T(8,128)(2,1)}), bf16[16,2,128,128]{3,2,1,0:T(8,128)(2,1)S(1)}, u32[]{:S(2)}, u32[]{:S(2)}) %all-to-all-start) | async-done | bytes 1048608 | tf_op jit(solution)/shard_map/all_to_all | solution.py:178
  35.0 0.0 copy-start.1
  35.0 1.0 %copy-done.1 = bf16[16,2,128,128]{3,2,1,0:T(8,128)(2,1)} copy-done((bf16[16,2,128,128]{3,2,1,0:T(8,128)(2,1)}, bf16[16,2,128,128]{3,2,1,0:T(8,128)(2,1)S(1)}, u32[]{:S(2)}) %copy-start.1) | copy-done | bytes 1048600
  36.0 9.7 %spans.1 = (bf16[16,128,128]{2,1,0:T(8,128)(2,1)}, f32[32,128]{1,0:T(8,128)}) custom-call(s32[32]{0:T(128)} %spans_ref.1, bf16[16,2,128,128]{3,2,1,0:T(8,128)(2,1)} %copy-done.1, f32[32,128]{1,0:T(8,128)} %constant_dynamic-slice_fusion.weight_ref, f32[1,128]{1,0:T(1,128)} %dynamic-slice_bitcast_fusion.gain_ref, ...), custom_call_target="tpu_custom_call" | custom-call | tf_op jit(solution)/shard_map/spans/pallas_call | solution.py:184
  45.7 21.3 %all_to_all.10 = bf16[16,128,128]{2,1,0:T(8,128)(2,1)S(1)} all-to-all(bf16[16,128,128]{2,1,0:T(8,128)(2,1)} %get-tuple-element.4), channel_id=1, replica_groups=mesh['groups'=2,'seq'=16] {'seq'}, dimensions={0} | all-to-all | bytes 1048576 | tf_op jit(solution)/shard_map/all_to_all | solution.py:201
  67.0 0.3 copy.27
  67.3 1.0 %copy.28 = bf16[128,2048]{1,0:T(8,128)(2,1)} copy(bf16[128,2048]{0,1:T(8,128)(2,1)S(1)} %bitcast.19) | data formatting | bytes 1048576
  (9 shorter events, 0.1 us)
Async XLA Ops:
  0.6 14.8 %copy-start = (f32[32,2048]{1,0:T(8,128)S(1)}, f32[32,2048]{1,0:T(8,128)}, u32[]{:S(2)}) copy-start(f32[32,2048]{1,0:T(8,128)} %param.11) | copy-start | bytes 786436
  2.0 1.0 %copy-start.2 = (bf16[128,2048]{1,0:T(8,128)(2,1)S(1)}, bf16[128,2048]{1,0:T(8,128)(2,1)}, u32[]{:S(2)}) copy-start(bf16[128,2048]{1,0:T(8,128)(2,1)} %param.10) | copy-start | bytes 1572868
  4.7 30.3 %all-to-all-start = ((bf16[16,2,128,128]{3,2,1,0:T(8,128)(2,1)}), bf16[16,2,128,128]{3,2,1,0:T(8,128)(2,1)S(1)}, u32[]{:S(2)}, u32[]{:S(2)}) async-start(bf16[16,2,128,128]{3,2,1,0:T(8,128)(2,1)} %maximum_bitcast_fusion), calls=%async_computation | async-start | bytes 2097152 | tf_op jit(solution)/shard_map/all_to_all | solution.py:178
  12.1 0.7 copy-start.5
  12.1 0.7 copy-start.6
  13.3 2.7 %copy-start.3 = (f32[128,64]{1,0:T(8,128)S(1)}, f32[128,64]{1,0:T(8,128)}, u32[]{:S(2)}) copy-start(f32[128,64]{1,0:T(8,128)} %constant.14.clone) | copy-start | bytes 98308
  17.4 0.8 %copy-start.4 = (f32[64,128]{1,0:T(8,128)S(1)}, f32[64,128]{1,0:T(8,128)}, u32[]{:S(2)}) copy-start(f32[64,128]{1,0:T(8,128)} %constant.15.clone) | copy-start | bytes 98308
  35.0 1.0 %copy-start.1 = (bf16[16,2,128,128]{3,2,1,0:T(8,128)(2,1)}, bf16[16,2,128,128]{3,2,1,0:T(8,128)(2,1)S(1)}, u32[]{:S(2)}) copy-start(bf16[16,2,128,128]{3,2,1,0:T(8,128)(2,1)S(1)} %all-to-all-done.gx_ref) | copy-start | bytes 3145732

commit v2 on v1

v2 whole, which is shorter than its diff:
```python
import functools
import math

import jax
import jax.numpy as jnp
import numpy as np
from jax import lax
from jax.experimental import pallas as pl
from jax.experimental.pallas import tpu as pltpu
from jax.sharding import PartitionSpec as P

HIGHEST = lax.Precision.HIGHEST
F32 = jnp.float32
BF16 = jnp.bfloat16
LANES = 128


def halves(value):
    high = value.astype(BF16)
    return high, (value - high.astype(F32)).astype(BF16)


def table_halves(value):
    high = lax.reduce_precision(value, 8, 7)
    return high.astype(BF16), (value - high).astype(BF16)


def odd_frequencies(rows):
    angles = np.pi * np.outer(2 * np.arange(rows) + 1, np.arange(rows)) / (2 * rows)
    return np.cos(angles), -np.sin(angles)


def tables(rows, rates, freqs):
    cos_part, sin_part = odd_frequencies(rows)
    forward = jnp.asarray(np.concatenate([cos_part, sin_part], 0), F32)
    inverse = jnp.asarray(np.concatenate([cos_part, sin_part], 0).T / rows, F32)
    lags = jnp.arange(rows + 1).astype(F32)[None, :]
    decay = jnp.exp(-lags * rates[:, None])
    power_real = decay * jnp.cos(lags * freqs[:, None])
    power_imag = decay * jnp.sin(lags * freqs[:, None])
    to_start = jnp.concatenate([power_real[:, :rows], power_imag[:, :rows]], 0)
    to_end = jnp.concatenate([power_real[:, :0:-1], power_imag[:, :0:-1]], 0)
    left_g = jnp.concatenate(table_halves(jnp.concatenate([forward, to_start], 0)), 1)
    left_x = jnp.concatenate(table_halves(jnp.concatenate([forward, to_end], 0)), 1)
    back = jnp.concatenate(
        [inverse, power_real[:, :0:-1].T, -power_imag[:, :0:-1].T], 1
    )
    back_high, back_low = table_halves(back)
    basis_spectrum = jnp.dot(
        forward, power_real[:, :rows].T, precision=HIGHEST, preferred_element_type=F32
    )
    step = jnp.stack([power_real[:, rows], power_imag[:, rows]], 0)[:, :, None]
    return left_g, left_x, back_high, back_low, basis_spectrum, step


def pair(gx_ref, source, which):
    rows = gx_ref.shape[2] // 2
    first = gx_ref[source, which, :rows, :]
    second = gx_ref[source, which, rows:, :]
    both = jnp.concatenate([first, second], 1)
    return jnp.concatenate([both, both], 0)


def fill_slots(spans_ref, slot_of):
    for slot in range(slot_of.shape[0]):
        slot_of[spans_ref[slot]] = slot


def step_rows(step_ref, width):
    return (
        jnp.broadcast_to(step_ref[0], (step_ref.shape[1], width)),
        jnp.broadcast_to(step_ref[1], (step_ref.shape[1], width)),
    )


def input_kernel(
    spans_ref,
    gx_ref,
    weight_ref,
    gain_ref,
    left_g_ref,
    back_high_ref,
    back_low_ref,
    spectrum_ref,
    step_ref,
    y_ref,
    states_ref,
    slot_of,
    sums,
    high,
    low,
):
    n_src, _, rows_dev, width = gx_ref.shape
    rows = rows_dev // 2
    n_basis = weight_ref.shape[0]
    n_spans = 2 * n_src
    fill_slots(spans_ref, slot_of)
    weight = weight_ref[...]
    taps = jnp.dot(spectrum_ref[...], weight, precision=HIGHEST, preferred_element_type=F32)
    taps_real, taps_imag = taps[:rows], taps[rows:]
    left = left_g_ref[...]
    for source in range(n_src):
        of_g = jnp.dot(left, pair(gx_ref, source, 0), preferred_element_type=F32)
        for half in range(2):
            at = slice(half * width, (half + 1) * width)
            slot = 2 * source + half
            sums[slot] = of_g[2 * rows :, at]
            g_real, g_imag = of_g[:rows, at], of_g[rows : 2 * rows, at]
            y_real = halves(taps_real * g_real + taps_imag * g_imag)
            y_imag = halves(taps_real * g_imag - taps_imag * g_real)
            high[slot, :rows] = y_real[0]
            high[slot, rows : 2 * rows] = y_imag[0]
            low[slot, :rows] = y_real[1]
            low[slot, rows : 2 * rows] = y_imag[1]
    step_real, step_imag = step_rows(step_ref, width)
    state_real = jnp.zeros((n_basis, width), F32)
    state_imag = jnp.zeros((n_basis, width), F32)
    for span in range(n_spans - 1, -1, -1):
        slot = slot_of[span]
        states_ref[slot, :n_basis] = state_real
        states_ref[slot, n_basis:] = state_imag
        far_real, far_imag = halves(weight * state_real), halves(weight * state_imag)
        high[slot, 2 * rows : 2 * rows + n_basis] = far_real[0]
        high[slot, 2 * rows + n_basis :] = far_imag[0]
        low[slot, 2 * rows : 2 * rows + n_basis] = far_real[1]
        low[slot, 2 * rows + n_basis :] = far_imag[1]
        next_real = sums[slot, :n_basis] + step_real * state_real - step_imag * state_imag
        state_imag = sums[slot, n_basis:] + step_real * state_imag + step_imag * state_real
        state_real = next_real
    gain = gain_ref[...]
    back_high, back_low = back_high_ref[...], back_low_ref[...]
    for source in range(n_src):
        both_high = jnp.concatenate([high[2 * source], high[2 * source + 1]], 1)
        both_low = jnp.concatenate([low[2 * source], low[2 * source + 1]], 1)
        value = (
            jnp.dot(back_high, both_high, preferred_element_type=F32)
            + jnp.dot(back_high, both_low, preferred_element_type=F32)
            + jnp.dot(back_low, both_high, preferred_element_type=F32)
        )
        for half in range(2):
            at = slice(half * rows, (half + 1) * rows)
            own = gx_ref[source, 0, at, :].astype(F32)
            y_ref[source, at, :] = (
                value[:, half * width : (half + 1) * width] + gain * own
            ).astype(BF16)


def weight_kernel(
    gx_ref, states_ref, left_g_ref, left_x_ref, spectrum_ref, wgrad_ref
):
    n_src, _, rows_dev, width = gx_ref.shape
    rows = rows_dev // 2
    n_basis = wgrad_ref.shape[0]

    def analyse(source, carry):
        cross_real, cross_imag, total = carry
        of_g = jnp.dot(
            left_g_ref[: 2 * rows], pair(gx_ref, source, 0), preferred_element_type=F32
        )
        of_x = jnp.dot(left_x_ref[...], pair(gx_ref, source, 1), preferred_element_type=F32)
        for half in range(2):
            at = slice(half * width, (half + 1) * width)
            slot = 2 * source + half
            g_real, g_imag = of_g[:rows, at], of_g[rows : 2 * rows, at]
            x_real, x_imag = of_x[:rows, at], of_x[rows : 2 * rows, at]
            sum_real = of_x[2 * rows : 2 * rows + n_basis, at]
            sum_imag = of_x[2 * rows + n_basis :, at]
            cross_real = cross_real + (x_real * g_real + x_imag * g_imag)
            cross_imag = cross_imag + (x_real * g_imag - x_imag * g_real)
            total = total + (
                states_ref[slot, :n_basis] * sum_real - states_ref[slot, n_basis:] * sum_imag
            )
        return cross_real, cross_imag, total

    zero = jnp.zeros((rows, width), F32)
    empty = jnp.zeros((n_basis, width), F32)
    cross_real, cross_imag, total = lax.fori_loop(0, n_src, analyse, (zero, zero, empty))
    near = lax.dot_general(
        spectrum_ref[...],
        jnp.concatenate([cross_real, cross_imag], 0) * (1.0 / rows),
        (((0,), (0,)), ((), ())),
        precision=HIGHEST,
        preferred_element_type=F32,
    )
    wgrad_ref[...] = total + near


def on_device(inputs, grad_out, filter_weight, filter_rates, filter_freqs, skip_gain, span_of_slot):
    rows_dev, channels = inputs.shape
    rows = rows_dev // 2
    n_basis = filter_weight.shape[0]
    devices = lax.axis_size("seq")
    position = lax.axis_index("seq")
    own = channels // devices
    width = -(-own // LANES) * LANES
    widen = ((0, 0), (0, width - own))
    gx = lax.all_to_all(
        jnp.concatenate([grad_out, inputs], 0), "seq", 1, 0, tiled=True
    ).reshape(devices, 2, rows_dev, own)
    gx = jnp.pad(gx, ((0, 0), (0, 0)) + widen)
    weight = jnp.pad(lax.dynamic_slice_in_dim(filter_weight, position * own, own, 1), widen)
    gain = jnp.pad(lax.dynamic_slice_in_dim(skip_gain[None, :], position * own, own, 1), widen)
    left_g, left_x, back_high, back_low, spectrum, step = tables(
        rows, filter_rates, filter_freqs
    )
    n_spans = 2 * devices
    depth = 2 * rows + 2 * n_basis
    vmem = pl.BlockSpec(memory_space=pltpu.VMEM)
    y, states = pl.pallas_call(
        input_kernel,
        out_shape=(
            jax.ShapeDtypeStruct((devices, rows_dev, width), BF16),
            jax.ShapeDtypeStruct((n_spans, 2 * n_basis, width), F32),
        ),
        in_specs=[pl.BlockSpec(memory_space=pltpu.SMEM)] + [vmem] * 8,
        out_specs=(vmem, vmem),
        scratch_shapes=[
            pltpu.SMEM((n_spans,), jnp.int32),
            pltpu.VMEM((n_spans, 2 * n_basis, width), F32),
            pltpu.VMEM((n_spans, depth, width), BF16),
            pltpu.VMEM((n_spans, depth, width), BF16),
        ],
        name="input_part",
    )(span_of_slot, gx, weight, gain, left_g, back_high, back_low, spectrum, step)
    y = y[:, :, :own].reshape(devices * rows_dev, own)
    input_grad = lax.all_to_all(y, "seq", 0, 1, tiled=True)
    wgrad = pl.pallas_call(
        weight_kernel,
        out_shape=jax.ShapeDtypeStruct((n_basis, width), F32),
        in_specs=[vmem] * 5,
        out_specs=vmem,
        cost_estimate=pl.CostEstimate(
            flops=2 * 2 * depth * rows_dev * n_spans * width,
            bytes_accessed=4 * n_spans * rows_dev * width,
            transcendentals=0,
        ),
        name="weight_part",
    )(gx, states, left_g, left_x, spectrum)
    return input_grad, wgrad[:, :own]


def solution(mesh):
    placed = (
        P(("groups", "seq"), None),
        P(("groups", "seq"), None),
        P(),
        P(),
        P(),
        P(),
        P("groups"),
    )
    return jax.shard_map(
        on_device,
        mesh=mesh,
        in_specs=placed,
        out_specs=(P(("groups", "seq"), None), P("groups", "seq")),
        check_vma=False,
    )
```

time: 68.8 us -> 61.9 us (0.90)
  blocking collectives: 21.3 us -> 0 us
  waiting for transfers between devices: 15.3 us -> 25.4 us
  starting transfers between devices: 7.39 us -> 14.4 us
  local copies, waits for them, and re-layouts: 9.56 us -> 5.5 us
  other arithmetic: 3.45 us -> 4.78 us
    all_to_all x1 -> x0, blocking collectives: 21.3 us -> none  [on_device(): y = lax.all_to_all(y[:, :, :own], 'seq', 0, 0, tiled=True)]
    all_to_all x1 -> x2, waiting for transfers between devices: 15.3 us -> 25.4 us  [the longest x1 17.2 us: on_device(): lax.all_to_all(jnp.concatenate([grad_out, inputs], 0), 'seq', 1, 0, tiled...]
    all_to_all x1 -> x2, starting transfers between devices: 7.39 us -> 14.4 us  [the longest x1 7.53 us: on_device(): lax.all_to_all(jnp.concatenate([grad_out, inputs], 0), 'seq', 1, 0, tiled...]
    unnamed x17 -> x13, local copies, waits for them, and re-layouts: 5.79 us -> 2.01 us
    all_to_all x0 -> x1, other arithmetic: none -> 2.49 us  [on_device(): lax.all_to_all(jnp.concatenate([grad_out, inputs], 0), 'seq', 1, 0, tiled...]
    transpose x1 -> x0, other arithmetic: 1.08 us -> none  [on_device(): gx = lax.all_to_all(both.transpose(2, 0, 1, 3), 'seq', 0, 0, tiled=True)]
    pallas_call x1 -> x2, Pallas kernels: 9.69 us -> 9.75 us  [the longest x1 5.58 us: on_device(): pl.pallas_call(weight_kernel, out_shape=jax.ShapeDtypeStruct((n_basis, wi...]
  transfers between devices with their start and end apart: 1 -> 2, of which waited for: 1 -> 2; matrix products, arithmetic and copies ran while one was open for 9% -> 10% of each run, Pallas kernels for 0% -> 9%
where the time goes in v2:
time: 61.9 us; the launch traced here: 61.4 us
  waiting for transfers between devices  25.4 us (41%)
  starting transfers between devices  14.4 us (23%)
  Pallas kernels  9.75 us (16%)
  local copies, waits for them, and re-layouts  5.5 us (9%)
  other arithmetic  4.78 us (8%)
  matrix products  0.83 us (1%)
  between operations  0.74 us (1%)
    all_to_all x1, waiting for transfers between devices, on_device(): lax.all_to_all(jnp.concatenate([grad_out, inputs], 0), 'seq', 1, 0, tiled...  17.2 us
    all_to_all x1, waiting for transfers between devices, on_device(): input_grad = lax.all_to_all(y, 'seq', 0, 1, tiled=True)  8.19 us
    all_to_all x1, starting transfers between devices, on_device(): lax.all_to_all(jnp.concatenate([grad_out, inputs], 0), 'seq', 1, 0, tiled...  7.53 us
    all_to_all x1, starting transfers between devices, on_device(): input_grad = lax.all_to_all(y, 'seq', 0, 1, tiled=True)  6.87 us
    pallas_call x1, Pallas kernels, on_device(): pl.pallas_call(weight_kernel, out_shape=jax.ShapeDtypeStruct((n_basis, wi...  5.58 us
    pallas_call x1, Pallas kernels, on_device(): pl.pallas_call(input_kernel, out_shape=(jax.ShapeDtypeStruct((devices, ro...  4.17 us
    all_to_all x1, other arithmetic, on_device(): lax.all_to_all(jnp.concatenate([grad_out, inputs], 0), 'seq', 1, 0, tiled...  2.49 us
    unnamed x13, local copies, waits for them, and re-layouts  2.01 us
  transfers between devices with their start and end apart: 2, of which 2 were waited for; matrix products, arithmetic and copies ran while one was open for 10% of the time, Pallas kernels for 9%

profile of v2, /device:TPU:0, one launch (start us, length us, event | category | flops | bytes accessed | tf_op | source)
XLA Modules:
  0.0 61.4 jit_solution(11061278751342604621)
XLA Ops:
  0.6 0.0 copy-start
  0.6 2.5 %copy_bitcast_fusion = bf16[256,16,128]{2,0,1:T(8,128)(2,1)} fusion(bf16[128,2048]{1,0:T(8,128)(2,1)} %param.9, bf16[128,2048]{1,0:T(8,128)(2,1)} %param.10), kind=kLoop, calls=%fused_computation | loop fusion | flops 2097152 | bytes 2097152 | tf_op jit(solution)/shard_map/all_to_all | solution.py:197
  3.1 0.0 copy-start.4
  3.1 0.0 copy-start.5
  3.1 0.0 copy-start.2
  3.1 0.0 copy-start.3
  3.1 7.5 %all-to-all-start = ((bf16[256,16,128]{2,0,1:T(8,128)(2,1)}), bf16[256,16,128]{2,0,1:T(8,128)(2,1)S(1)}, u32[]{:S(2)}, u32[]{:S(2)}) async-start(bf16[256,16,128]{2,0,1:T(8,128)(2,1)} %copy_bitcast_fusion), calls=%async_computation | async-start | bytes 2097152 | tf_op jit(solution)/shard_map/all_to_all | solution.py:197
  10.7 0.0 copy-done.4
  10.7 0.0 copy-done.5
  10.7 0.1 fusion.5
  10.9 0.2 slice_reduce_fusion
  11.1 0.7 %copy.21.step_ref = f32[2,32,1]{2,1,0:T(8,128)} copy(f32[2,32,1]{1,0,2:T(2,128)S(1)} %maximum_bitcast_fusion.1) | data formatting | bytes 512 | tf_op jit(solution)/shard_map/broadcast_in_dim | solution.py:52
  11.8 0.1 fusion.10
  11.9 0.1 rev.8
  11.9 0.1 rev.9
  12.0 0.1 copy.19
  12.1 0.1 copy.18
  12.2 1.3 %dynamic-slice_bitcast_fusion.gain_ref = f32[1,128]{1,0:T(1,128)} fusion(f32[2048]{0:T(1024)} %param.14, s32[]{:T(128)S(6)} %select_n.4), kind=kLoop, calls=%fused_computation.28 | loop fusion | bytes 1028 | tf_op jit(solution)/shard_map/dynamic_slice | solution.py:202
  13.5 0.0 copy-done
  13.5 0.6 constant_dynamic-slice_fusion.weight_ref
  14.1 0.0 copy-done.2
  14.2 0.7 %pad_maximum_fusion.3.left_g_ref = bf16[192,128]{1,0:T(8,128)(2,1)} fusion(bf16[192,64]{1,0:T(8,128)(2,1)S(1)} %get-tuple-element.14, bf16[192,64]{1,0:T(8,128)(2,1)S(1)} %get-tuple-element.15), kind=kLoop, calls=%fused_computation.16 | loop fusion | flops 98304 | bytes 98304 | tf_op jit(solution)/shard_map/concatenate | solution.py:43
  14.9 0.0 copy-done.3
  14.9 0.7 %fusion.4 = (bf16[64,192]{1,0:T(8,128)(2,1)}, bf16[64,192]{1,0:T(8,128)(2,1)}) fusion(f32[64,32]{1,0:T(8,128)S(1)} %copy.19, f32[64,32]{1,0:T(8,128)S(1)} %copy.18, f32[64,128]{1,0:T(8,128)S(1)} %copy-done.3), kind=kLoop, calls=%fused_computation.14 | loop fusion | flops 73728 | bytes 98304 | tf_op jit(solution)/shard_map/convert_element_type | solution.py:25
  15.6 0.8 %fusion.8.spectrum_ref = f32[128,32]{1,0:T(8,128)} fusion(f32[128,64]{1,0:T(8,128)S(1)} %copy-done.2, f32[32,65]{1,0:T(8,128)S(1)} %get-tuple-element.20), kind=kOutput, calls=%fused_computation.31 | convolution fusion | flops 3145728 | bytes 57472 | tf_op jit(solution)/shard_map/dot_general | solution.py:49
  16.4 17.2 %all-to-all-done = bf16[256,16,128]{2,0,1:T(8,128)(2,1)S(1)} async-done(((bf16[256,16,128]{2,0,1:T(8,128)(2,1)}), bf16[256,16,128]{2,0,1:T(8,128)(2,1)S(1)}, u32[]{:S(2)}, u32[]{:S(2)}) %all-to-all-start) | async-done | bytes 1048608 | tf_op jit(solution)/shard_map/all_to_all | solution.py:197
  33.6 0.0 copy-start.1
  33.6 1.0 %copy-done.1 = bf16[256,16,128]{2,0,1:T(8,128)(2,1)} copy-done((bf16[256,16,128]{2,0,1:T(8,128)(2,1)}, bf16[256,16,128]{2,0,1:T(8,128)(2,1)S(1)}, u32[]{:S(2)}) %copy-start.1) | copy-done | bytes 1048600
  34.6 4.2 %input_part.1 = (bf16[16,128,128]{2,1,0:T(8,128)(2,1)}, f32[32,64,128]{2,1,0:T(8,128)}) custom-call(s32[32]{0:T(128)} %spans_ref.1, bf16[16,2,128,128]{3,2,1,0:T(8,128)(2,1)} %bitcast.20, f32[32,128]{1,0:T(8,128)} %constant_dynamic-slice_fusion.weight_ref, f32[1,128]{1,0:T(1,128)} %dynamic-slice_bitcast_fusion.gain_ref, ...), custom_call_target="tpu_custom_call" | custom-call | tf_op jit(solution)/shard_map/input_part/pallas_call | solution.py:209
  38.8 6.9 %all-to-all-start.1 = ((bf16[16,128,128]{2,1,0:T(8,128)(2,1)}), bf16[16,128,128]{2,1,0:T(8,128)(2,1)S(1)}, u32[]{:S(2)}, u32[]{:S(2)}) async-start(bf16[16,128,128]{2,1,0:T(8,128)(2,1)} %get-tuple-element.4), calls=%async_computation.1 | async-start | bytes 1048576 | tf_op jit(solution)/shard_map/all_to_all | solution.py:226
  45.7 0.7 %pad_maximum_fusion.4.left_x_ref = bf16[192,128]{1,0:T(8,128)(2,1)} fusion(bf16[192,64]{1,0:T(8,128)(2,1)S(1)} %get-tuple-element.9, bf16[192,64]{1,0:T(8,128)(2,1)S(1)} %get-tuple-element.8), kind=kLoop, calls=%fused_computation.17 | loop fusion | flops 98304 | bytes 98304 | tf_op jit(solution)/shard_map/concatenate | solution.py:44
  46.4 5.6 %weight_part.1 = f32[32,128]{1,0:T(8,128)} custom-call(bf16[16,2,128,128]{3,2,1,0:T(8,128)(2,1)} %bitcast.21, f32[32,64,128]{2,1,0:T(8,128)} %get-tuple-element.5.states_ref, bf16[192,128]{1,0:T(8,128)(2,1)} %pad_maximum_fusion.3.left_g_ref, bf16[192,128]{1,0:T(8,128)(2,1)} %pad_maximum_fusion.4.left_x_ref, f32[128,32]{1,0:T(8,128)} %fusion.8.spectrum_ref), custom_call_target="tpu_custom_call" | custom-call | flops 402653184 | bytes 2097152 | tf_op jit(solution)/shard_map/weight_part/pallas_call | solution.py:227
  51.9 8.2 %all-to-all-done.1 = bf16[16,128,128]{2,1,0:T(8,128)(2,1)S(1)} async-done(((bf16[16,128,128]{2,1,0:T(8,128)(2,1)}), bf16[16,128,128]{2,1,0:T(8,128)(2,1)S(1)}, u32[]{:S(2)}, u32[]{:S(2)}) %all-to-all-start.1) | async-done | bytes 524320 | tf_op jit(solution)/shard_map/all_to_all | solution.py:226
  60.1 0.3 copy.22
  60.4 1.0 %copy.24 = bf16[128,2048]{1,0:T(8,128)(2,1)} copy(bf16[128,2048]{0,1:T(8,128)(2,1)S(1)} %bitcast.23) | data formatting | bytes 1048576
  (5 shorter events, 0.1 us)
Async XLA Ops:
  0.6 12.9 %copy-start = (f32[32,2048]{1,0:T(8,128)S(1)}, f32[32,2048]{1,0:T(8,128)}, u32[]{:S(2)}) copy-start(f32[32,2048]{1,0:T(8,128)} %param.11) | copy-start | bytes 786436
  3.1 7.6 %copy-start.4 = (f32[32]{0:T(128)S(1)}, f32[32]{0:T(128)}, u32[]{:S(2)}) copy-start(f32[32]{0:T(128)} %param.13) | copy-start | bytes 388
  3.1 7.6 %copy-start.5 = (f32[32]{0:T(128)S(1)}, f32[32]{0:T(128)}, u32[]{:S(2)}) copy-start(f32[32]{0:T(128)} %param.12) | copy-start | bytes 388
  3.1 11.0 %copy-start.2 = (f32[128,64]{1,0:T(8,128)S(1)}, f32[128,64]{1,0:T(8,128)}, u32[]{:S(2)}) copy-start(f32[128,64]{1,0:T(8,128)} %constant.14.clone) | copy-start | bytes 98308
  3.1 11.7 %copy-start.3 = (f32[64,128]{1,0:T(8,128)S(1)}, f32[64,128]{1,0:T(8,128)}, u32[]{:S(2)}) copy-start(f32[64,128]{1,0:T(8,128)} %constant.15.clone) | copy-start | bytes 98308
  3.1 30.5 %all-to-all-start = ((bf16[256,16,128]{2,0,1:T(8,128)(2,1)}), bf16[256,16,128]{2,0,1:T(8,128)(2,1)S(1)}, u32[]{:S(2)}, u32[]{:S(2)}) async-start(bf16[256,16,128]{2,0,1:T(8,128)(2,1)} %copy_bitcast_fusion), calls=%async_computation | async-start | bytes 2097152 | tf_op jit(solution)/shard_map/all_to_all | solution.py:197
  33.6 1.0 %copy-start.1 = (bf16[256,16,128]{2,0,1:T(8,128)(2,1)}, bf16[256,16,128]{2,0,1:T(8,128)(2,1)S(1)}, u32[]{:S(2)}) copy-start(bf16[256,16,128]{2,0,1:T(8,128)(2,1)S(1)} %all-to-all-done) | copy-start | bytes 3145732
  38.8 21.3 %all-to-all-start.1 = ((bf16[16,128,128]{2,1,0:T(8,128)(2,1)}), bf16[16,128,128]{2,1,0:T(8,128)(2,1)S(1)}, u32[]{:S(2)}, u32[]{:S(2)}) async-start(bf16[16,128,128]{2,1,0:T(8,128)(2,1)} %get-tuple-element.4), calls=%async_computation.1 | async-start | bytes 1048576 | tf_op jit(solution)/shard_map/all_to_all | solution.py:226

commit v3 on v2

v3 whole, which is shorter than its diff:
```python
import functools
import math

import jax
import jax.numpy as jnp
import numpy as np
from jax import lax
from jax.experimental import pallas as pl
from jax.experimental.pallas import tpu as pltpu
from jax.sharding import PartitionSpec as P

HIGHEST = lax.Precision.HIGHEST
F32 = jnp.float32
BF16 = jnp.bfloat16
LANES = 128


def halves(value):
    high = value.astype(BF16)
    return high, (value - high.astype(F32)).astype(BF16)


def table_halves(value):
    high = lax.reduce_precision(value, 8, 7)
    return high.astype(BF16), (value - high).astype(BF16)


def odd_frequencies(rows):
    angles = np.pi * np.outer(2 * np.arange(rows) + 1, np.arange(rows)) / (2 * rows)
    return np.cos(angles), -np.sin(angles)


def tables(rows, rates, freqs):
    cos_part, sin_part = odd_frequencies(rows)
    forward = jnp.asarray(np.concatenate([cos_part, sin_part], 0), F32)
    inverse = jnp.asarray(np.concatenate([cos_part, sin_part], 0).T / rows, F32)
    lags = jnp.arange(rows + 1).astype(F32)[None, :]
    decay = jnp.exp(-lags * rates[:, None])
    power_real = decay * jnp.cos(lags * freqs[:, None])
    power_imag = decay * jnp.sin(lags * freqs[:, None])
    to_start = jnp.concatenate([power_real[:, :rows], power_imag[:, :rows]], 0)
    to_end = jnp.concatenate([power_real[:, :0:-1], power_imag[:, :0:-1]], 0)
    left_g = jnp.concatenate(table_halves(jnp.concatenate([forward, to_start], 0)), 1)
    left_x = jnp.concatenate(table_halves(jnp.concatenate([forward, to_end], 0)), 1)
    back = jnp.concatenate(
        [inverse, power_real[:, :0:-1].T, -power_imag[:, :0:-1].T], 1
    )
    back_high, back_low = table_halves(back)
    basis_spectrum = jnp.dot(
        forward, power_real[:, :rows].T, precision=HIGHEST, preferred_element_type=F32
    )
    step = jnp.stack([power_real[:, rows], power_imag[:, rows]], 0)[:, :, None]
    return left_g, left_x, back_high, back_low, basis_spectrum, step


def side_by_side(ref, source, part):
    rows = ref.shape[2] // 2
    at = slice(part * rows, (part + 1) * rows)
    return jnp.concatenate([ref[source, 0, at, :], ref[source, 1, at, :]], 1)


def twice(value):
    return jnp.concatenate([value, value], 0)


def input_kernel(
    spans_ref,
    place_ref,
    g_ref,
    weight_ref,
    gain_ref,
    left_g_ref,
    back_high_ref,
    back_low_ref,
    spectrum_ref,
    step_ref,
    y_ref,
    states_ref,
    slot_of,
    sums,
    states,
    high,
    low,
):
    n_src, _, rows_dev, width = g_ref.shape
    rows = rows_dev // 2
    n_basis, lanes = weight_ref.shape
    n_spans = 2 * n_src
    n_own = n_src // 2
    own_base = place_ref[0] * n_own
    far_base = n_own - own_base
    for slot in range(n_spans):
        slot_of[spans_ref[slot]] = slot
    weight = weight_ref[...]
    taps = jnp.dot(spectrum_ref[...], weight, precision=HIGHEST, preferred_element_type=F32)
    taps_real, taps_imag = taps[:rows], taps[rows:]
    left = left_g_ref[...]
    for source in range(n_own):
        for part in range(2):
            far = twice(side_by_side(g_ref, far_base + source, part))
            sums[2 * (far_base + source) + part] = jnp.dot(
                left[2 * rows :], far, preferred_element_type=F32
            )
            near = twice(side_by_side(g_ref, own_base + source, part))
            of_g = jnp.dot(left, near, preferred_element_type=F32)
            sums[2 * (own_base + source) + part] = of_g[2 * rows :]
            g_real, g_imag = of_g[:rows], of_g[rows : 2 * rows]
            y_real = halves(taps_real * g_real + taps_imag * g_imag)
            y_imag = halves(taps_real * g_imag - taps_imag * g_real)
            slot = 2 * source + part
            high[slot, :rows] = y_real[0]
            high[slot, rows:] = y_imag[0]
            low[slot, :rows] = y_real[1]
            low[slot, rows:] = y_imag[1]
    step_real = jnp.broadcast_to(step_ref[0], (n_basis, lanes))
    step_imag = jnp.broadcast_to(step_ref[1], (n_basis, lanes))
    state_real = jnp.zeros((n_basis, lanes), F32)
    state_imag = jnp.zeros((n_basis, lanes), F32)
    for span in range(n_spans - 1, -1, -1):
        slot = slot_of[span]
        states[slot, :n_basis] = state_real
        states[slot, n_basis:] = state_imag
        if span:
            next_real = sums[slot, :n_basis] + step_real * state_real - step_imag * state_imag
            state_imag = sums[slot, n_basis:] + step_real * state_imag + step_imag * state_real
            state_real = next_real
    gain = gain_ref[...]
    back_high, back_low = back_high_ref[...], back_low_ref[...]
    both_weight = twice(weight)
    for source in range(n_own):
        for part in range(2):
            slot = 2 * source + part
            state = states[2 * own_base + slot]
            states_ref[slot] = state
            far = halves(both_weight * state)
            both_high = jnp.concatenate([high[slot], far[0]], 0)
            both_low = jnp.concatenate([low[slot], far[1]], 0)
            value = (
                jnp.dot(back_high, both_high, preferred_element_type=F32)
                + jnp.dot(back_high, both_low, preferred_element_type=F32)
                + jnp.dot(back_low, both_high, preferred_element_type=F32)
                + gain * side_by_side(g_ref, own_base + source, part).astype(F32)
            ).astype(BF16)
            at = slice(part * rows, (part + 1) * rows)
            y_ref[source, 0, at, :] = value[:, :width]
            y_ref[source, 1, at, :] = value[:, width:]


def weight_kernel(place_ref, g_ref, states_ref, left_g_ref, left_x_ref, spectrum_ref, *refs):
    x_refs, wgrad_ref = refs[:-1], refs[-1]
    n_own = len(x_refs)
    rows_dev, width = g_ref.shape[2:]
    rows = rows_dev // 2
    n_basis, lanes = states_ref.shape[1] // 2, states_ref.shape[2]
    half, own = place_ref[0], place_ref[1]
    left_g, left_x = left_g_ref[: 2 * rows], left_x_ref[...]
    cross_real = jnp.zeros((rows, lanes), F32)
    cross_imag = jnp.zeros((rows, lanes), F32)
    total = jnp.zeros((n_basis, lanes), F32)
    for offset, x_ref in enumerate(x_refs):
        source = own ^ offset
        for part in range(2):
            at = slice(part * rows, (part + 1) * rows)
            g = twice(side_by_side(g_ref, half * n_own + source, part))
            x = twice(jnp.concatenate([x_ref[0, at, :], x_ref[1, at, :]], 1))
            of_g = jnp.dot(left_g, g, preferred_element_type=F32)
            of_x = jnp.dot(left_x, x, preferred_element_type=F32)
            g_real, g_imag = of_g[:rows], of_g[rows:]
            x_real, x_imag = of_x[:rows], of_x[rows : 2 * rows]
            cross_real = cross_real + (x_real * g_real + x_imag * g_imag)
            cross_imag = cross_imag + (x_real * g_imag - x_imag * g_real)
            product = states_ref[2 * source + part] * of_x[2 * rows :]
            total = total + (product[:n_basis] - product[n_basis:])
    total = total + lax.dot_general(
        spectrum_ref[...],
        jnp.concatenate([cross_real, cross_imag], 0) * (1.0 / rows),
        (((0,), (0,)), ((), ())),
        precision=HIGHEST,
        preferred_element_type=F32,
    )
    for block in range(2):
        wgrad_ref[half ^ block] = total[:, block * width : (block + 1) * width]


def on_device(inputs, grad_out, filter_weight, filter_rates, filter_freqs, skip_gain, span_of_slot):
    rows_dev, channels = inputs.shape
    rows = rows_dev // 2
    n_basis = filter_weight.shape[0]
    devices = lax.axis_size("seq")
    position = lax.axis_index("seq")
    n_own = devices // 2
    half, rank = position // n_own, position % n_own
    own = channels // devices
    width = -(-own // LANES) * LANES
    lanes = 2 * width

    def widened(value):
        return jnp.pad(value, ((0, 0),) * (value.ndim - 1) + ((0, width - own),))

    def own_blocks(value):
        blocks = value.reshape(value.shape[0], 2, n_own, own)
        taken = lax.dynamic_index_in_dim(blocks, rank, 2, keepdims=False)
        return widened(taken).reshape(value.shape[0], lanes)

    blocks = grad_out.reshape(rows_dev, 2, n_own, own).transpose(2, 1, 0, 3)
    g = widened(lax.all_to_all(jnp.concatenate([blocks, blocks], 0), "seq", 0, 0, tiled=True))
    x_blocks = inputs.reshape(rows_dev, 2, n_own, own)
    x_parts = []
    for offset in range(n_own):
        part = lax.dynamic_index_in_dim(x_blocks, rank ^ offset, 2, keepdims=False)
        part = part.transpose(1, 0, 2)
        if offset:
            part = lax.ppermute(part, "seq", [(i, i ^ offset) for i in range(devices)])
        x_parts.append(widened(part))
    weight = own_blocks(filter_weight)
    gain = own_blocks(skip_gain[None, :])
    place = jnp.stack([half, rank]).astype(jnp.int32)
    left_g, left_x, back_high, back_low, spectrum, step = tables(
        rows, filter_rates, filter_freqs
    )
    n_spans = 2 * devices
    smem = pl.BlockSpec(memory_space=pltpu.SMEM)
    vmem = pl.BlockSpec(memory_space=pltpu.VMEM)
    params = pltpu.CompilerParams(vmem_limit_bytes=24 * 2**20)
    y, states = pl.pallas_call(
        input_kernel,
        out_shape=(
            jax.ShapeDtypeStruct((n_own, 2, rows_dev, width), BF16),
            jax.ShapeDtypeStruct((devices, 2 * n_basis, lanes), F32),
        ),
        in_specs=[smem, smem] + [vmem] * 8,
        out_specs=(vmem, vmem),
        scratch_shapes=[
            pltpu.SMEM((n_spans,), jnp.int32),
            pltpu.VMEM((n_spans, 2 * n_basis, lanes), F32),
            pltpu.VMEM((n_spans, 2 * n_basis, lanes), F32),
            pltpu.VMEM((devices, 2 * rows, lanes), BF16),
            pltpu.VMEM((devices, 2 * rows, lanes), BF16),
        ],
        compiler_params=params,
        name="input_part",
    )(span_of_slot, place, g, weight, gain, left_g, back_high, back_low, spectrum, step)
    y = lax.all_to_all(
        y[..., :own],
        "seq",
        0,
        0,
        tiled=True,
        axis_index_groups=[list(range(n_own)), list(range(n_own, devices))],
    )
    input_grad = y.transpose(2, 1, 0, 3).reshape(rows_dev, channels)
    wgrad = pl.pallas_call(
        weight_kernel,
        out_shape=jax.ShapeDtypeStruct((2, n_basis, width), F32),
        in_specs=[smem] + [vmem] * (5 + n_own),
        out_specs=vmem,
        compiler_params=params,
        cost_estimate=pl.CostEstimate(
            flops=8 * (rows + n_basis) * rows * n_spans * lanes,
            bytes_accessed=4 * n_spans * rows * lanes,
            transcendentals=0,
        ),
        name="weight_part",
    )(place, g, states, left_g, left_x, spectrum, *x_parts)
    other = lax.ppermute(wgrad[1], "seq", [(i, i ^ n_own) for i in range(devices)])
    return input_grad, (wgrad[0] + other)[:, :own]


def solution(mesh):
    placed = (
        P(("groups", "seq"), None),
        P(("groups", "seq"), None),
        P(),
        P(),
        P(),
        P(),
        P("groups"),
    )
    return jax.shard_map(
        on_device,
        mesh=mesh,
        in_specs=placed,
        out_specs=(P(("groups", "seq"), None), P("groups", "seq")),
        check_vma=False,
    )
```

time: 61.9 us -> 68.3 us (1.10)
  starting transfers between devices: 14.4 us -> 23.5 us
  Pallas kernels: 9.75 us -> 5.36 us
  local copies, waits for them, and re-layouts: 5.5 us -> 8.23 us
  other arithmetic: 4.78 us -> 2.23 us
  waiting for transfers between devices: 25.4 us -> 27.3 us
    ppermute x0 -> x8, starting transfers between devices: none -> 10.1 us  [the longest x7 7.38 us: on_device(): part = lax.ppermute(part, 'seq', [(i, i ^ offset) for i in range(devices)])]
    ppermute x0 -> x8, waiting for transfers between devices: none -> 7.3 us  [the longest x7 5.27 us: on_device(): part = lax.ppermute(part, 'seq', [(i, i ^ offset) for i in range(devices)])]
    all_to_all x2, waiting for transfers between devices: 25.4 us -> 20 us  [the longest x1 20 us: on_device(): lax.all_to_all(jnp.concatenate([blocks, blocks], 0), 'seq', 0, 0, tiled=T...]
    pallas_call x2, Pallas kernels: 9.75 us -> 5.36 us  [the longest x1 3.62 us: on_device(): pl.pallas_call(input_kernel, out_shape=(jax.ShapeDtypeStruct((n_own, 2, r...]
    unnamed x13 -> x27, local copies, waits for them, and re-layouts: 2.01 us -> 5.71 us
    all_to_all x1 -> x0, other arithmetic: 2.49 us -> none  [on_device(): lax.all_to_all(jnp.concatenate([grad_out, inputs], 0), 'seq', 1, 0, tiled...]
    concatenate x0 -> x1, other arithmetic: none -> 1.09 us  [on_device(): jnp.concatenate([blocks, blocks], 0)]
    all_to_all x2, starting transfers between devices: 14.4 us -> 13.4 us  [the longest x1 7.52 us: on_device(): lax.all_to_all(jnp.concatenate([blocks, blocks], 0), 'seq', 0, 0, tiled=T...]
  transfers between devices with their start and end apart: 2 -> 10, of which waited for: 2 -> 5; matrix products, arithmetic and copies ran while one was open for 10% -> 7% of each run, Pallas kernels for 9% -> 3%
where the time goes in v3:
time: 68.3 us; the launch traced here: 67.8 us
  waiting for transfers between devices  27.3 us (40%)
  starting transfers between devices  23.5 us (34%)
  local copies, waits for them, and re-layouts  8.23 us (12%)
  Pallas kernels  5.36 us (8%)
  other arithmetic  2.23 us (3%)
  between operations  0.98 us (1%)
    all_to_all x1, waiting for transfers between devices, on_device(): lax.all_to_all(jnp.concatenate([blocks, blocks], 0), 'seq', 0, 0, tiled=T...  20 us
    all_to_all x1, starting transfers between devices, on_device(): lax.all_to_all(jnp.concatenate([blocks, blocks], 0), 'seq', 0, 0, tiled=T...  7.52 us
    ppermute x7, starting transfers between devices, on_device(): part = lax.ppermute(part, 'seq', [(i, i ^ offset) for i in range(devices)])  7.38 us
    all_to_all x1, starting transfers between devices, on_device(): lax.all_to_all(y[..., :own], 'seq', 0, 0, tiled=True, axis_index_groups=[...  5.89 us
    unnamed x27, local copies, waits for them, and re-layouts  5.71 us
    ppermute x7, waiting for transfers between devices, on_device(): part = lax.ppermute(part, 'seq', [(i, i ^ offset) for i in range(devices)])  5.27 us
    pallas_call x1, Pallas kernels, on_device(): pl.pallas_call(input_kernel, out_shape=(jax.ShapeDtypeStruct((n_own, 2, r...  3.62 us
    ppermute x1, starting transfers between devices, on_device(): lax.ppermute(wgrad[1], 'seq', [(i, i ^ n_own) for i in range(devices)])  2.67 us
  transfers between devices with their start and end apart: 10, of which 5 were waited for; matrix products, arithmetic and copies ran while one was open for 7% of the time, Pallas kernels for 3%

profile of v3, /device:TPU:0, one launch (start us, length us, event | category | flops | bytes accessed | tf_op | source)
XLA Modules:
  0.0 67.8 jit_solution(15055795568941679748)
XLA Ops:
  0.6 0.0 copy-start
  0.6 1.3 %copy.25 = bf16[128,2048]{0,1:T(8,128)(2,1)S(1)} copy(bf16[128,2048]{1,0:T(8,128)(2,1)} %param.10) | data formatting | bytes 1048576 | tf_op args[1]
  2.0 0.3 copy.26
  2.3 1.1 %pad_maximum_fusion = bf16[16,2,128,128]{3,2,1,0:T(8,128)(2,1)} fusion(bf16[8,2,128,128]{3,2,1,0:T(8,128)(2,1)S(1)} %bitcast.80), kind=kLoop, calls=%fused_computation | loop fusion | flops 524288 | bytes 1572864 | tf_op jit(solution)/shard_map/concatenate | solution.py:206
  3.4 0.0 copy-start.5
  3.4 0.0 copy-start.6
  3.4 7.5 %all-to-all-start = ((bf16[16,2,128,128]{3,2,1,0:T(8,128)(2,1)}), bf16[16,2,128,128]{3,2,1,0:T(8,128)(2,1)S(1)}, u32[]{:S(2)}, u32[]{:S(2)}) async-start(bf16[16,2,128,128]{3,2,1,0:T(8,128)(2,1)} %pad_maximum_fusion), calls=%async_computation | async-start | bytes 2097152 | tf_op jit(solution)/shard_map/all_to_all | solution.py:206
  10.9 0.0 copy-start.3
  10.9 0.0 copy-done.5
  11.0 0.0 copy-done.6
  11.0 0.1 fusion.5
  11.1 0.2 slice_reduce_fusion
  11.3 0.1 copy.31.step_ref
  11.4 0.1 fusion.12
  11.5 0.1 rev.8
  11.5 0.1 rev.9
  11.6 0.1 copy.29
  11.7 0.1 copy.28
  11.8 0.0 copy-done.3
  11.9 0.0 copy-start.2
  12.0 0.1 pad_add_fusion.place_ref
  12.0 0.0 copy-done
  12.1 0.7 %copy-done.2 = f32[128,64]{1,0:T(8,128)S(1)} copy-done((f32[128,64]{1,0:T(8,128)S(1)}, f32[128,64]{1,0:T(8,128)}, u32[]{:S(2)}) %copy-start.2) | copy-done | bytes 32792
  12.8 0.0 copy-start.4
  12.8 0.1 pad_maximum_fusion.4.left_g_ref
  12.9 0.7 copy-done.4
  13.5 0.1 fusion.4
  13.6 0.2 fusion.10.spectrum_ref
  13.8 20.0 %all-to-all-done.g_ref = bf16[16,2,128,128]{3,2,1,0:T(8,128)(2,1)S(1)} async-done(((bf16[16,2,128,128]{3,2,1,0:T(8,128)(2,1)}), bf16[16,2,128,128]{3,2,1,0:T(8,128)(2,1)S(1)}, u32[]{:S(2)}, u32[]{:S(2)}) %all-to-all-start) | async-done | bytes 1048608 | tf_op jit(solution)/shard_map/all_to_all | solution.py:206
  33.8 0.0 copy-start.1
  33.8 0.7 copy-done.1
  34.5 3.6 %input_part.1 = (bf16[8,2,128,128]{3,2,1,0:T(8,128)(2,1)}, f32[16,64,256]{2,1,0:T(8,128)S(1)}) custom-call(s32[32]{0:T(128)S(1)} %copy-done.1, s32[2]{0:T(128)S(1)} %pad_add_fusion.place_ref, bf16[16,2,128,128]{3,2,1,0:T(8,128)(2,1)S(1)} %all-to-all-done.g_ref, f32[32,256]{1,0:T(8,128)S(1)} %bitcast.78, f32[1,256]{1,0:T(1,128)S(1)} %fusion.8.gain_ref, ...), custom_call_target="tpu_custom_call" | custom-call | tf_op jit(solution)/shard_map/input_part/pallas_call | solution.py:225
  38.1 5.9 %all-to-all-start.1 = ((bf16[8,2,128,128]{3,2,1,0:T(8,128)(2,1)}), bf16[8,2,128,128]{3,2,1,0:T(8,128)(2,1)S(1)}, u32[]{:S(2)}, u32[]{:S(2)}) async-start(bf16[8,2,128,128]{3,2,1,0:T(8,128)(2,1)} %get-tuple-element.4), calls=%async_computation.1 | async-start | bytes 1048576 | tf_op jit(solution)/shard_map/all_to_all | solution.py:243
  44.0 1.1 %copy.55 = bf16[16,8,16,128]{3,2,1,0:T(8,128)(2,1)S(1)} copy(bf16[16,8,16,128]{3,1,2,0:T(8,128)(2,1)} %bitcast.84) | data formatting | bytes 1048576
  45.2 1.2 %constant_dynamic-slice_fusion = (bf16[128,2,1,128]{3,2,1,0:T(2,128)(2,1)S(1)}, bf16[128,2,1,128]{3,2,1,0:T(2,128)(2,1)S(1)}, bf16[128,2,1,128]{3,2,1,0:T(2,128)...) fusion(bf16[128,2,8,128]{3,2,1,0:T(8,128)(2,1)S(1)} %bitcast.79, ...), kind=kLoop, calls=%fused_computation.37 | loop fusion | bytes 1048608 | tf_op jit(solution)/shard_map/jit(dynamic_index_in_dim)/dynamic_slice | solution.py:210
  46.4 0.6 collective-permute-start
  47.0 1.7 %collective-permute-start.1 = (bf16[2,128,128]{2,1,0:T(8,128)(2,1)S(1)}, bf16[2,128,128]{2,1,0:T(8,128)(2,1)S(1)}, u32[]{:S(2)}, u32[]{:S(2)}) collective-permute-start(bf16[2,128,128]{2,1,0:T(8,128)(2,1)S(1)} %bitcast.93), channel_id=1, source_target_pairs={{0,2},{1,3},{2,0},{3,1},{4,6},{5,7},{6,4},{7,5},{8,10},{9,11},{10,... | collective-permute-start | bytes 196616 | tf_op jit(solution)/shard_map/ppermute | solution.py:213
  48.8 0.1 collective-permute-start.2
  48.9 1.7 %collective-permute-start.3 = (bf16[2,128,128]{2,1,0:T(8,128)(2,1)S(1)}, bf16[2,128,128]{2,1,0:T(8,128)(2,1)S(1)}, u32[]{:S(2)}, u32[]{:S(2)}) collective-permute-start(bf16[2,128,128]{2,1,0:T(8,128)(2,1)S(1)} %bitcast.90), channel_id=1, source_target_pairs={{0,4},{1,5},{2,6},{3,7},{4,0},{5,1},{6,2},{7,3},{8,12},{9,13},{10,... | collective-permute-start | bytes 196616 | tf_op jit(solution)/shard_map/ppermute | solution.py:213
  50.7 0.2 collective-permute-start.4
  50.9 0.0 collective-permute-done.refs_1_
  50.9 2.6 %collective-permute-start.5 = (bf16[2,128,128]{2,1,0:T(8,128)(2,1)S(1)}, bf16[2,128,128]{2,1,0:T(8,128)(2,1)S(1)}, u32[]{:S(2)}, u32[]{:S(2)}) collective-permute-start(bf16[2,128,128]{2,1,0:T(8,128)(2,1)S(1)} %bitcast.95), channel_id=1, source_target_pairs={{0,6},{1,7},{2,4},{3,5},{4,2},{5,3},{6,0},{7,1},{8,14},{9,15},{10,... | collective-permute-start | bytes 196616 | tf_op jit(solution)/shard_map/ppermute | solution.py:213
  53.5 1.2 %collective-permute-done.1.refs_2_ = bf16[2,128,128]{2,1,0:T(8,128)(2,1)S(1)} collective-permute-done((bf16[2,128,128]{2,1,0:T(8,128)(2,1)S(1)}, bf16[2,128,128]{2,1,0:T(8,128)(2,1)S(1)}, u32[]{:S(2)}, u32[]{:S(2)}) %collective-permute-start.1) | collective-permute-done | bytes 65568 | tf_op jit(solution)/shard_map/ppermute | solution.py:213
  54.7 0.4 collective-permute-start.6
  55.1 0.1 pad_maximum_fusion.5.left_x_ref
  55.2 0.0 collective-permute-done.2.refs_3_
  55.2 0.0 collective-permute-done.3.refs_4_
  55.3 0.0 collective-permute-done.4.refs_5_
  55.3 2.7 %collective-permute-done.5.refs_6_ = bf16[2,128,128]{2,1,0:T(8,128)(2,1)S(1)} collective-permute-done((bf16[2,128,128]{2,1,0:T(8,128)(2,1)S(1)}, bf16[2,128,128]{2,1,0:T(8,128)(2,1)S(1)}, u32[]{:S(2)}, u32[]{:S(2)}) %collective-permute-start.5) | collective-permute-done | bytes 65568 | tf_op jit(solution)/shard_map/ppermute | solution.py:213
  58.0 1.4 %collective-permute-done.6.refs_7_ = bf16[2,128,128]{2,1,0:T(8,128)(2,1)S(1)} collective-permute-done((bf16[2,128,128]{2,1,0:T(8,128)(2,1)S(1)}, bf16[2,128,128]{2,1,0:T(8,128)(2,1)S(1)}, u32[]{:S(2)}, u32[]{:S(2)}) %collective-permute-start.6) | collective-permute-done | bytes 65568 | tf_op jit(solution)/shard_map/ppermute | solution.py:213
  59.4 1.7 %weight_part.1 = f32[2,32,128]{2,1,0:T(8,128)S(1)} custom-call(s32[2]{0:T(128)S(1)} %pad_add_fusion.place_ref, bf16[16,2,128,128]{3,2,1,0:T(8,128)(2,1)S(1)} %all-to-all-done.g_ref, f32[16,64,256]{2,1,0:T(8,128)S(1)} %get-tuple-element.5.states_ref, bf16[192,128]{1,0:T(8,128)(2,1)S(1)} %pad_maximum_fusion.4.left_g_ref, ...), custom_call_target="tpu_custom_call" | custom-call | flops 402653184 | bytes 2097152 | tf_op jit(solution)/shard_map/weight_part/pallas_call | solution.py:252
  61.1 2.7 %collective-permute-start.7 = (f32[32,128]{1,0:T(8,128)S(1)}, f32[32,128]{1,0:T(8,128)S(1)}, u32[]{:S(2)}, u32[]{:S(2)}) collective-permute-start(f32[32,128]{1,0:T(8,128)S(1)} %slice_bitcast_fusion), channel_id=1, source_target_pairs={{0,8},{1,9},{2,10},{3,11},{4,12},{5,13},{6,14},{7,15},{8,0},{9,1},... | collective-permute-start | bytes 49160 | tf_op jit(solution)/shard_map/ppermute | solution.py:265
  63.8 2.0 %collective-permute-done.7 = f32[32,128]{1,0:T(8,128)S(1)} collective-permute-done((f32[32,128]{1,0:T(8,128)S(1)}, f32[32,128]{1,0:T(8,128)S(1)}, u32[]{:S(2)}, u32[]{:S(2)}) %collective-permute-start.7) | collective-permute-done | bytes 16416 | tf_op jit(solution)/shard_map/ppermute | solution.py:265
  65.8 0.6 fusion.7
  66.4 0.0 all-to-all-done.1
  66.4 0.3 copy.32
  66.7 1.0 %copy.42 = bf16[128,2048]{1,0:T(8,128)(2,1)} copy(bf16[128,2048]{0,1:T(8,128)(2,1)S(1)} %bitcast.82) | data formatting | bytes 1048576
  (18 shorter events, 0.3 us)
Async XLA Ops:
  0.6 11.4 %copy-start = (f32[2048]{0:T(1024)S(1)}, f32[2048]{0:T(1024)}, u32[]{:S(2)}) copy-start(f32[2048]{0:T(1024)} %param.14) | copy-start | bytes 24580
  3.4 7.6 %copy-start.5 = (f32[32]{0:T(128)S(1)}, f32[32]{0:T(128)}, u32[]{:S(2)}) copy-start(f32[32]{0:T(128)} %param.13) | copy-start | bytes 388
  3.4 7.6 %copy-start.6 = (f32[32]{0:T(128)S(1)}, f32[32]{0:T(128)}, u32[]{:S(2)}) copy-start(f32[32]{0:T(128)} %param.12) | copy-start | bytes 388
  3.4 30.5 %all-to-all-start = ((bf16[16,2,128,128]{3,2,1,0:T(8,128)(2,1)}), bf16[16,2,128,128]{3,2,1,0:T(8,128)(2,1)S(1)}, u32[]{:S(2)}, u32[]{:S(2)}) async-start(bf16[16,2,128,128]{3,2,1,0:T(8,128)(2,1)} %pad_maximum_fusion), calls=%async_computation | async-start | bytes 2097152 | tf_op jit(solution)/shard_map/all_to_all | solution.py:206
  10.9 1.0 %copy-start.3 = (f32[32,2048]{1,0:T(8,128)S(1)}, f32[32,2048]{1,0:T(8,128)}, u32[]{:S(2)}) copy-start(f32[32,2048]{1,0:T(8,128)} %param.11) | copy-start | bytes 786436
  11.9 0.8 %copy-start.2 = (f32[128,64]{1,0:T(8,128)S(1)}, f32[128,64]{1,0:T(8,128)}, u32[]{:S(2)}) copy-start(f32[128,64]{1,0:T(8,128)} %constant.72.clone) | copy-start | bytes 98308
  12.8 0.8 %copy-start.4 = (f32[64,128]{1,0:T(8,128)S(1)}, f32[64,128]{1,0:T(8,128)}, u32[]{:S(2)}) copy-start(f32[64,128]{1,0:T(8,128)} %constant.73.clone) | copy-start | bytes 98308
  33.8 0.7 copy-start.1
  38.1 28.3 %all-to-all-start.1 = ((bf16[8,2,128,128]{3,2,1,0:T(8,128)(2,1)}), bf16[8,2,128,128]{3,2,1,0:T(8,128)(2,1)S(1)}, u32[]{:S(2)}, u32[]{:S(2)}) async-start(bf16[8,2,128,128]{3,2,1,0:T(8,128)(2,1)} %get-tuple-element.4), calls=%async_computation.1 | async-start | bytes 1048576 | tf_op jit(solution)/shard_map/all_to_all | solution.py:243
  46.4 4.5 %collective-permute-start = (bf16[2,128,128]{2,1,0:T(8,128)(2,1)S(1)}, bf16[2,128,128]{2,1,0:T(8,128)(2,1)S(1)}, u32[]{:S(2)}, u32[]{:S(2)}) collective-permute-start(bf16[2,128,128]{2,1,0:T(8,128)(2,1)S(1)} %bitcast.94), channel_id=1, source_target_pairs={{0,1},{1,0},{2,3},{3,2},{4,5},{5,4},{6,7},{7,6},{8,9},{9,8},{10,11... | collective-permute-start | bytes 196616 | tf_op jit(solution)/shard_map/ppermute | solution.py:213
  47.0 7.7 %collective-permute-start.1 = (bf16[2,128,128]{2,1,0:T(8,128)(2,1)S(1)}, bf16[2,128,128]{2,1,0:T(8,128)(2,1)S(1)}, u32[]{:S(2)}, u32[]{:S(2)}) collective-permute-start(bf16[2,128,128]{2,1,0:T(8,128)(2,1)S(1)} %bitcast.93), channel_id=1, source_target_pairs={{0,2},{1,3},{2,0},{3,1},{4,6},{5,7},{6,4},{7,5},{8,10},{9,11},{10,... | collective-permute-start | bytes 196616 | tf_op jit(solution)/shard_map/ppermute | solution.py:213
  48.8 6.4 %collective-permute-start.2 = (bf16[2,128,128]{2,1,0:T(8,128)(2,1)S(1)}, bf16[2,128,128]{2,1,0:T(8,128)(2,1)S(1)}, u32[]{:S(2)}, u32[]{:S(2)}) collective-permute-start(bf16[2,128,128]{2,1,0:T(8,128)(2,1)S(1)} %bitcast.89), channel_id=1, source_target_pairs={{0,3},{1,2},{2,1},{3,0},{4,7},{5,6},{6,5},{7,4},{8,11},{9,10},{10,... | collective-permute-start | bytes 196616 | tf_op jit(solution)/shard_map/ppermute | solution.py:213
  48.9 6.4 %collective-permute-start.3 = (bf16[2,128,128]{2,1,0:T(8,128)(2,1)S(1)}, bf16[2,128,128]{2,1,0:T(8,128)(2,1)S(1)}, u32[]{:S(2)}, u32[]{:S(2)}) collective-permute-start(bf16[2,128,128]{2,1,0:T(8,128)(2,1)S(1)} %bitcast.90), channel_id=1, source_target_pairs={{0,4},{1,5},{2,6},{3,7},{4,0},{5,1},{6,2},{7,3},{8,12},{9,13},{10,... | collective-permute-start | bytes 196616 | tf_op jit(solution)/shard_map/ppermute | solution.py:213
  50.7 4.6 %collective-permute-start.4 = (bf16[2,128,128]{2,1,0:T(8,128)(2,1)S(1)}, bf16[2,128,128]{2,1,0:T(8,128)(2,1)S(1)}, u32[]{:S(2)}, u32[]{:S(2)}) collective-permute-start(bf16[2,128,128]{2,1,0:T(8,128)(2,1)S(1)} %bitcast.92), channel_id=1, source_target_pairs={{0,5},{1,4},{2,7},{3,6},{4,1},{5,0},{6,3},{7,2},{8,13},{9,12},{10,... | collective-permute-start | bytes 196616 | tf_op jit(solution)/shard_map/ppermute | solution.py:213
  50.9 7.1 %collective-permute-start.5 = (bf16[2,128,128]{2,1,0:T(8,128)(2,1)S(1)}, bf16[2,128,128]{2,1,0:T(8,128)(2,1)S(1)}, u32[]{:S(2)}, u32[]{:S(2)}) collective-permute-start(bf16[2,128,128]{2,1,0:T(8,128)(2,1)S(1)} %bitcast.95), channel_id=1, source_target_pairs={{0,6},{1,7},{2,4},{3,5},{4,2},{5,3},{6,0},{7,1},{8,14},{9,15},{10,... | collective-permute-start | bytes 196616 | tf_op jit(solution)/shard_map/ppermute | solution.py:213
  54.7 4.6 %collective-permute-start.6 = (bf16[2,128,128]{2,1,0:T(8,128)(2,1)S(1)}, bf16[2,128,128]{2,1,0:T(8,128)(2,1)S(1)}, u32[]{:S(2)}, u32[]{:S(2)}) collective-permute-start(bf16[2,128,128]{2,1,0:T(8,128)(2,1)S(1)} %bitcast.91), channel_id=1, source_target_pairs={{0,7},{1,6},{2,5},{3,4},{4,3},{5,2},{6,1},{7,0},{8,15},{9,14},{10,... | collective-permute-start | bytes 196616 | tf_op jit(solution)/shard_map/ppermute | solution.py:213
  61.1 4.7 %collective-permute-start.7 = (f32[32,128]{1,0:T(8,128)S(1)}, f32[32,128]{1,0:T(8,128)S(1)}, u32[]{:S(2)}, u32[]{:S(2)}) collective-permute-start(f32[32,128]{1,0:T(8,128)S(1)} %slice_bitcast_fusion), channel_id=1, source_target_pairs={{0,8},{1,9},{2,10},{3,11},{4,12},{5,13},{6,14},{7,15},{8,0},{9,1},... | collective-permute-start | bytes 49160 | tf_op jit(solution)/shard_map/ppermute | solution.py:265

commit v4 on v3

--- a/solution.py
+++ b/solution.py
@@ -204,7 +204,11 @@
 
     blocks = grad_out.reshape(rows_dev, 2, n_own, own).transpose(2, 1, 0, 3)
     g = widened(lax.all_to_all(jnp.concatenate([blocks, blocks], 0), "seq", 0, 0, tiled=True))
-    x_blocks = inputs.reshape(rows_dev, 2, n_own, own)
+    left_g, left_x, back_high, back_low, spectrum, step = tables(
+        rows, filter_rates, filter_freqs
+    )
+    later_inputs, spectrum = lax.optimization_barrier((inputs, spectrum))
+    x_blocks = later_inputs.reshape(rows_dev, 2, n_own, own)
     x_parts = []
     for offset in range(n_own):
         part = lax.dynamic_index_in_dim(x_blocks, rank ^ offset, 2, keepdims=False)
@@ -212,12 +216,10 @@
         if offset:
             part = lax.ppermute(part, "seq", [(i, i ^ offset) for i in range(devices)])
         x_parts.append(widened(part))
+    g, *x_parts = lax.optimization_barrier((g, *x_parts))
     weight = own_blocks(filter_weight)
     gain = own_blocks(skip_gain[None, :])
     place = jnp.stack([half, rank]).astype(jnp.int32)
-    left_g, left_x, back_high, back_low, spectrum, step = tables(
-        rows, filter_rates, filter_freqs
-    )
     n_spans = 2 * devices
     smem = pl.BlockSpec(memory_space=pltpu.SMEM)
     vmem = pl.BlockSpec(memory_space=pltpu.VMEM)

time: 68.3 us -> 56.8 us (0.83)
  the two profiles are of different devices: /device:TPU:0 before, /device:TPU:8 now
where the time goes in v4:
time: 56.8 us; the launch traced here: 56.4 us
  starting transfers between devices  20.3 us (36%)
  waiting for transfers between devices  20.1 us (35%)
  local copies, waits for them, and re-layouts  7.23 us (13%)
  Pallas kernels  5.34 us (9%)
  other arithmetic  2.22 us (4%)
  between operations  1.02 us (2%)
    ppermute x7, waiting for transfers between devices, on_device(): part = lax.ppermute(part, 'seq', [(i, i ^ offset) for i in range(devices)])  14.8 us
    ppermute x7, starting transfers between devices, on_device(): part = lax.ppermute(part, 'seq', [(i, i ^ offset) for i in range(devices)])  6.64 us
    all_to_all x1, starting transfers between devices, on_device(): lax.all_to_all(jnp.concatenate([blocks, blocks], 0), 'seq', 0, 0, tiled=T...  6.43 us
    ppermute x1, waiting for transfers between devices, on_device(): lax.ppermute(wgrad[1], 'seq', [(i, i ^ n_own) for i in range(devices)])  5.25 us
    unnamed x29, local copies, waits for them, and re-layouts  4.62 us
    ppermute x1, starting transfers between devices, on_device(): lax.ppermute(wgrad[1], 'seq', [(i, i ^ n_own) for i in range(devices)])  3.73 us
    pallas_call x1, Pallas kernels, on_device(): pl.pallas_call(input_kernel, out_shape=(jax.ShapeDtypeStruct((n_own, 2, r...  3.6 us
    all_to_all x1, starting transfers between devices, on_device(): lax.all_to_all(y[..., :own], 'seq', 0, 0, tiled=True, axis_index_groups=[...  3.46 us
  transfers between devices with their start and end apart: 10, of which 5 were waited for; matrix products, arithmetic and copies ran while one was open for 6% of the time, Pallas kernels for 3%

profile of v4, /device:TPU:8, one launch (start us, length us, event | category | flops | bytes accessed | tf_op | source)
XLA Modules:
  0.0 56.4 jit_solution(3092841038512613084)
XLA Ops:
  0.6 0.0 copy-start
  0.6 1.3 %copy.25 = bf16[128,2048]{0,1:T(8,128)(2,1)S(1)} copy(bf16[128,2048]{1,0:T(8,128)(2,1)} %param.10) | data formatting | bytes 1048576 | tf_op args[1]
  2.0 0.3 copy.26
  2.3 1.1 %pad_maximum_fusion = bf16[16,2,128,128]{3,2,1,0:T(8,128)(2,1)} fusion(bf16[8,2,128,128]{3,2,1,0:T(8,128)(2,1)S(1)} %bitcast.80), kind=kLoop, calls=%fused_computation | loop fusion | flops 524288 | bytes 1572864 | tf_op jit(solution)/shard_map/concatenate | solution.py:206
  3.3 0.0 copy-start.2
  3.4 6.4 %all-to-all-start = ((bf16[16,2,128,128]{3,2,1,0:T(8,128)(2,1)}), bf16[16,2,128,128]{3,2,1,0:T(8,128)(2,1)S(1)}, u32[]{:S(2)}, u32[]{:S(2)}) async-start(bf16[16,2,128,128]{3,2,1,0:T(8,128)(2,1)} %pad_maximum_fusion), calls=%async_computation | async-start | bytes 2097152 | tf_op jit(solution)/shard_map/all_to_all | solution.py:206
  9.8 0.0 copy-start.3
  9.8 0.0 copy-start.6
  9.9 0.0 copy-start.7
  9.9 0.6 %copy-done.6 = f32[32]{0:T(128)S(1)} copy-done((f32[32]{0:T(128)S(1)}, f32[32]{0:T(128)}, u32[]{:S(2)}) %copy-start.6) | copy-done | bytes 152
  10.5 0.0 copy-done.7
  10.5 0.1 fusion.6
  10.7 0.0 copy-done.3
  10.7 0.2 fusion.10
  10.9 0.0 copy-done.2
  10.9 0.1 copy.52
  11.1 1.2 %constant_dynamic-slice_fusion.2 = (bf16[128,2,1,128]{3,2,1,0:T(2,128)(2,1)S(1)}, bf16[128,2,1,128]{3,2,1,0:T(2,128)(2,1)S(1)}, bf16[128,2,1,128]{3,2,1,0:T(2,12...) fusion(bf16[128,2,8,128]{3,2,1,0:T(8,128)(2,1)S(1)} %bitcast.79, ...), kind=kLoop, calls=%fused_computation.39 | loop fusion | bytes 1048608 | tf_op jit(solution)/shard_map/jit(dynamic_index_in_dim)/dynamic_slice | solution.py:214
  12.3 0.2 collective-permute-start
  12.6 1.5 %collective-permute-start.1 = (bf16[2,128,128]{2,1,0:T(8,128)(2,1)S(1)}, bf16[2,128,128]{2,1,0:T(8,128)(2,1)S(1)}, u32[]{:S(2)}, u32[]{:S(2)}) collective-permute-start(bf16[2,128,128]{2,1,0:T(8,128)(2,1)S(1)} %bitcast.92), channel_id=1, source_target_pairs={{0,2},{1,3},{2,0},{3,1},{4,6},{5,7},{6,4},{7,5},{8,10},{9,11},{10,... | collective-permute-start | bytes 196616 | tf_op jit(solution)/shard_map/ppermute | solution.py:217
  14.1 0.3 collective-permute-start.2
  14.4 0.4 collective-permute-start.3
  14.9 0.0 copy-start.4
  14.9 1.5 %collective-permute-start.4 = (bf16[2,128,128]{2,1,0:T(8,128)(2,1)S(1)}, bf16[2,128,128]{2,1,0:T(8,128)(2,1)S(1)}, u32[]{:S(2)}, u32[]{:S(2)}) collective-permute-start(bf16[2,128,128]{2,1,0:T(8,128)(2,1)S(1)} %bitcast.91), channel_id=1, source_target_pairs={{0,5},{1,4},{2,7},{3,6},{4,1},{5,0},{6,3},{7,2},{8,13},{9,12},{10,... | collective-permute-start | bytes 196616 | tf_op jit(solution)/shard_map/ppermute | solution.py:217
  16.4 0.2 slice_reduce_fusion
  16.6 0.1 copy.39.step_ref
  16.7 0.1 fusion.12
  16.8 0.1 rev.8
  16.8 0.1 rev.9
  16.9 0.1 copy.37
  17.0 0.1 copy.36
  17.1 0.1 copy.38.spectrum_ref
  17.2 0.0 copy-done.4
  17.4 0.0 copy-start.5
  17.4 0.1 pad_maximum_fusion.4.left_g_ref
  17.5 0.7 %copy-done.5 = f32[64,128]{1,0:T(8,128)S(1)} copy-done((f32[64,128]{1,0:T(8,128)S(1)}, f32[64,128]{1,0:T(8,128)}, u32[]{:S(2)}) %copy-start.5) | copy-done | bytes 32792
  18.2 0.1 fusion.4
  18.3 0.0 copy-done
  18.3 0.0 collective-permute-done.refs_1_
  18.3 1.5 %collective-permute-start.5 = (bf16[2,128,128]{2,1,0:T(8,128)(2,1)S(1)}, bf16[2,128,128]{2,1,0:T(8,128)(2,1)S(1)}, u32[]{:S(2)}, u32[]{:S(2)}) collective-permute-start(bf16[2,128,128]{2,1,0:T(8,128)(2,1)S(1)} %bitcast.95), channel_id=1, source_target_pairs={{0,6},{1,7},{2,4},{3,5},{4,2},{5,3},{6,0},{7,1},{8,14},{9,15},{10,... | collective-permute-start | bytes 196616 | tf_op jit(solution)/shard_map/ppermute | solution.py:217
  19.8 0.0 collective-permute-done.1.refs_2_
  19.8 1.1 %collective-permute-start.6 = (bf16[2,128,128]{2,1,0:T(8,128)(2,1)S(1)}, bf16[2,128,128]{2,1,0:T(8,128)(2,1)S(1)}, u32[]{:S(2)}, u32[]{:S(2)}) collective-permute-start(bf16[2,128,128]{2,1,0:T(8,128)(2,1)S(1)} %bitcast.94), channel_id=1, source_target_pairs={{0,7},{1,6},{2,5},{3,4},{4,3},{5,2},{6,1},{7,0},{8,15},{9,14},{10,... | collective-permute-start | bytes 196616 | tf_op jit(solution)/shard_map/ppermute | solution.py:217
  21.0 0.1 pad_add_fusion.place_ref
  21.1 0.0 collective-permute-done.2.refs_3_
  21.1 9.0 %collective-permute-done.3.refs_4_ = bf16[2,128,128]{2,1,0:T(8,128)(2,1)S(1)} collective-permute-done((bf16[2,128,128]{2,1,0:T(8,128)(2,1)S(1)}, bf16[2,128,128]{2,1,0:T(8,128)(2,1)S(1)}, u32[]{:S(2)}, u32[]{:S(2)}) %collective-permute-start.3) | collective-permute-done | bytes 65568 | tf_op jit(solution)/shard_map/ppermute | solution.py:217
  30.1 1.0 %collective-permute-done.4.refs_5_ = bf16[2,128,128]{2,1,0:T(8,128)(2,1)S(1)} collective-permute-done((bf16[2,128,128]{2,1,0:T(8,128)(2,1)S(1)}, bf16[2,128,128]{2,1,0:T(8,128)(2,1)S(1)}, u32[]{:S(2)}, u32[]{:S(2)}) %collective-permute-start.4) | collective-permute-done | bytes 65568 | tf_op jit(solution)/shard_map/ppermute | solution.py:217
  31.1 4.0 %collective-permute-done.5.refs_6_ = bf16[2,128,128]{2,1,0:T(8,128)(2,1)S(1)} collective-permute-done((bf16[2,128,128]{2,1,0:T(8,128)(2,1)S(1)}, bf16[2,128,128]{2,1,0:T(8,128)(2,1)S(1)}, u32[]{:S(2)}, u32[]{:S(2)}) %collective-permute-start.5) | collective-permute-done | bytes 65568 | tf_op jit(solution)/shard_map/ppermute | solution.py:217
  35.1 0.8 %collective-permute-done.6.refs_7_ = bf16[2,128,128]{2,1,0:T(8,128)(2,1)S(1)} collective-permute-done((bf16[2,128,128]{2,1,0:T(8,128)(2,1)S(1)}, bf16[2,128,128]{2,1,0:T(8,128)(2,1)S(1)}, u32[]{:S(2)}, u32[]{:S(2)}) %collective-permute-start.6) | collective-permute-done | bytes 65568 | tf_op jit(solution)/shard_map/ppermute | solution.py:217
  35.9 0.0 all-to-all-done.g_ref
  35.9 0.0 copy-start.1
  35.9 0.7 %copy-done.1 = s32[32]{0:T(128)S(1)} copy-done((s32[32]{0:T(128)S(1)}, s32[32]{0:T(128)}, u32[]{:S(2)}) %copy-start.1) | copy-done | bytes 152
  36.5 3.6 %input_part.1 = (bf16[8,2,128,128]{3,2,1,0:T(8,128)(2,1)}, f32[16,64,256]{2,1,0:T(8,128)S(1)}) custom-call(s32[32]{0:T(128)S(1)} %copy-done.1, s32[2]{0:T(128)S(1)} %pad_add_fusion.place_ref, bf16[16,2,128,128]{3,2,1,0:T(8,128)(2,1)S(1)} %all-to-all-done.g_ref, f32[32,256]{1,0:T(8,128)S(1)} %bitcast.78, f32[1,256]{1,0:T(1,128)S(1)} %fusion.8.gain_ref, ...), custom_call_target="tpu_custom_call" | custom-call | tf_op jit(solution)/shard_map/input_part/pallas_call | solution.py:227
  40.1 3.5 %all-to-all-start.1 = ((bf16[8,2,128,128]{3,2,1,0:T(8,128)(2,1)}), bf16[8,2,128,128]{3,2,1,0:T(8,128)(2,1)S(1)}, u32[]{:S(2)}, u32[]{:S(2)}) async-start(bf16[8,2,128,128]{3,2,1,0:T(8,128)(2,1)} %get-tuple-element.18), calls=%async_computation.1 | async-start | bytes 1048576 | tf_op jit(solution)/shard_map/all_to_all | solution.py:245
  43.6 0.1 pad_maximum_fusion.5.left_x_ref
  43.7 1.7 %weight_part.1 = f32[2,32,128]{2,1,0:T(8,128)S(1)} custom-call(s32[2]{0:T(128)S(1)} %pad_add_fusion.place_ref, bf16[16,2,128,128]{3,2,1,0:T(8,128)(2,1)S(1)} %all-to-all-done.g_ref, f32[16,64,256]{2,1,0:T(8,128)S(1)} %get-tuple-element.19.states_ref, bf16[192,128]{1,0:T(8,128)(2,1)S(1)} %pad_maximum_fusion.4.left_g_ref, ...), custom_call_target="tpu_custom_call" | custom-call | flops 402653184 | bytes 2097152 | tf_op jit(solution)/shard_map/weight_part/pallas_call | solution.py:254
  45.4 3.7 %collective-permute-start.7 = (f32[32,128]{1,0:T(8,128)S(1)}, f32[32,128]{1,0:T(8,128)S(1)}, u32[]{:S(2)}, u32[]{:S(2)}) collective-permute-start(f32[32,128]{1,0:T(8,128)S(1)} %slice_bitcast_fusion), channel_id=1, source_target_pairs={{0,8},{1,9},{2,10},{3,11},{4,12},{5,13},{6,14},{7,15},{8,0},{9,1},... | collective-permute-start | bytes 49160 | tf_op jit(solution)/shard_map/ppermute | solution.py:267
  49.2 5.3 %collective-permute-done.7 = f32[32,128]{1,0:T(8,128)S(1)} collective-permute-done((f32[32,128]{1,0:T(8,128)S(1)}, f32[32,128]{1,0:T(8,128)S(1)}, u32[]{:S(2)}, u32[]{:S(2)}) %collective-permute-start.7) | collective-permute-done | bytes 16416 | tf_op jit(solution)/shard_map/ppermute | solution.py:267
  54.4 0.6 %fusion.7 = f32[32,128]{1,0:T(8,128)} fusion(f32[32,128]{1,0:T(8,128)S(1)} %collective-permute-done.7, f32[2,32,128]{2,1,0:T(8,128)S(1)} %weight_part.1), kind=kLoop, calls=%fused_computation.32 | loop fusion | flops 4096 | bytes 49152 | tf_op jit(solution)/shard_map/add | solution.py:268
  55.0 0.0 all-to-all-done.1
  55.0 0.3 copy.40
  55.3 1.0 %copy.42 = bf16[128,2048]{1,0:T(8,128)(2,1)} copy(bf16[128,2048]{0,1:T(8,128)(2,1)S(1)} %bitcast.82) | data formatting | bytes 1048576
  (18 shorter events, 0.3 us)
Async XLA Ops:
  0.6 17.6 %copy-start = (f32[2048]{0:T(1024)S(1)}, f32[2048]{0:T(1024)}, u32[]{:S(2)}) copy-start(f32[2048]{0:T(1024)} %param.14) | copy-start | bytes 24580
  3.3 7.6 %copy-start.2 = (bf16[128,2048]{1,0:T(8,128)(2,1)S(1)}, bf16[128,2048]{1,0:T(8,128)(2,1)}, u32[]{:S(2)}) copy-start(bf16[128,2048]{1,0:T(8,128)(2,1)} %param.9) | copy-start | bytes 1572868
  3.4 32.5 %all-to-all-start = ((bf16[16,2,128,128]{3,2,1,0:T(8,128)(2,1)}), bf16[16,2,128,128]{3,2,1,0:T(8,128)(2,1)S(1)}, u32[]{:S(2)}, u32[]{:S(2)}) async-start(bf16[16,2,128,128]{3,2,1,0:T(8,128)(2,1)} %pad_maximum_fusion), calls=%async_computation | async-start | bytes 2097152 | tf_op jit(solution)/shard_map/all_to_all | solution.py:206
  9.8 0.9 %copy-start.3 = (f32[128,64]{1,0:T(8,128)S(1)}, f32[128,64]{1,0:T(8,128)}, u32[]{:S(2)}) copy-start(f32[128,64]{1,0:T(8,128)} %constant.72.clone) | copy-start | bytes 98308
  9.8 0.7 %copy-start.6 = (f32[32]{0:T(128)S(1)}, f32[32]{0:T(128)}, u32[]{:S(2)}) copy-start(f32[32]{0:T(128)} %param.13) | copy-start | bytes 388
  9.9 0.7 %copy-start.7 = (f32[32]{0:T(128)S(1)}, f32[32]{0:T(128)}, u32[]{:S(2)}) copy-start(f32[32]{0:T(128)} %param.12) | copy-start | bytes 388
  12.3 6.0 %collective-permute-start = (bf16[2,128,128]{2,1,0:T(8,128)(2,1)S(1)}, bf16[2,128,128]{2,1,0:T(8,128)(2,1)S(1)}, u32[]{:S(2)}, u32[]{:S(2)}) collective-permute-start(bf16[2,128,128]{2,1,0:T(8,128)(2,1)S(1)} %bitcast.93), channel_id=1, source_target_pairs={{0,1},{1,0},{2,3},{3,2},{4,5},{5,4},{6,7},{7,6},{8,9},{9,8},{10,11... | collective-permute-start | bytes 196616 | tf_op jit(solution)/shard_map/ppermute | solution.py:217
  12.6 7.3 %collective-permute-start.1 = (bf16[2,128,128]{2,1,0:T(8,128)(2,1)S(1)}, bf16[2,128,128]{2,1,0:T(8,128)(2,1)S(1)}, u32[]{:S(2)}, u32[]{:S(2)}) collective-permute-start(bf16[2,128,128]{2,1,0:T(8,128)(2,1)S(1)} %bitcast.92), channel_id=1, source_target_pairs={{0,2},{1,3},{2,0},{3,1},{4,6},{5,7},{6,4},{7,5},{8,10},{9,11},{10,... | collective-permute-start | bytes 196616 | tf_op jit(solution)/shard_map/ppermute | solution.py:217
  14.1 6.9 %collective-permute-start.2 = (bf16[2,128,128]{2,1,0:T(8,128)(2,1)S(1)}, bf16[2,128,128]{2,1,0:T(8,128)(2,1)S(1)}, u32[]{:S(2)}, u32[]{:S(2)}) collective-permute-start(bf16[2,128,128]{2,1,0:T(8,128)(2,1)S(1)} %bitcast.89), channel_id=1, source_target_pairs={{0,3},{1,2},{2,1},{3,0},{4,7},{5,6},{6,5},{7,4},{8,11},{9,10},{10,... | collective-permute-start | bytes 196616 | tf_op jit(solution)/shard_map/ppermute | solution.py:217
  14.4 15.6 %collective-permute-start.3 = (bf16[2,128,128]{2,1,0:T(8,128)(2,1)S(1)}, bf16[2,128,128]{2,1,0:T(8,128)(2,1)S(1)}, u32[]{:S(2)}, u32[]{:S(2)}) collective-permute-start(bf16[2,128,128]{2,1,0:T(8,128)(2,1)S(1)} %bitcast.90), channel_id=1, source_target_pairs={{0,4},{1,5},{2,6},{3,7},{4,0},{5,1},{6,2},{7,3},{8,12},{9,13},{10,... | collective-permute-start | bytes 196616 | tf_op jit(solution)/shard_map/ppermute | solution.py:217
  14.9 2.3 %copy-start.4 = (f32[32,2048]{1,0:T(8,128)S(1)}, f32[32,2048]{1,0:T(8,128)}, u32[]{:S(2)}) copy-start(f32[32,2048]{1,0:T(8,128)} %param.11) | copy-start | bytes 786436
  14.9 16.2 %collective-permute-start.4 = (bf16[2,128,128]{2,1,0:T(8,128)(2,1)S(1)}, bf16[2,128,128]{2,1,0:T(8,128)(2,1)S(1)}, u32[]{:S(2)}, u32[]{:S(2)}) collective-permute-start(bf16[2,128,128]{2,1,0:T(8,128)(2,1)S(1)} %bitcast.91), channel_id=1, source_target_pairs={{0,5},{1,4},{2,7},{3,6},{4,1},{5,0},{6,3},{7,2},{8,13},{9,12},{10,... | collective-permute-start | bytes 196616 | tf_op jit(solution)/shard_map/ppermute | solution.py:217
  17.4 0.8 %copy-start.5 = (f32[64,128]{1,0:T(8,128)S(1)}, f32[64,128]{1,0:T(8,128)}, u32[]{:S(2)}) copy-start(f32[64,128]{1,0:T(8,128)} %constant.73.clone) | copy-start | bytes 98308
  18.3 16.8 %collective-permute-start.5 = (bf16[2,128,128]{2,1,0:T(8,128)(2,1)S(1)}, bf16[2,128,128]{2,1,0:T(8,128)(2,1)S(1)}, u32[]{:S(2)}, u32[]{:S(2)}) collective-permute-start(bf16[2,128,128]{2,1,0:T(8,128)(2,1)S(1)} %bitcast.95), channel_id=1, source_target_pairs={{0,6},{1,7},{2,4},{3,5},{4,2},{5,3},{6,0},{7,1},{8,14},{9,15},{10,... | collective-permute-start | bytes 196616 | tf_op jit(solution)/shard_map/ppermute | solution.py:217
  19.8 16.0 %collective-permute-start.6 = (bf16[2,128,128]{2,1,0:T(8,128)(2,1)S(1)}, bf16[2,128,128]{2,1,0:T(8,128)(2,1)S(1)}, u32[]{:S(2)}, u32[]{:S(2)}) collective-permute-start(bf16[2,128,128]{2,1,0:T(8,128)(2,1)S(1)} %bitcast.94), channel_id=1, source_target_pairs={{0,7},{1,6},{2,5},{3,4},{4,3},{5,2},{6,1},{7,0},{8,15},{9,14},{10,... | collective-permute-start | bytes 196616 | tf_op jit(solution)/shard_map/ppermute | solution.py:217
  35.9 0.7 %copy-start.1 = (s32[32]{0:T(128)S(1)}, s32[32]{0:T(128)}, u32[]{:S(2)}) copy-start(s32[32]{0:T(128)} %spans_ref.1) | copy-start | bytes 388
  40.1 14.9 %all-to-all-start.1 = ((bf16[8,2,128,128]{3,2,1,0:T(8,128)(2,1)}), bf16[8,2,128,128]{3,2,1,0:T(8,128)(2,1)S(1)}, u32[]{:S(2)}, u32[]{:S(2)}) async-start(bf16[8,2,128,128]{3,2,1,0:T(8,128)(2,1)} %get-tuple-element.18), calls=%async_computation.1 | async-start | bytes 1048576 | tf_op jit(solution)/shard_map/all_to_all | solution.py:245
  45.4 9.0 %collective-permute-start.7 = (f32[32,128]{1,0:T(8,128)S(1)}, f32[32,128]{1,0:T(8,128)S(1)}, u32[]{:S(2)}, u32[]{:S(2)}) collective-permute-start(f32[32,128]{1,0:T(8,128)S(1)} %slice_bitcast_fusion), channel_id=1, source_target_pairs={{0,8},{1,9},{2,10},{3,11},{4,12},{5,13},{6,14},{7,15},{8,0},{9,1},... | collective-permute-start | bytes 49160 | tf_op jit(solution)/shard_map/ppermute | solution.py:267

commit v5 on v4

--- a/solution.py
+++ b/solution.py
@@ -64,7 +64,6 @@
 
 
 def input_kernel(
-    spans_ref,
     place_ref,
     g_ref,
     weight_ref,
@@ -90,7 +89,7 @@
     own_base = place_ref[0] * n_own
     far_base = n_own - own_base
     for slot in range(n_spans):
-        slot_of[spans_ref[slot]] = slot
+        slot_of[place_ref[2 + slot]] = slot
     weight = weight_ref[...]
     taps = jnp.dot(spectrum_ref[...], weight, precision=HIGHEST, preferred_element_type=F32)
     taps_real, taps_imag = taps[:rows], taps[rows:]
@@ -182,6 +181,41 @@
         wgrad_ref[half ^ block] = total[:, block * width : (block + 1) * width]
 
 
+def split_kernel(value_ref, parts_ref, sems):
+    copies, groups, _, own = parts_ref.shape
+    n_own = value_ref.shape[1] // (groups * own)
+    moves = []
+    for target in range(copies):
+        for group in range(groups):
+            at = (group * n_own + target % n_own) * own
+            moves.append(
+                pltpu.make_async_copy(
+                    value_ref.at[:, at : at + own], parts_ref.at[target, group], sems.at[target, group]
+                )
+            )
+    for move in moves:
+        move.start()
+    for move in moves:
+        move.wait()
+
+
+def join_kernel(parts_ref, value_ref, sems):
+    n_own, groups, _, own = parts_ref.shape
+    moves = []
+    for source in range(n_own):
+        for group in range(groups):
+            at = (group * n_own + source) * own
+            moves.append(
+                pltpu.make_async_copy(
+                    parts_ref.at[source, group], value_ref.at[:, at : at + own], sems.at[source, group]
+                )
+            )
+    for move in moves:
+        move.start()
+    for move in moves:
+        move.wait()
+
+
 def on_device(inputs, grad_out, filter_weight, filter_rates, filter_freqs, skip_gain, span_of_slot):
     rows_dev, channels = inputs.shape
     rows = rows_dev // 2
@@ -202,24 +236,38 @@
         taken = lax.dynamic_index_in_dim(blocks, rank, 2, keepdims=False)
         return widened(taken).reshape(value.shape[0], lanes)
 
-    blocks = grad_out.reshape(rows_dev, 2, n_own, own).transpose(2, 1, 0, 3)
-    g = widened(lax.all_to_all(jnp.concatenate([blocks, blocks], 0), "seq", 0, 0, tiled=True))
+    anywhere = pl.BlockSpec(memory_space=pl.ANY)
+    small = pltpu.CompilerParams(vmem_limit_bytes=2**20)
+    if own % LANES == 0:
+        blocks = pl.pallas_call(
+            split_kernel,
+            out_shape=jax.ShapeDtypeStruct((devices, 2, rows_dev, own), BF16),
+            in_specs=[anywhere],
+            out_specs=anywhere,
+            scratch_shapes=[pltpu.SemaphoreType.DMA((devices, 2))],
+            compiler_params=small,
+            name="split",
+        )(grad_out)
+    else:
+        blocks = grad_out.reshape(rows_dev, 2, n_own, own).transpose(2, 1, 0, 3)
+        blocks = jnp.concatenate([blocks, blocks], 0)
+    g = widened(lax.all_to_all(blocks, "seq", 0, 0, tiled=True))
     left_g, left_x, back_high, back_low, spectrum, step = tables(
         rows, filter_rates, filter_freqs
     )
     later_inputs, spectrum = lax.optimization_barrier((inputs, spectrum))
     x_blocks = later_inputs.reshape(rows_dev, 2, n_own, own)
-    x_parts = []
-    for offset in range(n_own):
+    x_parts = [None] * n_own
+    for offset in range(n_own - 1, -1, -1):
         part = lax.dynamic_index_in_dim(x_blocks, rank ^ offset, 2, keepdims=False)
         part = part.transpose(1, 0, 2)
         if offset:
             part = lax.ppermute(part, "seq", [(i, i ^ offset) for i in range(devices)])
-        x_parts.append(widened(part))
-    g, *x_parts = lax.optimization_barrier((g, *x_parts))
+        x_parts[offset] = widened(part)
     weight = own_blocks(filter_weight)
     gain = own_blocks(skip_gain[None, :])
-    place = jnp.stack([half, rank]).astype(jnp.int32)
+    g, *x_parts = lax.optimization_barrier((g, *x_parts))
+    place = jnp.concatenate([jnp.stack([half, rank]).astype(jnp.int32), span_of_slot])
     n_spans = 2 * devices
     smem = pl.BlockSpec(memory_space=pltpu.SMEM)
     vmem = pl.BlockSpec(memory_space=pltpu.VMEM)
@@ -230,7 +278,7 @@
             jax.ShapeDtypeStruct((n_own, 2, rows_dev, width), BF16),
             jax.ShapeDtypeStruct((devices, 2 * n_basis, lanes), F32),
         ),
-        in_specs=[smem, smem] + [vmem] * 8,
+        in_specs=[smem] + [vmem] * 8,
         out_specs=(vmem, vmem),
         scratch_shapes=[
             pltpu.SMEM((n_spans,), jnp.int32),
@@ -241,7 +289,7 @@
         ],
         compiler_params=params,
         name="input_part",
-    )(span_of_slot, place, g, weight, gain, left_g, back_high, back_low, spectrum, step)
+    )(place, g, weight, gain, left_g, back_high, back_low, spectrum, step)
     y = lax.all_to_all(
         y[..., :own],
         "seq",
@@ -250,7 +298,18 @@
         tiled=True,
         axis_index_groups=[list(range(n_own)), list(range(n_own, devices))],
     )
-    input_grad = y.transpose(2, 1, 0, 3).reshape(rows_dev, channels)
+    if own % LANES == 0:
+        input_grad = pl.pallas_call(
+            join_kernel,
+            out_shape=jax.ShapeDtypeStruct((rows_dev, channels), BF16),
+            in_specs=[anywhere],
+            out_specs=anywhere,
+            scratch_shapes=[pltpu.SemaphoreType.DMA((n_own, 2))],
+            compiler_params=small,
+            name="join",
+        )(y)
+    else:
+        input_grad = y.transpose(2, 1, 0, 3).reshape(rows_dev, channels)
     wgrad = pl.pallas_call(
         weight_kernel,
         out_shape=jax.ShapeDtypeStruct((2, n_basis, width), F32),

time: 56.8 us -> 55.4 us (0.975)
  Pallas kernels: 5.34 us -> 7.54 us
  local copies, waits for them, and re-layouts: 7.23 us -> 5.36 us
  other arithmetic: 2.22 us -> 1.14 us
  waiting for transfers between devices: 20.1 us -> 19.4 us
    pallas_call x0 -> x2, Pallas kernels: none -> 2.2 us  [the longest x1 1.28 us: on_device(): pl.pallas_call(split_kernel, out_shape=jax.ShapeDtypeStruct((devices, 2,...]
    unnamed x29, local copies, waits for them, and re-layouts: 4.62 us -> 3.33 us
    concatenate x1, other arithmetic: 1.08 us -> 0.08 us  [on_device(): jnp.concatenate([jnp.stack([half, rank]).astype(jnp.int32), span_of_slot])]
    ppermute x7, waiting for transfers between devices: 14.8 us -> 14.2 us  [on_device(): part = lax.ppermute(part, 'seq', [(i, i ^ offset) for i in range(devices)])]
  transfers between devices with their start and end apart: 10 -> 10, of which waited for: 5 -> 5; matrix products, arithmetic and copies ran while one was open for 6% -> 7% of each run, Pallas kernels for 3% -> 3%
where the time goes in v5:
time: 55.4 us; the launch traced here: 55 us
  starting transfers between devices  20.3 us (37%)
  waiting for transfers between devices  19.4 us (35%)
  Pallas kernels  7.54 us (14%)
  local copies, waits for them, and re-layouts  5.36 us (10%)
  other arithmetic  1.14 us (2%)
  between operations  1.03 us (2%)
    ppermute x7, waiting for transfers between devices, on_device(): part = lax.ppermute(part, 'seq', [(i, i ^ offset) for i in range(devices)])  14.2 us
    ppermute x7, starting transfers between devices, on_device(): part = lax.ppermute(part, 'seq', [(i, i ^ offset) for i in range(devices)])  6.64 us
    all_to_all x1, starting transfers between devices, on_device(): g = widened(lax.all_to_all(blocks, 'seq', 0, 0, tiled=True))  6.44 us
    ppermute x1, waiting for transfers between devices, on_device(): lax.ppermute(wgrad[1], 'seq', [(i, i ^ n_own) for i in range(devices)])  5.25 us
    ppermute x1, starting transfers between devices, on_device(): lax.ppermute(wgrad[1], 'seq', [(i, i ^ n_own) for i in range(devices)])  3.73 us
    pallas_call x1, Pallas kernels, on_device(): pl.pallas_call(input_kernel, out_shape=(jax.ShapeDtypeStruct((n_own, 2, r...  3.6 us
    all_to_all x1, starting transfers between devices, on_device(): lax.all_to_all(y[..., :own], 'seq', 0, 0, tiled=True, axis_index_groups=[...  3.46 us
    unnamed x29, local copies, waits for them, and re-layouts  3.33 us
  transfers between devices with their start and end apart: 10, of which 5 were waited for; matrix products, arithmetic and copies ran while one was open for 7% of the time, Pallas kernels for 3%

profile of v5, /device:TPU:8, one launch (start us, length us, event | category | flops | bytes accessed | tf_op | source)
XLA Modules:
  0.0 55.0 jit_solution(16445399841360018465)
XLA Ops:
  0.6 0.0 copy-start
  0.6 0.0 copy-start.1
  0.7 1.0 %copy-done.1 = bf16[128,2048]{1,0:T(8,128)(2,1)S(1)} copy-done((bf16[128,2048]{1,0:T(8,128)(2,1)S(1)}, bf16[128,2048]{1,0:T(8,128)(2,1)}, u32[]{:S(2)}) %copy-start.1) | copy-done | bytes 524312
  1.7 1.3 %split.1 = bf16[16,2,128,128]{3,2,1,0:T(8,128)(2,1)} custom-call(bf16[128,2048]{1,0:T(8,128)(2,1)S(1)} %copy-done.1), custom_call_target="tpu_custom_call" | custom-call | tf_op jit(solution)/shard_map/split/pallas_call | solution.py:242
  3.0 0.0 copy-start.2
  3.0 6.4 %all-to-all-start = ((bf16[16,2,128,128]{3,2,1,0:T(8,128)(2,1)}), bf16[16,2,128,128]{3,2,1,0:T(8,128)(2,1)S(1)}, u32[]{:S(2)}, u32[]{:S(2)}) async-start(bf16[16,2,128,128]{3,2,1,0:T(8,128)(2,1)} %split.1), calls=%async_computation | async-start | bytes 2097152 | tf_op jit(solution)/shard_map/all_to_all | solution.py:254
  9.4 0.0 copy-start.3
  9.5 0.0 copy-start.6
  9.5 0.0 copy-start.7
  9.5 0.6 %copy-done.6 = f32[32]{0:T(128)S(1)} copy-done((f32[32]{0:T(128)S(1)}, f32[32]{0:T(128)}, u32[]{:S(2)}) %copy-start.6) | copy-done | bytes 152
  10.2 0.0 copy-done.7
  10.2 0.1 fusion.6
  10.3 0.0 copy-done.3
  10.3 0.2 fusion.10
  10.5 0.0 copy-done.2
  10.6 0.1 copy.48
  10.7 1.2 %constant_dynamic-slice_fusion.2 = (bf16[128,2,1,128]{3,2,1,0:T(2,128)(2,1)S(1)}, bf16[128,2,1,128]{3,2,1,0:T(2,128)(2,1)S(1)}, bf16[128,2,1,128]{3,2,1,0:T(2,12...) fusion(bf16[128,2,8,128]{3,2,1,0:T(8,128)(2,1)S(1)} %bitcast.75, ...), kind=kLoop, calls=%fused_computation.38 | loop fusion | bytes 1048608 | tf_op jit(solution)/shard_map/jit(dynamic_index_in_dim)/dynamic_slice | solution.py:262
  12.0 0.2 collective-permute-start
  12.2 1.5 %collective-permute-start.1 = (bf16[2,128,128]{2,1,0:T(8,128)(2,1)S(1)}, bf16[2,128,128]{2,1,0:T(8,128)(2,1)S(1)}, u32[]{:S(2)}, u32[]{:S(2)}) collective-permute-start(bf16[2,128,128]{2,1,0:T(8,128)(2,1)S(1)} %bitcast.84), channel_id=1, source_target_pairs={{0,2},{1,3},{2,0},{3,1},{4,6},{5,7},{6,4},{7,5},{8,10},{9,11},{10,... | collective-permute-start | bytes 196616 | tf_op jit(solution)/shard_map/ppermute | solution.py:265
  13.8 0.3 collective-permute-start.2
  14.1 0.4 collective-permute-start.3
  14.5 0.0 copy-start.4
  14.5 1.5 %collective-permute-start.4 = (bf16[2,128,128]{2,1,0:T(8,128)(2,1)S(1)}, bf16[2,128,128]{2,1,0:T(8,128)(2,1)S(1)}, u32[]{:S(2)}, u32[]{:S(2)}) collective-permute-start(bf16[2,128,128]{2,1,0:T(8,128)(2,1)S(1)} %bitcast.83), channel_id=1, source_target_pairs={{0,5},{1,4},{2,7},{3,6},{4,1},{5,0},{6,3},{7,2},{8,13},{9,12},{10,... | collective-permute-start | bytes 196616 | tf_op jit(solution)/shard_map/ppermute | solution.py:265
  16.0 0.2 slice_reduce_fusion
  16.2 0.1 copy.37.step_ref
  16.3 0.1 fusion.12
  16.4 0.1 rev.8
  16.5 0.1 rev.9
  16.6 0.1 copy.35
  16.7 0.1 copy.34
  16.7 0.1 copy.36.spectrum_ref
  16.9 0.0 copy-done.4
  17.1 0.0 copy-start.5
  17.1 0.1 pad_maximum_fusion.3.left_g_ref
  17.2 0.7 %copy-done.5 = f32[64,128]{1,0:T(8,128)S(1)} copy-done((f32[64,128]{1,0:T(8,128)S(1)}, f32[64,128]{1,0:T(8,128)}, u32[]{:S(2)}) %copy-start.5) | copy-done | bytes 32792
  17.8 0.1 fusion.4
  17.9 0.0 copy-done
  18.0 0.0 collective-permute-done.refs_1_
  18.0 1.5 %collective-permute-start.5 = (bf16[2,128,128]{2,1,0:T(8,128)(2,1)S(1)}, bf16[2,128,128]{2,1,0:T(8,128)(2,1)S(1)}, u32[]{:S(2)}, u32[]{:S(2)}) collective-permute-start(bf16[2,128,128]{2,1,0:T(8,128)(2,1)S(1)} %bitcast.87), channel_id=1, source_target_pairs={{0,6},{1,7},{2,4},{3,5},{4,2},{5,3},{6,0},{7,1},{8,14},{9,15},{10,... | collective-permute-start | bytes 196616 | tf_op jit(solution)/shard_map/ppermute | solution.py:265
  19.5 0.0 collective-permute-done.1.refs_2_
  19.5 1.1 %collective-permute-start.6 = (bf16[2,128,128]{2,1,0:T(8,128)(2,1)S(1)}, bf16[2,128,128]{2,1,0:T(8,128)(2,1)S(1)}, u32[]{:S(2)}, u32[]{:S(2)}) collective-permute-start(bf16[2,128,128]{2,1,0:T(8,128)(2,1)S(1)} %bitcast.86), channel_id=1, source_target_pairs={{0,7},{1,6},{2,5},{3,4},{4,3},{5,2},{6,1},{7,0},{8,15},{9,14},{10,... | collective-permute-start | bytes 196616 | tf_op jit(solution)/shard_map/ppermute | solution.py:265
  20.6 0.0 copy-start.8
  20.6 0.7 %copy-done.8 = s32[32]{0:T(128)S(1)} copy-done((s32[32]{0:T(128)S(1)}, s32[32]{0:T(128)}, u32[]{:S(2)}) %copy-start.8) | copy-done | bytes 152
  21.3 0.1 pad_add_fusion.place_ref
  21.4 0.0 collective-permute-done.2.refs_3_
  21.4 8.3 %collective-permute-done.3.refs_4_ = bf16[2,128,128]{2,1,0:T(8,128)(2,1)S(1)} collective-permute-done((bf16[2,128,128]{2,1,0:T(8,128)(2,1)S(1)}, bf16[2,128,128]{2,1,0:T(8,128)(2,1)S(1)}, u32[]{:S(2)}, u32[]{:S(2)}) %collective-permute-start.3) | collective-permute-done | bytes 65568 | tf_op jit(solution)/shard_map/ppermute | solution.py:265
  29.7 1.0 %collective-permute-done.4.refs_5_ = bf16[2,128,128]{2,1,0:T(8,128)(2,1)S(1)} collective-permute-done((bf16[2,128,128]{2,1,0:T(8,128)(2,1)S(1)}, bf16[2,128,128]{2,1,0:T(8,128)(2,1)S(1)}, u32[]{:S(2)}, u32[]{:S(2)}) %collective-permute-start.4) | collective-permute-done | bytes 65568 | tf_op jit(solution)/shard_map/ppermute | solution.py:265
  30.7 4.0 %collective-permute-done.5.refs_6_ = bf16[2,128,128]{2,1,0:T(8,128)(2,1)S(1)} collective-permute-done((bf16[2,128,128]{2,1,0:T(8,128)(2,1)S(1)}, bf16[2,128,128]{2,1,0:T(8,128)(2,1)S(1)}, u32[]{:S(2)}, u32[]{:S(2)}) %collective-permute-start.5) | collective-permute-done | bytes 65568 | tf_op jit(solution)/shard_map/ppermute | solution.py:265
  34.7 0.8 %collective-permute-done.6.refs_7_ = bf16[2,128,128]{2,1,0:T(8,128)(2,1)S(1)} collective-permute-done((bf16[2,128,128]{2,1,0:T(8,128)(2,1)S(1)}, bf16[2,128,128]{2,1,0:T(8,128)(2,1)S(1)}, u32[]{:S(2)}, u32[]{:S(2)}) %collective-permute-start.6) | collective-permute-done | bytes 65568 | tf_op jit(solution)/shard_map/ppermute | solution.py:265
  35.5 0.0 all-to-all-done.g_ref
  35.5 3.6 %input_part.1 = (bf16[8,2,128,128]{3,2,1,0:T(8,128)(2,1)}, f32[16,64,256]{2,1,0:T(8,128)S(1)}) custom-call(s32[34]{0:T(128)S(1)} %pad_add_fusion.place_ref, bf16[16,2,128,128]{3,2,1,0:T(8,128)(2,1)S(1)} %all-to-all-done.g_ref, f32[32,256]{1,0:T(8,128)S(1)} %bitcast.74, f32[1,256]{1,0:T(1,128)S(1)} %fusion.8.gain_ref, ...), custom_call_target="tpu_custom_call" | custom-call | tf_op jit(solution)/shard_map/input_part/pallas_call | solution.py:275
  39.1 3.5 %all-to-all-start.1 = ((bf16[8,2,128,128]{3,2,1,0:T(8,128)(2,1)}), bf16[8,2,128,128]{3,2,1,0:T(8,128)(2,1)S(1)}, u32[]{:S(2)}, u32[]{:S(2)}) async-start(bf16[8,2,128,128]{3,2,1,0:T(8,128)(2,1)} %get-tuple-element.18), calls=%async_computation.1 | async-start | bytes 1048576 | tf_op jit(solution)/shard_map/all_to_all | solution.py:293
  42.6 0.1 pad_maximum_fusion.4.left_x_ref
  42.7 1.7 %weight_part.1 = f32[2,32,128]{2,1,0:T(8,128)S(1)} custom-call(s32[34]{0:T(128)S(1)} %pad_add_fusion.place_ref, bf16[16,2,128,128]{3,2,1,0:T(8,128)(2,1)S(1)} %all-to-all-done.g_ref, f32[16,64,256]{2,1,0:T(8,128)S(1)} %get-tuple-element.19.states_ref, bf16[192,128]{1,0:T(8,128)(2,1)S(1)} %pad_maximum_fusion.3.left_g_ref, ...), custom_call_target="tpu_custom_call" | custom-call | flops 402653184 | bytes 2097152 | tf_op jit(solution)/shard_map/weight_part/pallas_call | solution.py:313
  44.5 3.7 %collective-permute-start.7 = (f32[32,128]{1,0:T(8,128)S(1)}, f32[32,128]{1,0:T(8,128)S(1)}, u32[]{:S(2)}, u32[]{:S(2)}) collective-permute-start(f32[32,128]{1,0:T(8,128)S(1)} %slice_bitcast_fusion), channel_id=1, source_target_pairs={{0,8},{1,9},{2,10},{3,11},{4,12},{5,13},{6,14},{7,15},{8,0},{9,1},... | collective-permute-start | bytes 49160 | tf_op jit(solution)/shard_map/ppermute | solution.py:326
  48.2 5.3 %collective-permute-done.7 = f32[32,128]{1,0:T(8,128)S(1)} collective-permute-done((f32[32,128]{1,0:T(8,128)S(1)}, f32[32,128]{1,0:T(8,128)S(1)}, u32[]{:S(2)}, u32[]{:S(2)}) %collective-permute-start.7) | collective-permute-done | bytes 16416 | tf_op jit(solution)/shard_map/ppermute | solution.py:326
  53.4 0.6 %fusion.7 = f32[32,128]{1,0:T(8,128)} fusion(f32[32,128]{1,0:T(8,128)S(1)} %collective-permute-done.7, f32[2,32,128]{2,1,0:T(8,128)S(1)} %weight_part.1), kind=kLoop, calls=%fused_computation.31 | loop fusion | flops 4096 | bytes 49152 | tf_op jit(solution)/shard_map/add | solution.py:327
  54.0 0.0 all-to-all-done.1.parts_ref
  54.0 0.9 %join.1 = bf16[128,2048]{1,0:T(8,128)(2,1)} custom-call(bf16[8,2,128,128]{3,2,1,0:T(8,128)(2,1)S(1)} %all-to-all-done.1.parts_ref), custom_call_target="tpu_custom_call" | custom-call | tf_op jit(solution)/shard_map/join/pallas_call | solution.py:302
  (18 shorter events, 0.3 us)
Async XLA Ops:
  0.6 17.3 %copy-start = (f32[2048]{0:T(1024)S(1)}, f32[2048]{0:T(1024)}, u32[]{:S(2)}) copy-start(f32[2048]{0:T(1024)} %param.14) | copy-start | bytes 24580
  0.6 1.0 %copy-start.1 = (bf16[128,2048]{1,0:T(8,128)(2,1)S(1)}, bf16[128,2048]{1,0:T(8,128)(2,1)}, u32[]{:S(2)}) copy-start(bf16[128,2048]{1,0:T(8,128)(2,1)} %value_ref.1) | copy-start | bytes 1572868
  3.0 7.6 %copy-start.2 = (bf16[128,2048]{1,0:T(8,128)(2,1)S(1)}, bf16[128,2048]{1,0:T(8,128)(2,1)}, u32[]{:S(2)}) copy-start(bf16[128,2048]{1,0:T(8,128)(2,1)} %param.9) | copy-start | bytes 1572868
  3.0 32.5 %all-to-all-start = ((bf16[16,2,128,128]{3,2,1,0:T(8,128)(2,1)}), bf16[16,2,128,128]{3,2,1,0:T(8,128)(2,1)S(1)}, u32[]{:S(2)}, u32[]{:S(2)}) async-start(bf16[16,2,128,128]{3,2,1,0:T(8,128)(2,1)} %split.1), calls=%async_computation | async-start | bytes 2097152 | tf_op jit(solution)/shard_map/all_to_all | solution.py:254
  9.4 0.9 %copy-start.3 = (f32[128,64]{1,0:T(8,128)S(1)}, f32[128,64]{1,0:T(8,128)}, u32[]{:S(2)}) copy-start(f32[128,64]{1,0:T(8,128)} %constant.72.clone) | copy-start | bytes 98308
  9.5 0.7 %copy-start.6 = (f32[32]{0:T(128)S(1)}, f32[32]{0:T(128)}, u32[]{:S(2)}) copy-start(f32[32]{0:T(128)} %param.13) | copy-start | bytes 388
  9.5 0.7 %copy-start.7 = (f32[32]{0:T(128)S(1)}, f32[32]{0:T(128)}, u32[]{:S(2)}) copy-start(f32[32]{0:T(128)} %param.12) | copy-start | bytes 388
  12.0 6.0 %collective-permute-start = (bf16[2,128,128]{2,1,0:T(8,128)(2,1)S(1)}, bf16[2,128,128]{2,1,0:T(8,128)(2,1)S(1)}, u32[]{:S(2)}, u32[]{:S(2)}) collective-permute-start(bf16[2,128,128]{2,1,0:T(8,128)(2,1)S(1)} %bitcast.85), channel_id=1, source_target_pairs={{0,1},{1,0},{2,3},{3,2},{4,5},{5,4},{6,7},{7,6},{8,9},{9,8},{10,11... | collective-permute-start | bytes 196616 | tf_op jit(solution)/shard_map/ppermute | solution.py:265
  12.2 7.3 %collective-permute-start.1 = (bf16[2,128,128]{2,1,0:T(8,128)(2,1)S(1)}, bf16[2,128,128]{2,1,0:T(8,128)(2,1)S(1)}, u32[]{:S(2)}, u32[]{:S(2)}) collective-permute-start(bf16[2,128,128]{2,1,0:T(8,128)(2,1)S(1)} %bitcast.84), channel_id=1, source_target_pairs={{0,2},{1,3},{2,0},{3,1},{4,6},{5,7},{6,4},{7,5},{8,10},{9,11},{10,... | collective-permute-start | bytes 196616 | tf_op jit(solution)/shard_map/ppermute | solution.py:265
  13.8 7.6 %collective-permute-start.2 = (bf16[2,128,128]{2,1,0:T(8,128)(2,1)S(1)}, bf16[2,128,128]{2,1,0:T(8,128)(2,1)S(1)}, u32[]{:S(2)}, u32[]{:S(2)}) collective-permute-start(bf16[2,128,128]{2,1,0:T(8,128)(2,1)S(1)} %bitcast.81), channel_id=1, source_target_pairs={{0,3},{1,2},{2,1},{3,0},{4,7},{5,6},{6,5},{7,4},{8,11},{9,10},{10,... | collective-permute-start | bytes 196616 | tf_op jit(solution)/shard_map/ppermute | solution.py:265
  14.1 15.6 %collective-permute-start.3 = (bf16[2,128,128]{2,1,0:T(8,128)(2,1)S(1)}, bf16[2,128,128]{2,1,0:T(8,128)(2,1)S(1)}, u32[]{:S(2)}, u32[]{:S(2)}) collective-permute-start(bf16[2,128,128]{2,1,0:T(8,128)(2,1)S(1)} %bitcast.82), channel_id=1, source_target_pairs={{0,4},{1,5},{2,6},{3,7},{4,0},{5,1},{6,2},{7,3},{8,12},{9,13},{10,... | collective-permute-start | bytes 196616 | tf_op jit(solution)/shard_map/ppermute | solution.py:265
  14.5 2.3 %copy-start.4 = (f32[32,2048]{1,0:T(8,128)S(1)}, f32[32,2048]{1,0:T(8,128)}, u32[]{:S(2)}) copy-start(f32[32,2048]{1,0:T(8,128)} %param.11) | copy-start | bytes 786436
  14.5 16.2 %collective-permute-start.4 = (bf16[2,128,128]{2,1,0:T(8,128)(2,1)S(1)}, bf16[2,128,128]{2,1,0:T(8,128)(2,1)S(1)}, u32[]{:S(2)}, u32[]{:S(2)}) collective-permute-start(bf16[2,128,128]{2,1,0:T(8,128)(2,1)S(1)} %bitcast.83), channel_id=1, source_target_pairs={{0,5},{1,4},{2,7},{3,6},{4,1},{5,0},{6,3},{7,2},{8,13},{9,12},{10,... | collective-permute-start | bytes 196616 | tf_op jit(solution)/shard_map/ppermute | solution.py:265
  17.1 0.8 %copy-start.5 = (f32[64,128]{1,0:T(8,128)S(1)}, f32[64,128]{1,0:T(8,128)}, u32[]{:S(2)}) copy-start(f32[64,128]{1,0:T(8,128)} %constant.73.clone) | copy-start | bytes 98308
  18.0 16.8 %collective-permute-start.5 = (bf16[2,128,128]{2,1,0:T(8,128)(2,1)S(1)}, bf16[2,128,128]{2,1,0:T(8,128)(2,1)S(1)}, u32[]{:S(2)}, u32[]{:S(2)}) collective-permute-start(bf16[2,128,128]{2,1,0:T(8,128)(2,1)S(1)} %bitcast.87), channel_id=1, source_target_pairs={{0,6},{1,7},{2,4},{3,5},{4,2},{5,3},{6,0},{7,1},{8,14},{9,15},{10,... | collective-permute-start | bytes 196616 | tf_op jit(solution)/shard_map/ppermute | solution.py:265
  19.5 16.0 %collective-permute-start.6 = (bf16[2,128,128]{2,1,0:T(8,128)(2,1)S(1)}, bf16[2,128,128]{2,1,0:T(8,128)(2,1)S(1)}, u32[]{:S(2)}, u32[]{:S(2)}) collective-permute-start(bf16[2,128,128]{2,1,0:T(8,128)(2,1)S(1)} %bitcast.86), channel_id=1, source_target_pairs={{0,7},{1,6},{2,5},{3,4},{4,3},{5,2},{6,1},{7,0},{8,15},{9,14},{10,... | collective-permute-start | bytes 196616 | tf_op jit(solution)/shard_map/ppermute | solution.py:265
  20.6 0.7 %copy-start.8 = (s32[32]{0:T(128)S(1)}, s32[32]{0:T(128)}, u32[]{:S(2)}) copy-start(s32[32]{0:T(128)} %param.15) | copy-start | bytes 388
  39.1 14.9 %all-to-all-start.1 = ((bf16[8,2,128,128]{3,2,1,0:T(8,128)(2,1)}), bf16[8,2,128,128]{3,2,1,0:T(8,128)(2,1)S(1)}, u32[]{:S(2)}, u32[]{:S(2)}) async-start(bf16[8,2,128,128]{3,2,1,0:T(8,128)(2,1)} %get-tuple-element.18), calls=%async_computation.1 | async-start | bytes 1048576 | tf_op jit(solution)/shard_map/all_to_all | solution.py:293
  44.5 9.0 %collective-permute-start.7 = (f32[32,128]{1,0:T(8,128)S(1)}, f32[32,128]{1,0:T(8,128)S(1)}, u32[]{:S(2)}, u32[]{:S(2)}) collective-permute-start(f32[32,128]{1,0:T(8,128)S(1)} %slice_bitcast_fusion), channel_id=1, source_target_pairs={{0,8},{1,9},{2,10},{3,11},{4,12},{5,13},{6,14},{7,15},{8,0},{9,1},... | collective-permute-start | bytes 49160 | tf_op jit(solution)/shard_map/ppermute | solution.py:326

commit v6 on v5

--- a/solution.py
+++ b/solution.py
@@ -30,7 +30,7 @@
     return np.cos(angles), -np.sin(angles)
 
 
-def tables(rows, rates, freqs):
+def tables(rows, rates, freqs, inputs):
     cos_part, sin_part = odd_frequencies(rows)
     forward = jnp.asarray(np.concatenate([cos_part, sin_part], 0), F32)
     inverse = jnp.asarray(np.concatenate([cos_part, sin_part], 0).T / rows, F32)
@@ -45,12 +45,13 @@
     back = jnp.concatenate(
         [inverse, power_real[:, :0:-1].T, -power_imag[:, :0:-1].T], 1
     )
-    back_high, back_low = table_halves(back)
+    back = jnp.concatenate(table_halves(back), 0)
     basis_spectrum = jnp.dot(
         forward, power_real[:, :rows].T, precision=HIGHEST, preferred_element_type=F32
     )
+    later_inputs, basis_spectrum = lax.optimization_barrier((inputs, basis_spectrum))
     step = jnp.stack([power_real[:, rows], power_imag[:, rows]], 0)[:, :, None]
-    return left_g, left_x, back_high, back_low, basis_spectrum, step
+    return (left_g, left_x, back, basis_spectrum, step), later_inputs
 
 
 def side_by_side(ref, source, part):
@@ -69,8 +70,7 @@
     weight_ref,
     gain_ref,
     left_g_ref,
-    back_high_ref,
-    back_low_ref,
+    back_ref,
     spectrum_ref,
     step_ref,
     y_ref,
@@ -124,7 +124,6 @@
             state_imag = sums[slot, n_basis:] + step_real * state_imag + step_imag * state_real
             state_real = next_real
     gain = gain_ref[...]
-    back_high, back_low = back_high_ref[...], back_low_ref[...]
     both_weight = twice(weight)
     for source in range(n_own):
         for part in range(2):
@@ -134,10 +133,10 @@
             far = halves(both_weight * state)
             both_high = jnp.concatenate([high[slot], far[0]], 0)
             both_low = jnp.concatenate([low[slot], far[1]], 0)
+            by_high = jnp.dot(back_ref[...], both_high, preferred_element_type=F32)
             value = (
-                jnp.dot(back_high, both_high, preferred_element_type=F32)
-                + jnp.dot(back_high, both_low, preferred_element_type=F32)
-                + jnp.dot(back_low, both_high, preferred_element_type=F32)
+                (by_high[:rows] + by_high[rows:])
+                + jnp.dot(back_ref[:rows], both_low, preferred_element_type=F32)
                 + gain * side_by_side(g_ref, own_base + source, part).astype(F32)
             ).astype(BF16)
             at = slice(part * rows, (part + 1) * rows)
@@ -245,24 +244,25 @@
             in_specs=[anywhere],
             out_specs=anywhere,
             scratch_shapes=[pltpu.SemaphoreType.DMA((devices, 2))],
-            compiler_params=small,
+            compiler_params=pltpu.CompilerParams(vmem_limit_bytes=60 * 2**20),
             name="split",
         )(grad_out)
     else:
         blocks = grad_out.reshape(rows_dev, 2, n_own, own).transpose(2, 1, 0, 3)
         blocks = jnp.concatenate([blocks, blocks], 0)
     g = widened(lax.all_to_all(blocks, "seq", 0, 0, tiled=True))
-    left_g, left_x, back_high, back_low, spectrum, step = tables(
-        rows, filter_rates, filter_freqs
-    )
-    later_inputs, spectrum = lax.optimization_barrier((inputs, spectrum))
-    x_blocks = later_inputs.reshape(rows_dev, 2, n_own, own)
+    made, later_inputs = tables(rows, filter_rates, filter_freqs, inputs)
+    left_g, left_x, back, spectrum, step = made
     x_parts = [None] * n_own
     for offset in range(n_own - 1, -1, -1):
+        taken = later_inputs if offset >= n_own // 2 else near_inputs
+        x_blocks = taken.reshape(rows_dev, 2, n_own, own)
         part = lax.dynamic_index_in_dim(x_blocks, rank ^ offset, 2, keepdims=False)
         part = part.transpose(1, 0, 2)
         if offset:
             part = lax.ppermute(part, "seq", [(i, i ^ offset) for i in range(devices)])
+        if offset == n_own - 1:
+            near_inputs, part = lax.optimization_barrier((later_inputs, part))
         x_parts[offset] = widened(part)
     weight = own_blocks(filter_weight)
     gain = own_blocks(skip_gain[None, :])
@@ -278,7 +278,7 @@
             jax.ShapeDtypeStruct((n_own, 2, rows_dev, width), BF16),
             jax.ShapeDtypeStruct((devices, 2 * n_basis, lanes), F32),
         ),
-        in_specs=[smem] + [vmem] * 8,
+        in_specs=[smem] + [vmem] * 7,
         out_specs=(vmem, vmem),
         scratch_shapes=[
             pltpu.SMEM((n_spans,), jnp.int32),
@@ -289,7 +289,7 @@
         ],
         compiler_params=params,
         name="input_part",
-    )(place, g, weight, gain, left_g, back_high, back_low, spectrum, step)
+    )(place, g, weight, gain, left_g, back, spectrum, step)
     y = lax.all_to_all(
         y[..., :own],
         "seq",

time: 55.4 us -> 88.6 us (1.60)
  Pallas kernels: 7.54 us -> 39.2 us
  waiting for transfers between devices: 19.4 us -> 21.6 us
  local copies, waits for them, and re-layouts: 5.36 us -> 4.42 us
    pallas_call x1, Pallas kernels: 1.28 us -> 33.2 us  [on_device(): pl.pallas_call(split_kernel, out_shape=jax.ShapeDtypeStruct((devices, 2,...]
    ppermute x7, waiting for transfers between devices: 14.2 us -> 16.4 us  [on_device(): part = lax.ppermute(part, 'seq', [(i, i ^ offset) for i in range(devices)])]
    unnamed x29 -> x28, local copies, waits for them, and re-layouts: 3.33 us -> 2.51 us
  transfers between devices with their start and end apart: 10 -> 10, of which waited for: 5 -> 5; matrix products, arithmetic and copies ran while one was open for 7% -> 4% of each run, Pallas kernels for 3% -> 2%
where the time goes in v6:
time: 88.6 us; the launch traced here: 88.2 us
  Pallas kernels  39.2 us (44%)
  waiting for transfers between devices  21.6 us (24%)
  starting transfers between devices  20.5 us (23%)
  local copies, waits for them, and re-layouts  4.42 us (5%)
  other arithmetic  1.15 us (1%)
  between operations  1.02 us (1%)
    pallas_call x1, Pallas kernels, on_device(): pl.pallas_call(split_kernel, out_shape=jax.ShapeDtypeStruct((devices, 2,...  33.2 us
    ppermute x7, waiting for transfers between devices, on_device(): part = lax.ppermute(part, 'seq', [(i, i ^ offset) for i in range(devices)])  16.4 us
    ppermute x7, starting transfers between devices, on_device(): part = lax.ppermute(part, 'seq', [(i, i ^ offset) for i in range(devices)])  6.92 us
    all_to_all x1, starting transfers between devices, on_device(): g = widened(lax.all_to_all(blocks, 'seq', 0, 0, tiled=True))  6.44 us
    ppermute x1, waiting for transfers between devices, on_device(): lax.ppermute(wgrad[1], 'seq', [(i, i ^ n_own) for i in range(devices)])  5.29 us
    all_to_all x1, starting transfers between devices, on_device(): lax.all_to_all(y[..., :own], 'seq', 0, 0, tiled=True, axis_index_groups=[...  4.09 us
    pallas_call x1, Pallas kernels, on_device(): pl.pallas_call(input_kernel, out_shape=(jax.ShapeDtypeStruct((n_own, 2, r...  3.43 us
    ppermute x1, starting transfers between devices, on_device(): lax.ppermute(wgrad[1], 'seq', [(i, i ^ n_own) for i in range(devices)])  3.07 us
  transfers between devices with their start and end apart: 10, of which 5 were waited for; matrix products, arithmetic and copies ran while one was open for 4% of the time, Pallas kernels for 2%

profile of v6, /device:TPU:8, one launch (start us, length us, event | category | flops | bytes accessed | tf_op | source)
XLA Modules:
  0.0 88.2 jit_solution(7156840410843051738)
XLA Ops:
  0.6 0.0 copy-start
  0.6 33.2 %split.1 = bf16[16,2,128,128]{3,2,1,0:T(8,128)(2,1)} custom-call(bf16[128,2048]{1,0:T(8,128)(2,1)} %value_ref.1), custom_call_target="tpu_custom_call" | custom-call | tf_op jit(solution)/shard_map/split/pallas_call | solution.py:241
  33.8 0.0 copy-start.5
  33.8 0.0 copy-start.6
  33.8 0.0 copy-start.1
  33.8 6.4 %all-to-all-start = ((bf16[16,2,128,128]{3,2,1,0:T(8,128)(2,1)}), bf16[16,2,128,128]{3,2,1,0:T(8,128)(2,1)S(1)}, u32[]{:S(2)}, u32[]{:S(2)}) async-start(bf16[16,2,128,128]{3,2,1,0:T(8,128)(2,1)} %split.1), calls=%async_computation | async-start | bytes 2097152 | tf_op jit(solution)/shard_map/all_to_all | solution.py:253
  40.3 0.0 copy-start.2
  40.3 0.0 copy-done.5
  40.3 0.0 copy-done.6
  40.3 0.1 fusion.6
  40.5 0.6 copy-done.2
  41.1 0.2 fusion.10
  41.3 0.0 copy-done.1
  41.4 0.1 copy.48
  41.5 0.5 constant_dynamic-slice_fusion.2
  42.1 1.3 %collective-permute-start = (bf16[2,128,128]{2,1,0:T(8,128)(2,1)S(1)}, bf16[2,128,128]{2,1,0:T(8,128)(2,1)S(1)}, u32[]{:S(2)}, u32[]{:S(2)}) collective-permute-start(bf16[2,128,128]{2,1,0:T(8,128)(2,1)S(1)} %bitcast.89), channel_id=1, source_target_pairs={{0,7},{1,6},{2,5},{3,4},{4,3},{5,2},{6,1},{7,0},{8,15},{9,14},{10,... | collective-permute-start | bytes 196616 | tf_op jit(solution)/shard_map/ppermute | solution.py:263
  43.4 1.5 %collective-permute-start.4 = (bf16[2,128,128]{2,1,0:T(8,128)(2,1)S(1)}, bf16[2,128,128]{2,1,0:T(8,128)(2,1)S(1)}, u32[]{:S(2)}, u32[]{:S(2)}) collective-permute-start(bf16[2,128,128]{2,1,0:T(8,128)(2,1)S(1)} %bitcast.88), channel_id=1, source_target_pairs={{0,4},{1,5},{2,6},{3,7},{4,0},{5,1},{6,2},{7,3},{8,12},{9,13},{10,... | collective-permute-start | bytes 196616 | tf_op jit(solution)/shard_map/ppermute | solution.py:263
  44.9 0.3 collective-permute-start.5
  45.2 1.5 %collective-permute-start.6 = (bf16[2,128,128]{2,1,0:T(8,128)(2,1)S(1)}, bf16[2,128,128]{2,1,0:T(8,128)(2,1)S(1)}, u32[]{:S(2)}, u32[]{:S(2)}) collective-permute-start(bf16[2,128,128]{2,1,0:T(8,128)(2,1)S(1)} %bitcast.87), channel_id=1, source_target_pairs={{0,6},{1,7},{2,4},{3,5},{4,2},{5,3},{6,0},{7,1},{8,14},{9,15},{10,... | collective-permute-start | bytes 196616 | tf_op jit(solution)/shard_map/ppermute | solution.py:263
  46.8 0.0 copy-start.3
  46.8 0.2 slice_reduce_fusion
  47.0 0.1 copy.37.step_ref
  47.1 0.1 fusion.12
  47.1 0.1 rev.8
  47.2 0.1 rev.9
  47.3 0.1 copy.35
  47.4 0.1 copy.34
  47.5 0.1 copy.36.spectrum_ref
  47.6 0.1 copy-done.3
  47.9 0.0 copy-start.4
  47.9 0.1 pad_maximum_fusion.4.left_g_ref
  48.0 0.7 copy-done.4
  48.7 0.1 reduce-precision_convert_fusion.2
  48.8 0.0 copy-done
  48.8 12.0 %collective-permute-done.refs_7_ = bf16[2,128,128]{2,1,0:T(8,128)(2,1)S(1)} collective-permute-done((bf16[2,128,128]{2,1,0:T(8,128)(2,1)S(1)}, bf16[2,128,128]{2,1,0:T(8,128)(2,1)S(1)}, u32[]{:S(2)}, u32[]{:S(2)}) %collective-permute-start) | collective-permute-done | bytes 65568 | tf_op jit(solution)/shard_map/ppermute | solution.py:263
  60.8 0.1 copy.49
  60.9 0.6 constant_dynamic-slice_fusion.5
  61.6 0.8 collective-permute-start.1
  62.4 0.9 %collective-permute-start.2 = (bf16[2,128,128]{2,1,0:T(8,128)(2,1)S(1)}, bf16[2,128,128]{2,1,0:T(8,128)(2,1)S(1)}, u32[]{:S(2)}, u32[]{:S(2)}) collective-permute-start(bf16[2,128,128]{2,1,0:T(8,128)(2,1)S(1)} %bitcast.91), channel_id=1, source_target_pairs={{0,2},{1,3},{2,0},{3,1},{4,6},{5,7},{6,4},{7,5},{8,10},{9,11},{10,... | collective-permute-start | bytes 196616 | tf_op jit(solution)/shard_map/ppermute | solution.py:263
  63.3 0.0 collective-permute-done.4.refs_4_
  63.3 0.5 collective-permute-start.3
  63.8 0.0 copy-start.7
  63.8 0.7 copy-done.7
  64.5 0.1 pad_add_fusion.place_ref
  64.6 0.0 collective-permute-done.5.refs_5_
  64.6 1.7 %collective-permute-done.6.refs_6_ = bf16[2,128,128]{2,1,0:T(8,128)(2,1)S(1)} collective-permute-done((bf16[2,128,128]{2,1,0:T(8,128)(2,1)S(1)}, bf16[2,128,128]{2,1,0:T(8,128)(2,1)S(1)}, u32[]{:S(2)}, u32[]{:S(2)}) %collective-permute-start.6) | collective-permute-done | bytes 65568 | tf_op jit(solution)/shard_map/ppermute | solution.py:263
  66.3 0.0 collective-permute-done.1.refs_1_
  66.3 1.4 %collective-permute-done.2.refs_2_ = bf16[2,128,128]{2,1,0:T(8,128)(2,1)S(1)} collective-permute-done((bf16[2,128,128]{2,1,0:T(8,128)(2,1)S(1)}, bf16[2,128,128]{2,1,0:T(8,128)(2,1)S(1)}, u32[]{:S(2)}, u32[]{:S(2)}) %collective-permute-start.2) | collective-permute-done | bytes 65568 | tf_op jit(solution)/shard_map/ppermute | solution.py:263
  67.7 1.2 %collective-permute-done.3.refs_3_ = bf16[2,128,128]{2,1,0:T(8,128)(2,1)S(1)} collective-permute-done((bf16[2,128,128]{2,1,0:T(8,128)(2,1)S(1)}, bf16[2,128,128]{2,1,0:T(8,128)(2,1)S(1)}, u32[]{:S(2)}, u32[]{:S(2)}) %collective-permute-start.3) | collective-permute-done | bytes 65568 | tf_op jit(solution)/shard_map/ppermute | solution.py:263
  68.9 0.0 all-to-all-done.g_ref
  68.9 3.4 %input_part.1 = (bf16[8,2,128,128]{3,2,1,0:T(8,128)(2,1)}, f32[16,64,256]{2,1,0:T(8,128)S(1)}) custom-call(s32[34]{0:T(128)S(1)} %pad_add_fusion.place_ref, bf16[16,2,128,128]{3,2,1,0:T(8,128)(2,1)S(1)} %all-to-all-done.g_ref, f32[32,256]{1,0:T(8,128)S(1)} %bitcast.77, f32[1,256]{1,0:T(1,128)S(1)} %fusion.8.gain_ref, ...), custom_call_target="tpu_custom_call" | custom-call | tf_op jit(solution)/shard_map/input_part/pallas_call | solution.py:275
  72.4 4.1 %all-to-all-start.1 = ((bf16[8,2,128,128]{3,2,1,0:T(8,128)(2,1)}), bf16[8,2,128,128]{3,2,1,0:T(8,128)(2,1)S(1)}, u32[]{:S(2)}, u32[]{:S(2)}) async-start(bf16[8,2,128,128]{3,2,1,0:T(8,128)(2,1)} %get-tuple-element.22), calls=%async_computation.1 | async-start | bytes 1048576 | tf_op jit(solution)/shard_map/all_to_all | solution.py:293
  76.4 0.1 pad_maximum_fusion.5.left_x_ref
  76.5 1.7 %weight_part.1 = f32[2,32,128]{2,1,0:T(8,128)S(1)} custom-call(s32[34]{0:T(128)S(1)} %pad_add_fusion.place_ref, bf16[16,2,128,128]{3,2,1,0:T(8,128)(2,1)S(1)} %all-to-all-done.g_ref, f32[16,64,256]{2,1,0:T(8,128)S(1)} %get-tuple-element.23.states_ref, bf16[192,128]{1,0:T(8,128)(2,1)S(1)} %pad_maximum_fusion.4.left_g_ref, ...), custom_call_target="tpu_custom_call" | custom-call | flops 402653184 | bytes 2097152 | tf_op jit(solution)/shard_map/weight_part/pallas_call | solution.py:313
  78.3 3.1 %collective-permute-start.7 = (f32[32,128]{1,0:T(8,128)S(1)}, f32[32,128]{1,0:T(8,128)S(1)}, u32[]{:S(2)}, u32[]{:S(2)}) collective-permute-start(f32[32,128]{1,0:T(8,128)S(1)} %slice_bitcast_fusion), channel_id=1, source_target_pairs={{0,8},{1,9},{2,10},{3,11},{4,12},{5,13},{6,14},{7,15},{8,0},{9,1},... | collective-permute-start | bytes 49160 | tf_op jit(solution)/shard_map/ppermute | solution.py:326
  81.3 5.3 %collective-permute-done.7 = f32[32,128]{1,0:T(8,128)S(1)} collective-permute-done((f32[32,128]{1,0:T(8,128)S(1)}, f32[32,128]{1,0:T(8,128)S(1)}, u32[]{:S(2)}, u32[]{:S(2)}) %collective-permute-start.7) | collective-permute-done | bytes 16416 | tf_op jit(solution)/shard_map/ppermute | solution.py:326
  86.6 0.6 fusion.7
  87.2 0.0 all-to-all-done.1.parts_ref
  87.2 0.9 %join.1 = bf16[128,2048]{1,0:T(8,128)(2,1)} custom-call(bf16[8,2,128,128]{3,2,1,0:T(8,128)(2,1)S(1)} %all-to-all-done.1.parts_ref), custom_call_target="tpu_custom_call" | custom-call | tf_op jit(solution)/shard_map/join/pallas_call | solution.py:302
  (19 shorter events, 0.3 us)
Async XLA Ops:
  0.6 48.1 %copy-start = (f32[2048]{0:T(1024)S(1)}, f32[2048]{0:T(1024)}, u32[]{:S(2)}) copy-start(f32[2048]{0:T(1024)} %param.14) | copy-start | bytes 24580
  33.8 6.5 %copy-start.5 = (f32[32]{0:T(128)S(1)}, f32[32]{0:T(128)}, u32[]{:S(2)}) copy-start(f32[32]{0:T(128)} %param.13) | copy-start | bytes 388
  33.8 6.5 %copy-start.6 = (f32[32]{0:T(128)S(1)}, f32[32]{0:T(128)}, u32[]{:S(2)}) copy-start(f32[32]{0:T(128)} %param.12) | copy-start | bytes 388
  33.8 7.5 %copy-start.1 = (bf16[128,2048]{1,0:T(8,128)(2,1)S(1)}, bf16[128,2048]{1,0:T(8,128)(2,1)}, u32[]{:S(2)}) copy-start(bf16[128,2048]{1,0:T(8,128)(2,1)} %param.9) | copy-start | bytes 1572868
  33.8 35.1 %all-to-all-start = ((bf16[16,2,128,128]{3,2,1,0:T(8,128)(2,1)}), bf16[16,2,128,128]{3,2,1,0:T(8,128)(2,1)S(1)}, u32[]{:S(2)}, u32[]{:S(2)}) async-start(bf16[16,2,128,128]{3,2,1,0:T(8,128)(2,1)} %split.1), calls=%async_computation | async-start | bytes 2097152 | tf_op jit(solution)/shard_map/all_to_all | solution.py:253
  40.3 0.8 copy-start.2
  42.1 18.7 %collective-permute-start = (bf16[2,128,128]{2,1,0:T(8,128)(2,1)S(1)}, bf16[2,128,128]{2,1,0:T(8,128)(2,1)S(1)}, u32[]{:S(2)}, u32[]{:S(2)}) collective-permute-start(bf16[2,128,128]{2,1,0:T(8,128)(2,1)S(1)} %bitcast.89), channel_id=1, source_target_pairs={{0,7},{1,6},{2,5},{3,4},{4,3},{5,2},{6,1},{7,0},{8,15},{9,14},{10,... | collective-permute-start | bytes 196616 | tf_op jit(solution)/shard_map/ppermute | solution.py:263
  43.4 19.9 %collective-permute-start.4 = (bf16[2,128,128]{2,1,0:T(8,128)(2,1)S(1)}, bf16[2,128,128]{2,1,0:T(8,128)(2,1)S(1)}, u32[]{:S(2)}, u32[]{:S(2)}) collective-permute-start(bf16[2,128,128]{2,1,0:T(8,128)(2,1)S(1)} %bitcast.88), channel_id=1, source_target_pairs={{0,4},{1,5},{2,6},{3,7},{4,0},{5,1},{6,2},{7,3},{8,12},{9,13},{10,... | collective-permute-start | bytes 196616 | tf_op jit(solution)/shard_map/ppermute | solution.py:263
  44.9 19.6 %collective-permute-start.5 = (bf16[2,128,128]{2,1,0:T(8,128)(2,1)S(1)}, bf16[2,128,128]{2,1,0:T(8,128)(2,1)S(1)}, u32[]{:S(2)}, u32[]{:S(2)}) collective-permute-start(bf16[2,128,128]{2,1,0:T(8,128)(2,1)S(1)} %bitcast.86), channel_id=1, source_target_pairs={{0,5},{1,4},{2,7},{3,6},{4,1},{5,0},{6,3},{7,2},{8,13},{9,12},{10,... | collective-permute-start | bytes 196616 | tf_op jit(solution)/shard_map/ppermute | solution.py:263
  45.2 21.1 %collective-permute-start.6 = (bf16[2,128,128]{2,1,0:T(8,128)(2,1)S(1)}, bf16[2,128,128]{2,1,0:T(8,128)(2,1)S(1)}, u32[]{:S(2)}, u32[]{:S(2)}) collective-permute-start(bf16[2,128,128]{2,1,0:T(8,128)(2,1)S(1)} %bitcast.87), channel_id=1, source_target_pairs={{0,6},{1,7},{2,4},{3,5},{4,2},{5,3},{6,0},{7,1},{8,14},{9,15},{10,... | collective-permute-start | bytes 196616 | tf_op jit(solution)/shard_map/ppermute | solution.py:263
  46.8 0.9 %copy-start.3 = (f32[32,2048]{1,0:T(8,128)S(1)}, f32[32,2048]{1,0:T(8,128)}, u32[]{:S(2)}) copy-start(f32[32,2048]{1,0:T(8,128)} %param.11) | copy-start | bytes 786436
  47.9 0.8 copy-start.4
  61.6 4.7 %collective-permute-start.1 = (bf16[2,128,128]{2,1,0:T(8,128)(2,1)S(1)}, bf16[2,128,128]{2,1,0:T(8,128)(2,1)S(1)}, u32[]{:S(2)}, u32[]{:S(2)}) collective-permute-start(bf16[2,128,128]{2,1,0:T(8,128)(2,1)S(1)} %bitcast.92), channel_id=1, source_target_pairs={{0,1},{1,0},{2,3},{3,2},{4,5},{5,4},{6,7},{7,6},{8,9},{9,8},{10,11... | collective-permute-start | bytes 196616 | tf_op jit(solution)/shard_map/ppermute | solution.py:263
  62.4 5.3 %collective-permute-start.2 = (bf16[2,128,128]{2,1,0:T(8,128)(2,1)S(1)}, bf16[2,128,128]{2,1,0:T(8,128)(2,1)S(1)}, u32[]{:S(2)}, u32[]{:S(2)}) collective-permute-start(bf16[2,128,128]{2,1,0:T(8,128)(2,1)S(1)} %bitcast.91), channel_id=1, source_target_pairs={{0,2},{1,3},{2,0},{3,1},{4,6},{5,7},{6,4},{7,5},{8,10},{9,11},{10,... | collective-permute-start | bytes 196616 | tf_op jit(solution)/shard_map/ppermute | solution.py:263
  63.3 5.6 %collective-permute-start.3 = (bf16[2,128,128]{2,1,0:T(8,128)(2,1)S(1)}, bf16[2,128,128]{2,1,0:T(8,128)(2,1)S(1)}, u32[]{:S(2)}, u32[]{:S(2)}) collective-permute-start(bf16[2,128,128]{2,1,0:T(8,128)(2,1)S(1)} %bitcast.90), channel_id=1, source_target_pairs={{0,3},{1,2},{2,1},{3,0},{4,7},{5,6},{6,5},{7,4},{8,11},{9,10},{10,... | collective-permute-start | bytes 196616 | tf_op jit(solution)/shard_map/ppermute | solution.py:263
  63.8 0.7 copy-start.7
  72.4 14.9 %all-to-all-start.1 = ((bf16[8,2,128,128]{3,2,1,0:T(8,128)(2,1)}), bf16[8,2,128,128]{3,2,1,0:T(8,128)(2,1)S(1)}, u32[]{:S(2)}, u32[]{:S(2)}) async-start(bf16[8,2,128,128]{3,2,1,0:T(8,128)(2,1)} %get-tuple-element.22), calls=%async_computation.1 | async-start | bytes 1048576 | tf_op jit(solution)/shard_map/all_to_all | solution.py:293
  78.3 8.4 %collective-permute-start.7 = (f32[32,128]{1,0:T(8,128)S(1)}, f32[32,128]{1,0:T(8,128)S(1)}, u32[]{:S(2)}, u32[]{:S(2)}) collective-permute-start(f32[32,128]{1,0:T(8,128)S(1)} %slice_bitcast_fusion), channel_id=1, source_target_pairs={{0,8},{1,9},{2,10},{3,11},{4,12},{5,13},{6,14},{7,15},{8,0},{9,1},... | collective-permute-start | bytes 49160 | tf_op jit(solution)/shard_map/ppermute | solution.py:326

commit v7 on v6

--- a/solution.py
+++ b/solution.py
@@ -80,6 +80,8 @@
     states,
     high,
     low,
+    result,
+    sems,
 ):
     n_src, _, rows_dev, width = g_ref.shape
     rows = rows_dev // 2
@@ -125,6 +127,7 @@
             state_real = next_real
     gain = gain_ref[...]
     both_weight = twice(weight)
+    leaving = []
     for source in range(n_own):
         for part in range(2):
             slot = 2 * source + part
@@ -140,8 +143,14 @@
                 + gain * side_by_side(g_ref, own_base + source, part).astype(F32)
             ).astype(BF16)
             at = slice(part * rows, (part + 1) * rows)
-            y_ref[source, 0, at, :] = value[:, :width]
-            y_ref[source, 1, at, :] = value[:, width:]
+            result[source, 0, at, :] = value[:, :width]
+            result[source, 1, at, :] = value[:, width:]
+        leaving.append(
+            pltpu.make_async_copy(result.at[source], y_ref.at[source], sems.at[source])
+        )
+        leaving[-1].start()
+    for move in leaving:
+        move.wait()
 
 
 def weight_kernel(place_ref, g_ref, states_ref, left_g_ref, left_x_ref, spectrum_ref, *refs):
@@ -180,21 +189,34 @@
         wgrad_ref[half ^ block] = total[:, block * width : (block + 1) * width]
 
 
-def split_kernel(value_ref, parts_ref, sems):
-    copies, groups, _, own = parts_ref.shape
-    n_own = value_ref.shape[1] // (groups * own)
-    moves = []
-    for target in range(copies):
-        for group in range(groups):
-            at = (group * n_own + target % n_own) * own
-            moves.append(
+def split_kernel(value_ref, parts_ref, held, parts, sems_in, sems_out):
+    n_own, groups, rows_dev, own = parts.shape
+    chunks = sems_in.shape[0]
+    rows = rows_dev // chunks
+    copies = parts_ref.shape[0] // n_own
+    arrivals = []
+    for chunk in range(chunks):
+        at = pl.ds(chunk * rows, rows)
+        arrivals.append(pltpu.make_async_copy(value_ref.at[at], held.at[at], sems_in.at[chunk]))
+        arrivals[-1].start()
+    leaving = []
+    for chunk in range(chunks):
+        at = pl.ds(chunk * rows, rows)
+        arrivals[chunk].wait()
+        for target in range(n_own):
+            for group in range(groups):
+                column = (group * n_own + target) * own
+                parts[target, group, at] = held[at, column : column + own]
+        for copy in range(copies):
+            leaving.append(
                 pltpu.make_async_copy(
-                    value_ref.at[:, at : at + own], parts_ref.at[target, group], sems.at[target, group]
+                    parts.at[:, :, at],
+                    parts_ref.at[pl.ds(copy * n_own, n_own), :, at],
+                    sems_out.at[chunk, copy],
                 )
             )
-    for move in moves:
-        move.start()
-    for move in moves:
+            leaving[-1].start()
+    for move in leaving:
         move.wait()
 
 
@@ -241,9 +263,14 @@
         blocks = pl.pallas_call(
             split_kernel,
             out_shape=jax.ShapeDtypeStruct((devices, 2, rows_dev, own), BF16),
-            in_specs=[anywhere],
+            in_specs=[pl.BlockSpec(memory_space=pltpu.HBM)],
             out_specs=anywhere,
-            scratch_shapes=[pltpu.SemaphoreType.DMA((devices, 2))],
+            scratch_shapes=[
+                pltpu.VMEM((rows_dev, channels), BF16),
+                pltpu.VMEM((n_own, 2, rows_dev, own), BF16),
+                pltpu.SemaphoreType.DMA((4,)),
+                pltpu.SemaphoreType.DMA((4, 2)),
+            ],
             compiler_params=pltpu.CompilerParams(vmem_limit_bytes=60 * 2**20),
             name="split",
         )(grad_out)
@@ -253,20 +280,16 @@
     g = widened(lax.all_to_all(blocks, "seq", 0, 0, tiled=True))
     made, later_inputs = tables(rows, filter_rates, filter_freqs, inputs)
     left_g, left_x, back, spectrum, step = made
-    x_parts = [None] * n_own
-    for offset in range(n_own - 1, -1, -1):
-        taken = later_inputs if offset >= n_own // 2 else near_inputs
-        x_blocks = taken.reshape(rows_dev, 2, n_own, own)
+    x_blocks = later_inputs.reshape(rows_dev, 2, n_own, own)
+    x_parts = []
+    for offset in range(n_own):
         part = lax.dynamic_index_in_dim(x_blocks, rank ^ offset, 2, keepdims=False)
         part = part.transpose(1, 0, 2)
         if offset:
             part = lax.ppermute(part, "seq", [(i, i ^ offset) for i in range(devices)])
-        if offset == n_own - 1:
-            near_inputs, part = lax.optimization_barrier((later_inputs, part))
-        x_parts[offset] = widened(part)
+        x_parts.append(widened(part))
     weight = own_blocks(filter_weight)
     gain = own_blocks(skip_gain[None, :])
-    g, *x_parts = lax.optimization_barrier((g, *x_parts))
     place = jnp.concatenate([jnp.stack([half, rank]).astype(jnp.int32), span_of_slot])
     n_spans = 2 * devices
     smem = pl.BlockSpec(memory_space=pltpu.SMEM)
@@ -279,15 +302,18 @@
             jax.ShapeDtypeStruct((devices, 2 * n_basis, lanes), F32),
         ),
         in_specs=[smem] + [vmem] * 7,
-        out_specs=(vmem, vmem),
+        out_specs=(anywhere, vmem),
         scratch_shapes=[
             pltpu.SMEM((n_spans,), jnp.int32),
             pltpu.VMEM((n_spans, 2 * n_basis, lanes), F32),
             pltpu.VMEM((n_spans, 2 * n_basis, lanes), F32),
             pltpu.VMEM((devices, 2 * rows, lanes), BF16),
             pltpu.VMEM((devices, 2 * rows, lanes), BF16),
+            pltpu.VMEM((n_own, 2, rows_dev, width), BF16),
+            pltpu.SemaphoreType.DMA((n_own,)),
         ],
         compiler_params=params,
+        cost_estimate=pl.CostEstimate(flops=4*10**10, bytes_accessed=2**20, transcendentals=0),
         name="input_part",
     )(place, g, weight, gain, left_g, back, spectrum, step)
     y = lax.all_to_all(
@@ -317,7 +343,7 @@
         out_specs=vmem,
         compiler_params=params,
         cost_estimate=pl.CostEstimate(
-            flops=8 * (rows + n_basis) * rows * n_spans * lanes,
+            flops=50 * 8 * (rows + n_basis) * rows * n_spans * lanes,
             bytes_accessed=4 * n_spans * rows * lanes,
             transcendentals=0,
         ),

time: 88.6 us -> 54.4 us (0.61)
  Pallas kernels: 39.2 us -> 7.99 us
  waiting for transfers between devices: 21.6 us -> 16.9 us
  local copies, waits for them, and re-layouts: 4.42 us -> 5.99 us
    pallas_call x1, Pallas kernels: 33.2 us -> 2.04 us  [on_device(): pl.pallas_call(split_kernel, out_shape=jax.ShapeDtypeStruct((devices, 2,...]
    ppermute x7, waiting for transfers between devices: 16.4 us -> 0.02 us  [on_device(): part = lax.ppermute(part, 'seq', [(i, i ^ offset) for i in range(devices)])]
    all_to_all x1, waiting for transfers between devices: 0.01 us -> 11.5 us  [on_device(): g = widened(lax.all_to_all(blocks, 'seq', 0, 0, tiled=True))]
    unnamed x28 -> x27, local copies, waits for them, and re-layouts: 2.51 us -> 4.09 us
  transfers between devices with their start and end apart: 10 -> 10, of which waited for: 5 -> 2; matrix products, arithmetic and copies ran while one was open for 4% -> 10% of each run, Pallas kernels for 2% -> 9%
where the time goes in v7:
time: 54.4 us; the launch traced here: 54 us
  starting transfers between devices  20.7 us (38%)
  waiting for transfers between devices  16.9 us (31%)
  Pallas kernels  7.99 us (15%)
  local copies, waits for them, and re-layouts  5.99 us (11%)
  other arithmetic  1.16 us (2%)
  between operations  1.04 us (2%)
    all_to_all x1, waiting for transfers between devices, on_device(): g = widened(lax.all_to_all(blocks, 'seq', 0, 0, tiled=True))  11.5 us
    ppermute x7, starting transfers between devices, on_device(): part = lax.ppermute(part, 'seq', [(i, i ^ offset) for i in range(devices)])  6.52 us
    all_to_all x1, starting transfers between devices, on_device(): g = widened(lax.all_to_all(blocks, 'seq', 0, 0, tiled=True))  6.44 us
    ppermute x1, waiting for transfers between devices, on_device(): lax.ppermute(wgrad[1], 'seq', [(i, i ^ n_own) for i in range(devices)])  5.35 us
    all_to_all x1, starting transfers between devices, on_device(): lax.all_to_all(y[..., :own], 'seq', 0, 0, tiled=True, axis_index_groups=[...  4.36 us
    unnamed x27, local copies, waits for them, and re-layouts  4.09 us
    ppermute x1, starting transfers between devices, on_device(): lax.ppermute(wgrad[1], 'seq', [(i, i ^ n_own) for i in range(devices)])  3.38 us
    pallas_call x1, Pallas kernels, on_device(): pl.pallas_call(input_kernel, out_shape=(jax.ShapeDtypeStruct((n_own, 2, r...  3.34 us
  transfers between devices with their start and end apart: 10, of which 2 were waited for; matrix products, arithmetic and copies ran while one was open for 10% of the time, Pallas kernels for 9%

profile of v7, /device:TPU:8, one launch (start us, length us, event | category | flops | bytes accessed | tf_op | source)
XLA Modules:
  0.0 54.0 jit_solution(17238975267003450209)
XLA Ops:
  0.6 0.0 copy-start
  0.6 2.0 %split.1 = bf16[16,2,128,128]{3,2,1,0:T(8,128)(2,1)} custom-call(bf16[128,2048]{1,0:T(8,128)(2,1)} %value_ref.1), custom_call_target="tpu_custom_call" | custom-call | tf_op jit(solution)/shard_map/split/pallas_call | solution.py:263
  2.7 0.0 copy-start.5
  2.7 0.0 copy-start.6
  2.7 0.0 copy-start.1
  2.7 6.4 %all-to-all-start = ((bf16[16,2,128,128]{3,2,1,0:T(8,128)(2,1)}), bf16[16,2,128,128]{3,2,1,0:T(8,128)(2,1)S(1)}, u32[]{:S(2)}, u32[]{:S(2)}) async-start(bf16[16,2,128,128]{3,2,1,0:T(8,128)(2,1)} %split.1), calls=%async_computation | async-start | bytes 2097152 | tf_op jit(solution)/shard_map/all_to_all | solution.py:280
  9.2 0.0 copy-start.2
  9.2 0.0 copy-done.5
  9.2 0.0 copy-done.6
  9.2 0.1 fusion.5
  9.4 0.6 %copy-done.2 = f32[128,64]{1,0:T(8,128)S(1)} copy-done((f32[128,64]{1,0:T(8,128)S(1)}, f32[128,64]{1,0:T(8,128)}, u32[]{:S(2)}) %copy-start.2) | copy-done | bytes 32792
  10.0 0.2 fusion.10
  10.2 0.0 copy-done.1
  10.2 0.1 copy.50
  10.4 1.1 %constant_dynamic-slice_fusion = (bf16[128,2,1,128]{3,2,1,0:T(2,128)(2,1)S(1)}, bf16[128,2,1,128]{3,2,1,0:T(2,128)(2,1)S(1)}, bf16[128,2,1,128]{3,2,1,0:T(2,128)...) fusion(bf16[128,2,8,128]{3,2,1,0:T(8,128)(2,1)S(1)} %bitcast.75, ...), kind=kLoop, calls=%fused_computation.37 | loop fusion | bytes 1048608 | tf_op jit(solution)/shard_map/jit(dynamic_index_in_dim)/dynamic_slice | solution.py:286
  11.5 0.2 collective-permute-start
  11.8 1.5 %collective-permute-start.1 = (bf16[2,128,128]{2,1,0:T(8,128)(2,1)S(1)}, bf16[2,128,128]{2,1,0:T(8,128)(2,1)S(1)}, u32[]{:S(2)}, u32[]{:S(2)}) collective-permute-start(bf16[2,128,128]{2,1,0:T(8,128)(2,1)S(1)} %bitcast.83), channel_id=1, source_target_pairs={{0,2},{1,3},{2,0},{3,1},{4,6},{5,7},{6,4},{7,5},{8,10},{9,11},{10,... | collective-permute-start | bytes 196616 | tf_op jit(solution)/shard_map/ppermute | solution.py:289
  13.3 0.3 collective-permute-start.2
  13.6 0.4 collective-permute-start.3
  14.0 0.6 %copy.62 = bf16[128,2,1,128]{3,0,1,2:T(8,128)(2,1)} copy(bf16[128,2,1,128]{3,2,1,0:T(2,128)(2,1)S(1)} %get-tuple-element.12) | data formatting | bytes 131072
  14.7 0.0 copy-start.3
  14.7 1.4 %collective-permute-start.4 = (bf16[2,128,128]{2,1,0:T(8,128)(2,1)}, bf16[2,128,128]{2,1,0:T(8,128)(2,1)S(1)}, u32[]{:S(2)}, u32[]{:S(2)}) collective-permute-start(bf16[2,128,128]{2,1,0:T(8,128)(2,1)} %bitcast.65), channel_id=1, source_target_pairs={{0,5},{1,4},{2,7},{3,6},{4,1},{5,0},{6,3},{7,2},{8,13},{9,12},{10,... | collective-permute-start | bytes 196616 | tf_op jit(solution)/shard_map/ppermute | solution.py:289
  16.1 0.2 slice_reduce_fusion
  16.3 0.1 copy.29.step_ref
  16.4 0.1 fusion.12
  16.5 0.1 rev.8
  16.6 0.1 rev.9
  16.6 0.1 copy.27
  16.7 0.1 copy.26
  16.8 0.1 copy.28.spectrum_ref
  16.9 0.0 copy-done.3
  17.0 0.6 %copy.60 = bf16[128,2,1,128]{3,0,1,2:T(8,128)(2,1)} copy(bf16[128,2,1,128]{3,2,1,0:T(2,128)(2,1)S(1)} %get-tuple-element.10) | data formatting | bytes 131072
  17.7 0.6 %copy.61 = bf16[128,2,1,128]{3,0,1,2:T(8,128)(2,1)} copy(bf16[128,2,1,128]{3,2,1,0:T(2,128)(2,1)S(1)} %get-tuple-element.11) | data formatting | bytes 131072
  18.3 0.0 copy-done
  18.4 0.1 pad_maximum_fusion.5.left_x_ref
  18.5 0.0 copy-start.4
  18.5 0.1 pad_maximum_fusion.4.left_g_ref
  18.6 0.7 %copy-done.4 = f32[64,128]{1,0:T(8,128)S(1)} copy-done((f32[64,128]{1,0:T(8,128)S(1)}, f32[64,128]{1,0:T(8,128)}, u32[]{:S(2)}) %copy-start.4) | copy-done | bytes 32792
  19.3 0.1 reduce-precision_convert_fusion.2
  19.4 0.0 copy-start.7
  19.4 0.6 %copy-done.7 = s32[32]{0:T(128)S(1)} copy-done((s32[32]{0:T(128)S(1)}, s32[32]{0:T(128)}, u32[]{:S(2)}) %copy-start.7) | copy-done | bytes 152
  20.0 0.1 pad_add_fusion.place_ref
  20.1 0.0 collective-permute-done.refs_1_
  20.1 1.5 %collective-permute-start.5 = (bf16[2,128,128]{2,1,0:T(8,128)(2,1)}, bf16[2,128,128]{2,1,0:T(8,128)(2,1)S(1)}, u32[]{:S(2)}, u32[]{:S(2)}) collective-permute-start(bf16[2,128,128]{2,1,0:T(8,128)(2,1)} %bitcast.64), channel_id=1, source_target_pairs={{0,6},{1,7},{2,4},{3,5},{4,2},{5,3},{6,0},{7,1},{8,14},{9,15},{10,... | collective-permute-start | bytes 196616 | tf_op jit(solution)/shard_map/ppermute | solution.py:289
  21.6 0.0 collective-permute-done.1.refs_2_
  21.6 1.1 %collective-permute-start.6 = (bf16[2,128,128]{2,1,0:T(8,128)(2,1)}, bf16[2,128,128]{2,1,0:T(8,128)(2,1)S(1)}, u32[]{:S(2)}, u32[]{:S(2)}) collective-permute-start(bf16[2,128,128]{2,1,0:T(8,128)(2,1)} %bitcast.63), channel_id=1, source_target_pairs={{0,7},{1,6},{2,5},{3,4},{4,3},{5,2},{6,1},{7,0},{8,15},{9,14},{10,... | collective-permute-start | bytes 196616 | tf_op jit(solution)/shard_map/ppermute | solution.py:289
  22.7 11.5 %all-to-all-done.g_ref = bf16[16,2,128,128]{3,2,1,0:T(8,128)(2,1)S(1)} async-done(((bf16[16,2,128,128]{3,2,1,0:T(8,128)(2,1)}), bf16[16,2,128,128]{3,2,1,0:T(8,128)(2,1)S(1)}, u32[]{:S(2)}, u32[]{:S(2)}) %all-to-all-start) | async-done | bytes 1048608 | tf_op jit(solution)/shard_map/all_to_all | solution.py:280
  34.2 3.3 %input_part.1 = (bf16[8,2,128,128]{3,2,1,0:T(8,128)(2,1)}, f32[16,64,256]{2,1,0:T(8,128)S(1)}) custom-call(s32[34]{0:T(128)S(1)} %pad_add_fusion.place_ref, bf16[16,2,128,128]{3,2,1,0:T(8,128)(2,1)S(1)} %all-to-all-done.g_ref, f32[32,256]{1,0:T(8,128)S(1)} %bitcast.74, f32[1,256]{1,0:T(1,128)S(1)} %fusion.8.gain_ref, ...), custom_call_target="tpu_custom_call" | custom-call | flops 40000000000 | bytes 1048576 | tf_op jit(solution)/shard_map/input_part/pallas_call | solution.py:298
  37.6 4.4 %all-to-all-start.1 = ((bf16[8,2,128,128]{3,2,1,0:T(8,128)(2,1)}), bf16[8,2,128,128]{3,2,1,0:T(8,128)(2,1)S(1)}, u32[]{:S(2)}, u32[]{:S(2)}) async-start(bf16[8,2,128,128]{3,2,1,0:T(8,128)(2,1)} %get-tuple-element.7), calls=%async_computation.1 | async-start | bytes 1048576 | tf_op jit(solution)/shard_map/all_to_all | solution.py:319
  41.9 0.0 collective-permute-done.2.refs_3_
  41.9 0.0 collective-permute-done.3.refs_4_
  42.0 0.0 collective-permute-done.4.refs_5_
  42.0 0.0 collective-permute-done.5.refs_6_
  42.0 0.0 collective-permute-done.6.refs_7_
  42.0 1.7 %weight_part.1 = f32[2,32,128]{2,1,0:T(8,128)S(1)} custom-call(s32[34]{0:T(128)S(1)} %pad_add_fusion.place_ref, bf16[16,2,128,128]{3,2,1,0:T(8,128)(2,1)S(1)} %all-to-all-done.g_ref, f32[16,64,256]{2,1,0:T(8,128)S(1)} %get-tuple-element.8.states_ref, bf16[192,128]{1,0:T(8,128)(2,1)S(1)} %pad_maximum_fusion.4.left_g_ref, ...), custom_call_target="tpu_custom_call" | custom-call | flops 20132659200 | bytes 2097152 | tf_op jit(solution)/shard_map/weight_part/pallas_call | solution.py:339
  43.7 3.4 %collective-permute-start.7 = (f32[32,128]{1,0:T(8,128)S(1)}, f32[32,128]{1,0:T(8,128)S(1)}, u32[]{:S(2)}, u32[]{:S(2)}) collective-permute-start(f32[32,128]{1,0:T(8,128)S(1)} %slice_bitcast_fusion), channel_id=1, source_target_pairs={{0,8},{1,9},{2,10},{3,11},{4,12},{5,13},{6,14},{7,15},{8,0},{9,1},... | collective-permute-start | bytes 49160 | tf_op jit(solution)/shard_map/ppermute | solution.py:352
  47.1 5.3 %collective-permute-done.7 = f32[32,128]{1,0:T(8,128)S(1)} collective-permute-done((f32[32,128]{1,0:T(8,128)S(1)}, f32[32,128]{1,0:T(8,128)S(1)}, u32[]{:S(2)}, u32[]{:S(2)}) %collective-permute-start.7) | collective-permute-done | bytes 16416 | tf_op jit(solution)/shard_map/ppermute | solution.py:352
  52.4 0.6 %fusion.7 = f32[32,128]{1,0:T(8,128)} fusion(f32[32,128]{1,0:T(8,128)S(1)} %collective-permute-done.7, f32[2,32,128]{2,1,0:T(8,128)S(1)} %weight_part.1), kind=kLoop, calls=%fused_computation.32 | loop fusion | flops 4096 | bytes 49152 | tf_op jit(solution)/shard_map/add | solution.py:353
  53.0 0.0 all-to-all-done.1.parts_ref
  53.0 0.9 %join.1 = bf16[128,2048]{1,0:T(8,128)(2,1)} custom-call(bf16[8,2,128,128]{3,2,1,0:T(8,128)(2,1)S(1)} %all-to-all-done.1.parts_ref), custom_call_target="tpu_custom_call" | custom-call | tf_op jit(solution)/shard_map/join/pallas_call | solution.py:328
  (16 shorter events, 0.2 us)
Async XLA Ops:
  0.6 17.7 %copy-start = (f32[2048]{0:T(1024)S(1)}, f32[2048]{0:T(1024)}, u32[]{:S(2)}) copy-start(f32[2048]{0:T(1024)} %param.14) | copy-start | bytes 24580
  2.7 6.5 %copy-start.5 = (f32[32]{0:T(128)S(1)}, f32[32]{0:T(128)}, u32[]{:S(2)}) copy-start(f32[32]{0:T(128)} %param.13) | copy-start | bytes 388
  2.7 6.5 %copy-start.6 = (f32[32]{0:T(128)S(1)}, f32[32]{0:T(128)}, u32[]{:S(2)}) copy-start(f32[32]{0:T(128)} %param.12) | copy-start | bytes 388
  2.7 7.5 %copy-start.1 = (bf16[128,2048]{1,0:T(8,128)(2,1)S(1)}, bf16[128,2048]{1,0:T(8,128)(2,1)}, u32[]{:S(2)}) copy-start(bf16[128,2048]{1,0:T(8,128)(2,1)} %param.9) | copy-start | bytes 1572868
  2.7 31.5 %all-to-all-start = ((bf16[16,2,128,128]{3,2,1,0:T(8,128)(2,1)}), bf16[16,2,128,128]{3,2,1,0:T(8,128)(2,1)S(1)}, u32[]{:S(2)}, u32[]{:S(2)}) async-start(bf16[16,2,128,128]{3,2,1,0:T(8,128)(2,1)} %split.1), calls=%async_computation | async-start | bytes 2097152 | tf_op jit(solution)/shard_map/all_to_all | solution.py:280
  9.2 0.8 %copy-start.2 = (f32[128,64]{1,0:T(8,128)S(1)}, f32[128,64]{1,0:T(8,128)}, u32[]{:S(2)}) copy-start(f32[128,64]{1,0:T(8,128)} %constant.72.clone) | copy-start | bytes 98308
  11.5 8.6 %collective-permute-start = (bf16[2,128,128]{2,1,0:T(8,128)(2,1)S(1)}, bf16[2,128,128]{2,1,0:T(8,128)(2,1)S(1)}, u32[]{:S(2)}, u32[]{:S(2)}) collective-permute-start(bf16[2,128,128]{2,1,0:T(8,128)(2,1)S(1)} %bitcast.84), channel_id=1, source_target_pairs={{0,1},{1,0},{2,3},{3,2},{4,5},{5,4},{6,7},{7,6},{8,9},{9,8},{10,11... | collective-permute-start | bytes 196616 | tf_op jit(solution)/shard_map/ppermute | solution.py:289
  11.8 9.8 %collective-permute-start.1 = (bf16[2,128,128]{2,1,0:T(8,128)(2,1)S(1)}, bf16[2,128,128]{2,1,0:T(8,128)(2,1)S(1)}, u32[]{:S(2)}, u32[]{:S(2)}) collective-permute-start(bf16[2,128,128]{2,1,0:T(8,128)(2,1)S(1)} %bitcast.83), channel_id=1, source_target_pairs={{0,2},{1,3},{2,0},{3,1},{4,6},{5,7},{6,4},{7,5},{8,10},{9,11},{10,... | collective-permute-start | bytes 196616 | tf_op jit(solution)/shard_map/ppermute | solution.py:289
  13.3 28.6 %collective-permute-start.2 = (bf16[2,128,128]{2,1,0:T(8,128)(2,1)S(1)}, bf16[2,128,128]{2,1,0:T(8,128)(2,1)S(1)}, u32[]{:S(2)}, u32[]{:S(2)}) collective-permute-start(bf16[2,128,128]{2,1,0:T(8,128)(2,1)S(1)} %bitcast.81), channel_id=1, source_target_pairs={{0,3},{1,2},{2,1},{3,0},{4,7},{5,6},{6,5},{7,4},{8,11},{9,10},{10,... | collective-permute-start | bytes 196616 | tf_op jit(solution)/shard_map/ppermute | solution.py:289
  13.6 28.3 %collective-permute-start.3 = (bf16[2,128,128]{2,1,0:T(8,128)(2,1)S(1)}, bf16[2,128,128]{2,1,0:T(8,128)(2,1)S(1)}, u32[]{:S(2)}, u32[]{:S(2)}) collective-permute-start(bf16[2,128,128]{2,1,0:T(8,128)(2,1)S(1)} %bitcast.82), channel_id=1, source_target_pairs={{0,4},{1,5},{2,6},{3,7},{4,0},{5,1},{6,2},{7,3},{8,12},{9,13},{10,... | collective-permute-start | bytes 196616 | tf_op jit(solution)/shard_map/ppermute | solution.py:289
  14.7 2.3 %copy-start.3 = (f32[32,2048]{1,0:T(8,128)S(1)}, f32[32,2048]{1,0:T(8,128)}, u32[]{:S(2)}) copy-start(f32[32,2048]{1,0:T(8,128)} %param.11) | copy-start | bytes 786436
  14.7 27.3 %collective-permute-start.4 = (bf16[2,128,128]{2,1,0:T(8,128)(2,1)}, bf16[2,128,128]{2,1,0:T(8,128)(2,1)S(1)}, u32[]{:S(2)}, u32[]{:S(2)}) collective-permute-start(bf16[2,128,128]{2,1,0:T(8,128)(2,1)} %bitcast.65), channel_id=1, source_target_pairs={{0,5},{1,4},{2,7},{3,6},{4,1},{5,0},{6,3},{7,2},{8,13},{9,12},{10,... | collective-permute-start | bytes 196616 | tf_op jit(solution)/shard_map/ppermute | solution.py:289
  18.5 0.8 %copy-start.4 = (f32[64,128]{1,0:T(8,128)S(1)}, f32[64,128]{1,0:T(8,128)}, u32[]{:S(2)}) copy-start(f32[64,128]{1,0:T(8,128)} %constant.73.clone) | copy-start | bytes 98308
  19.4 0.7 %copy-start.7 = (s32[32]{0:T(128)S(1)}, s32[32]{0:T(128)}, u32[]{:S(2)}) copy-start(s32[32]{0:T(128)} %param.15) | copy-start | bytes 388
  20.1 21.9 %collective-permute-start.5 = (bf16[2,128,128]{2,1,0:T(8,128)(2,1)}, bf16[2,128,128]{2,1,0:T(8,128)(2,1)S(1)}, u32[]{:S(2)}, u32[]{:S(2)}) collective-permute-start(bf16[2,128,128]{2,1,0:T(8,128)(2,1)} %bitcast.64), channel_id=1, source_target_pairs={{0,6},{1,7},{2,4},{3,5},{4,2},{5,3},{6,0},{7,1},{8,14},{9,15},{10,... | collective-permute-start | bytes 196616 | tf_op jit(solution)/shard_map/ppermute | solution.py:289
  21.6 20.4 %collective-permute-start.6 = (bf16[2,128,128]{2,1,0:T(8,128)(2,1)}, bf16[2,128,128]{2,1,0:T(8,128)(2,1)S(1)}, u32[]{:S(2)}, u32[]{:S(2)}) collective-permute-start(bf16[2,128,128]{2,1,0:T(8,128)(2,1)} %bitcast.63), channel_id=1, source_target_pairs={{0,7},{1,6},{2,5},{3,4},{4,3},{5,2},{6,1},{7,0},{8,15},{9,14},{10,... | collective-permute-start | bytes 196616 | tf_op jit(solution)/shard_map/ppermute | solution.py:289
  37.6 15.5 %all-to-all-start.1 = ((bf16[8,2,128,128]{3,2,1,0:T(8,128)(2,1)}), bf16[8,2,128,128]{3,2,1,0:T(8,128)(2,1)S(1)}, u32[]{:S(2)}, u32[]{:S(2)}) async-start(bf16[8,2,128,128]{3,2,1,0:T(8,128)(2,1)} %get-tuple-element.7), calls=%async_computation.1 | async-start | bytes 1048576 | tf_op jit(solution)/shard_map/all_to_all | solution.py:319
  43.7 8.7 %collective-permute-start.7 = (f32[32,128]{1,0:T(8,128)S(1)}, f32[32,128]{1,0:T(8,128)S(1)}, u32[]{:S(2)}, u32[]{:S(2)}) collective-permute-start(f32[32,128]{1,0:T(8,128)S(1)} %slice_bitcast_fusion), channel_id=1, source_target_pairs={{0,8},{1,9},{2,10},{3,11},{4,12},{5,13},{6,14},{7,15},{8,0},{9,1},... | collective-permute-start | bytes 49160 | tf_op jit(solution)/shard_map/ppermute | solution.py:352

commit v8 on v7

--- a/solution.py
+++ b/solution.py
@@ -30,7 +30,7 @@
     return np.cos(angles), -np.sin(angles)
 
 
-def tables(rows, rates, freqs, inputs):
+def tables(rows, rates, freqs):
     cos_part, sin_part = odd_frequencies(rows)
     forward = jnp.asarray(np.concatenate([cos_part, sin_part], 0), F32)
     inverse = jnp.asarray(np.concatenate([cos_part, sin_part], 0).T / rows, F32)
@@ -49,9 +49,8 @@
     basis_spectrum = jnp.dot(
         forward, power_real[:, :rows].T, precision=HIGHEST, preferred_element_type=F32
     )
-    later_inputs, basis_spectrum = lax.optimization_barrier((inputs, basis_spectrum))
     step = jnp.stack([power_real[:, rows], power_imag[:, rows]], 0)[:, :, None]
-    return (left_g, left_x, back, basis_spectrum, step), later_inputs
+    return left_g, left_x, back, basis_spectrum, step
 
 
 def side_by_side(ref, source, part):
@@ -153,9 +152,9 @@
         move.wait()
 
 
-def weight_kernel(place_ref, g_ref, states_ref, left_g_ref, left_x_ref, spectrum_ref, *refs):
-    x_refs, wgrad_ref = refs[:-1], refs[-1]
-    n_own = len(x_refs)
+def weight_kernel(place_ref, g_ref, states_ref, left_g_ref, left_x_ref, spectrum_ref, x_ref, wgrad_ref):
+    n_own = x_ref.shape[0]
+    bits = n_own.bit_length() - 1
     rows_dev, width = g_ref.shape[2:]
     rows = rows_dev // 2
     n_basis, lanes = states_ref.shape[1] // 2, states_ref.shape[2]
@@ -164,12 +163,11 @@
     cross_real = jnp.zeros((rows, lanes), F32)
     cross_imag = jnp.zeros((rows, lanes), F32)
     total = jnp.zeros((n_basis, lanes), F32)
-    for offset, x_ref in enumerate(x_refs):
-        source = own ^ offset
+    for index in range(n_own):
+        source = own ^ sum((index >> bit & 1) << (bits - 1 - bit) for bit in range(bits))
         for part in range(2):
-            at = slice(part * rows, (part + 1) * rows)
             g = twice(side_by_side(g_ref, half * n_own + source, part))
-            x = twice(jnp.concatenate([x_ref[0, at, :], x_ref[1, at, :]], 1))
+            x = twice(side_by_side(x_ref, index, part))
             of_g = jnp.dot(left_g, g, preferred_element_type=F32)
             of_x = jnp.dot(left_x, x, preferred_element_type=F32)
             g_real, g_imag = of_g[:rows], of_g[rows:]
@@ -189,33 +187,43 @@
         wgrad_ref[half ^ block] = total[:, block * width : (block + 1) * width]
 
 
-def split_kernel(value_ref, parts_ref, held, parts, sems_in, sems_out):
-    n_own, groups, rows_dev, own = parts.shape
+def split_kernel(side_ref, g_ref, x_ref, g_parts_ref, x_parts_ref, g_held, x_held, g_parts, sems_in, sems_out):
+    n_own, groups, rows_dev, own = g_parts.shape
+    n_side = n_own // 2
     chunks = sems_in.shape[0]
     rows = rows_dev // chunks
-    copies = parts_ref.shape[0] // n_own
     arrivals = []
     for chunk in range(chunks):
         at = pl.ds(chunk * rows, rows)
-        arrivals.append(pltpu.make_async_copy(value_ref.at[at], held.at[at], sems_in.at[chunk]))
-        arrivals[-1].start()
+        for index, (whole_ref, held) in enumerate(((g_ref, g_held), (x_ref, x_held))):
+            move = pltpu.make_async_copy(whole_ref.at[at], held.at[at], sems_in.at[chunk, index])
+            move.start()
+            arrivals.append(move)
     leaving = []
+
+    def leave(source, target, sem):
+        leaving.append(pltpu.make_async_copy(source, target, sem))
+        leaving[-1].start()
+
     for chunk in range(chunks):
         at = pl.ds(chunk * rows, rows)
-        arrivals[chunk].wait()
+        arrivals[2 * chunk].wait()
         for target in range(n_own):
             for group in range(groups):
                 column = (group * n_own + target) * own
-                parts[target, group, at] = held[at, column : column + own]
-        for copy in range(copies):
-            leaving.append(
-                pltpu.make_async_copy(
-                    parts.at[:, :, at],
-                    parts_ref.at[pl.ds(copy * n_own, n_own), :, at],
-                    sems_out.at[chunk, copy],
-                )
+                g_parts[target, group, at] = g_held[at, column : column + own]
+        for copy in range(2):
+            leave(
+                g_parts.at[:, :, at],
+                g_parts_ref.at[pl.ds(copy * n_own, n_own), :, at],
+                sems_out.at[chunk, copy],
             )
-            leaving[-1].start()
+        arrivals[2 * chunk + 1].wait()
+        for target in range(n_side):
+            for group in range(groups):
+                block = group * n_own + (1 - side_ref[0]) * n_side + target
+                column = pl.multiple_of(block * own, own)
+                x_parts_ref[target, group, at] = x_held[at, pl.ds(column, own)]
     for move in leaving:
         move.wait()
 
@@ -237,6 +245,10 @@
         move.wait()
 
 
+def exchanged(value, devices, bit):
+    return lax.ppermute(value, "seq", [(i, i ^ bit) for i in range(devices)])
+
+
 def on_device(inputs, grad_out, filter_weight, filter_rates, filter_freqs, skip_gain, span_of_slot):
     rows_dev, channels = inputs.shape
     rows = rows_dev // 2
@@ -258,42 +270,58 @@
         return widened(taken).reshape(value.shape[0], lanes)
 
     anywhere = pl.BlockSpec(memory_space=pl.ANY)
+    smem = pl.BlockSpec(memory_space=pltpu.SMEM)
+    vmem = pl.BlockSpec(memory_space=pltpu.VMEM)
     small = pltpu.CompilerParams(vmem_limit_bytes=2**20)
+    n_side = n_own // 2
+    side = rank // n_side
+    x_blocks = inputs.reshape(rows_dev, 2, n_own, own).transpose(2, 1, 0, 3)
     if own % LANES == 0:
-        blocks = pl.pallas_call(
+        blocks, x_sent = pl.pallas_call(
             split_kernel,
-            out_shape=jax.ShapeDtypeStruct((devices, 2, rows_dev, own), BF16),
-            in_specs=[pl.BlockSpec(memory_space=pltpu.HBM)],
-            out_specs=anywhere,
+            out_shape=(
+                jax.ShapeDtypeStruct((devices, 2, rows_dev, own), BF16),
+                jax.ShapeDtypeStruct((n_side, 2, rows_dev, own), BF16),
+            ),
+            in_specs=[smem, pl.BlockSpec(memory_space=pltpu.HBM), pl.BlockSpec(memory_space=pltpu.HBM)],
+            out_specs=(anywhere, vmem),
             scratch_shapes=[
                 pltpu.VMEM((rows_dev, channels), BF16),
+                pltpu.VMEM((rows_dev, channels), BF16),
                 pltpu.VMEM((n_own, 2, rows_dev, own), BF16),
-                pltpu.SemaphoreType.DMA((4,)),
+                pltpu.SemaphoreType.DMA((4, 2)),
                 pltpu.SemaphoreType.DMA((4, 2)),
             ],
             compiler_params=pltpu.CompilerParams(vmem_limit_bytes=60 * 2**20),
             name="split",
-        )(grad_out)
+        )(side.astype(jnp.int32)[None], grad_out, inputs)
     else:
         blocks = grad_out.reshape(rows_dev, 2, n_own, own).transpose(2, 1, 0, 3)
         blocks = jnp.concatenate([blocks, blocks], 0)
+        x_sent = lax.dynamic_slice_in_dim(x_blocks, (1 - side) * n_side, n_side, 0)
+    received = exchanged(x_sent, devices, n_side)
+    received, *others = lax.optimization_barrier(
+        (received, filter_weight, filter_rates, filter_freqs, skip_gain, span_of_slot, x_blocks)
+    )
+    filter_weight, filter_rates, filter_freqs, skip_gain, span_of_slot, x_blocks = others
+    x_kept = lax.dynamic_slice_in_dim(x_blocks, side * n_side, n_side, 0)
+    x_all = jnp.stack([x_kept, received], 1)
+    bit = n_side // 2
+    while bit:
+        x_all = x_all.reshape(2, bit, *x_all.shape[1:])
+        mine = rank // bit % 2
+        x_kept = lax.dynamic_index_in_dim(x_all, mine, 0, keepdims=False)
+        x_sent = lax.dynamic_index_in_dim(x_all, 1 - mine, 0, keepdims=False)
+        x_all = jnp.concatenate([x_kept, exchanged(x_sent, devices, bit)], 1)
+        bit //= 2
     g = widened(lax.all_to_all(blocks, "seq", 0, 0, tiled=True))
-    made, later_inputs = tables(rows, filter_rates, filter_freqs, inputs)
-    left_g, left_x, back, spectrum, step = made
-    x_blocks = later_inputs.reshape(rows_dev, 2, n_own, own)
-    x_parts = []
-    for offset in range(n_own):
-        part = lax.dynamic_index_in_dim(x_blocks, rank ^ offset, 2, keepdims=False)
-        part = part.transpose(1, 0, 2)
-        if offset:
-            part = lax.ppermute(part, "seq", [(i, i ^ offset) for i in range(devices)])
-        x_parts.append(widened(part))
+    x = widened(x_all[0])
+    left_g, left_x, back, spectrum, step = tables(rows, filter_rates, filter_freqs)
+    g, x = lax.optimization_barrier((g, x))
     weight = own_blocks(filter_weight)
     gain = own_blocks(skip_gain[None, :])
     place = jnp.concatenate([jnp.stack([half, rank]).astype(jnp.int32), span_of_slot])
     n_spans = 2 * devices
-    smem = pl.BlockSpec(memory_space=pltpu.SMEM)
-    vmem = pl.BlockSpec(memory_space=pltpu.VMEM)
     params = pltpu.CompilerParams(vmem_limit_bytes=24 * 2**20)
     y, states = pl.pallas_call(
         input_kernel,
@@ -339,7 +367,7 @@
     wgrad = pl.pallas_call(
         weight_kernel,
         out_shape=jax.ShapeDtypeStruct((2, n_basis, width), F32),
-        in_specs=[smem] + [vmem] * (5 + n_own),
+        in_specs=[smem] + [vmem] * 6,
         out_specs=vmem,
         compiler_params=params,
         cost_estimate=pl.CostEstimate(
@@ -348,7 +376,7 @@
             transcendentals=0,
         ),
         name="weight_part",
-    )(place, g, states, left_g, left_x, spectrum, *x_parts)
+    )(place, g, states, left_g, left_x, spectrum, x)
     other = lax.ppermute(wgrad[1], "seq", [(i, i ^ n_own) for i in range(devices)])
     return input_grad, (wgrad[0] + other)[:, :own]
 

time: 54.4 us -> 54.6 us (level)
  waiting for transfers between devices: 16.9 us -> 23.5 us
  starting transfers between devices: 20.7 us -> 16.1 us
  local copies, waits for them, and re-layouts: 5.99 us -> 3.3 us
  Pallas kernels: 7.99 us -> 8.8 us
    ppermute x7 -> x3, waiting for transfers between devices: 0.02 us -> 11.8 us  [exchanged(): return lax.ppermute(value, 'seq', [(i, i ^ bit) for i in range(devices)])]
    all_to_all x1, waiting for transfers between devices: 11.5 us -> 6.33 us  [on_device(): g = widened(lax.all_to_all(blocks, 'seq', 0, 0, tiled=True))]
    ppermute x7 -> x3, starting transfers between devices: 6.52 us -> 1.73 us  [exchanged(): return lax.ppermute(value, 'seq', [(i, i ^ bit) for i in range(devices)])]
    unnamed x27 -> x19, local copies, waits for them, and re-layouts: 4.09 us -> 2.44 us
    dynamic_slice x1 -> x2, local copies, waits for them, and re-layouts: 1.09 us -> 0.18 us  [on_device(): x_kept = lax.dynamic_slice_in_dim(x_blocks, side * n_side, n_side, 0)]
    pallas_call x1, Pallas kernels: 2.04 us -> 2.82 us  [on_device(): pl.pallas_call(split_kernel, out_shape=(jax.ShapeDtypeStruct((devices, 2,...]
    ppermute x1, starting transfers between devices: 3.38 us -> 2.67 us  [on_device(): lax.ppermute(wgrad[1], 'seq', [(i, i ^ n_own) for i in range(devices)])]
  transfers between devices with their start and end apart: 10 -> 6, of which waited for: 2 -> 5; matrix products, arithmetic and copies ran while one was open for 10% -> 5% of each run, Pallas kernels for 9% -> 3%
where the time goes in v8:
time: 54.6 us; the launch traced here: 54.2 us
  waiting for transfers between devices  23.5 us (43%)
  starting transfers between devices  16.1 us (29%)
  Pallas kernels  8.8 us (16%)
  local copies, waits for them, and re-layouts  3.3 us (6%)
  other arithmetic  1.3 us (2%)
  between operations  0.95 us (2%)
    ppermute x3, waiting for transfers between devices, exchanged(): return lax.ppermute(value, 'seq', [(i, i ^ bit) for i in range(devices)])  11.8 us
    all_to_all x1, starting transfers between devices, on_device(): g = widened(lax.all_to_all(blocks, 'seq', 0, 0, tiled=True))  6.97 us
    all_to_all x1, waiting for transfers between devices, on_device(): g = widened(lax.all_to_all(blocks, 'seq', 0, 0, tiled=True))  6.33 us
    ppermute x1, waiting for transfers between devices, on_device(): lax.ppermute(wgrad[1], 'seq', [(i, i ^ n_own) for i in range(devices)])  5.37 us
    all_to_all x1, starting transfers between devices, on_device(): lax.all_to_all(y[..., :own], 'seq', 0, 0, tiled=True, axis_index_groups=[...  4.71 us
    pallas_call x1, Pallas kernels, on_device(): pl.pallas_call(input_kernel, out_shape=(jax.ShapeDtypeStruct((n_own, 2, r...  3.34 us
    pallas_call x1, Pallas kernels, on_device(): pl.pallas_call(split_kernel, out_shape=(jax.ShapeDtypeStruct((devices, 2,...  2.82 us
    ppermute x1, starting transfers between devices, on_device(): lax.ppermute(wgrad[1], 'seq', [(i, i ^ n_own) for i in range(devices)])  2.67 us
  transfers between devices with their start and end apart: 6, of which 5 were waited for; matrix products, arithmetic and copies ran while one was open for 5% of the time, Pallas kernels for 3%

profile of v8, /device:TPU:8, one launch (start us, length us, event | category | flops | bytes accessed | tf_op | source)
XLA Modules:
  0.0 54.2 jit_solution(4919670555664334300)
XLA Ops:
  0.6 0.0 copy-start
  0.7 2.8 %split.1 = (bf16[16,2,128,128]{3,2,1,0:T(8,128)(2,1)}, bf16[4,2,128,128]{3,2,1,0:T(8,128)(2,1)}) custom-call(s32[1]{0:T(128)} %bitcast.2.side_ref, bf16[128,2048]{1,0:T(8,128)(2,1)} %g_ref.1, bf16[128,2048]{1,0:T(8,128)(2,1)} %x_ref.1), custom_call_target="tpu_custom_call" | custom-call | tf_op jit(solution)/shard_map/split/pallas_call | solution.py:280
  3.5 0.1 collective-permute-start
  3.6 0.0 copy-start.1
  3.6 7.0 %all-to-all-start = ((bf16[16,2,128,128]{3,2,1,0:T(8,128)(2,1)}), bf16[16,2,128,128]{3,2,1,0:T(8,128)(2,1)S(1)}, u32[]{:S(2)}, u32[]{:S(2)}) async-start(bf16[16,2,128,128]{3,2,1,0:T(8,128)(2,1)} %get-tuple-element.17), calls=%async_computation | async-start | bytes 2097152 | tf_op jit(solution)/shard_map/all_to_all | solution.py:317
  10.6 0.0 copy-done.1
  10.6 0.1 copy.29
  10.8 0.0 copy-start.5
  10.8 0.0 copy-start.6
  10.8 1.1 %collective-permute-done = bf16[4,2,128,128]{3,2,1,0:T(8,128)(2,1)S(1)} collective-permute-done((bf16[4,2,128,128]{3,2,1,0:T(8,128)(2,1)}, bf16[4,2,128,128]{3,2,1,0:T(8,128)(2,1)S(1)}, u32[]{:S(2)}, u32[]{:S(2)}) %collective-permute-start) | collective-permute-done | bytes 262176 | tf_op jit(solution)/shard_map/ppermute | solution.py:249
  11.8 0.0 copy-done.5
  11.8 0.0 copy-done.6
  11.8 0.1 fusion.11
  12.0 0.1 fusion.18
  12.1 0.1 constant_dynamic-slice_fusion.2
  12.2 0.1 rev.8
  12.3 0.1 rev.9
  12.4 0.0 copy-start.3
  12.4 0.9 %copy-done.3 = f32[32,2048]{1,0:T(8,128)S(1)} copy-done((f32[32,2048]{1,0:T(8,128)S(1)}, f32[32,2048]{1,0:T(8,128)}, u32[]{:S(2)}) %copy-start.3) | copy-done | bytes 262168
  13.4 0.1 fusion.3
  13.4 0.0 copy-start.2
  13.4 1.6 %collective-permute-start.1 = (bf16[2,2,2,128,128]{4,3,2,1,0:T(8,128)(2,1)S(1)}, bf16[2,2,2,128,128]{4,3,2,1,0:T(8,128)(2,1)S(1)}, u32[]{:S(2)}, u32[]{:S(2)}) collective-permute-start(bf16[2,2,2,128,128]{4,3,2,1,0:T(8,128)(2,1)S(1)} %get-tuple-element.30), channel_id=1, source_target_pairs={{0,2},{1,3},{2,0},{3,1},{4,6},{5,7},{6,4},{7,5},{8,10},{9,11},{10,... | collective-permute-start | bytes 786440 | tf_op jit(solution)/shard_map/ppermute | solution.py:249
  15.0 0.0 copy-done
  15.1 0.2 slice_reduce_fusion
  15.2 0.0 copy-done.2
  15.3 0.1 pad_maximum_fusion.5.left_x_ref
  15.4 0.1 pad_maximum_fusion.4.left_g_ref
  15.5 0.1 copy.23
  15.6 0.0 copy-start.4
  15.6 0.1 copy.22
  15.7 0.7 %copy-done.4 = f32[64,128]{1,0:T(8,128)S(1)} copy-done((f32[64,128]{1,0:T(8,128)S(1)}, f32[64,128]{1,0:T(8,128)}, u32[]{:S(2)}) %copy-start.4) | copy-done | bytes 32792
  16.4 0.1 reduce-precision_convert_fusion.2
  16.5 10.3 %collective-permute-done.1 = bf16[2,2,2,128,128]{4,3,2,1,0:T(8,128)(2,1)S(1)} collective-permute-done((bf16[2,2,2,128,128]{4,3,2,1,0:T(8,128)(2,1)S(1)}, bf16[2,2,2,128,128]{4,3,2,1,0:T(8,128)(2,1)S(1)}, u32[]{:S(2)}, u32[]{:S(2)}) %collective-permute-start.1) | collective-permute-done | bytes 262176 | tf_op jit(solution)/shard_map/ppermute | solution.py:249
  26.8 0.1 collective-permute-start.2
  26.9 0.0 copy-start.7
  26.9 0.6 %copy-done.7 = s32[32]{0:T(128)S(1)} copy-done((s32[32]{0:T(128)S(1)}, s32[32]{0:T(128)}, u32[]{:S(2)}) %copy-start.7) | copy-done | bytes 152
  27.6 0.1 pad_add_fusion.place_ref
  27.6 0.1 copy.25.step_ref
  27.7 0.2 fusion.16.spectrum_ref
  27.9 0.5 collective-permute-done.2
  28.5 6.3 %all-to-all-done.g_ref = bf16[16,2,128,128]{3,2,1,0:T(8,128)(2,1)S(1)} async-done(((bf16[16,2,128,128]{3,2,1,0:T(8,128)(2,1)}), bf16[16,2,128,128]{3,2,1,0:T(8,128)(2,1)S(1)}, u32[]{:S(2)}, u32[]{:S(2)}) %all-to-all-start) | async-done | bytes 1048608 | tf_op jit(solution)/shard_map/all_to_all | solution.py:317
  34.8 3.3 %input_part.1 = (bf16[8,2,128,128]{3,2,1,0:T(8,128)(2,1)}, f32[16,64,256]{2,1,0:T(8,128)S(1)}) custom-call(s32[34]{0:T(128)S(1)} %pad_add_fusion.place_ref, bf16[16,2,128,128]{3,2,1,0:T(8,128)(2,1)S(1)} %all-to-all-done.g_ref, f32[32,256]{1,0:T(8,128)S(1)} %bitcast.46, f32[1,256]{1,0:T(1,128)S(1)} %fusion.14.gain_ref, ...), custom_call_target="tpu_custom_call" | custom-call | flops 40000000000 | bytes 1048576 | tf_op jit(solution)/shard_map/input_part/pallas_call | solution.py:326
  38.1 4.7 %all-to-all-start.1 = ((bf16[8,2,128,128]{3,2,1,0:T(8,128)(2,1)}), bf16[8,2,128,128]{3,2,1,0:T(8,128)(2,1)S(1)}, u32[]{:S(2)}, u32[]{:S(2)}) async-start(bf16[8,2,128,128]{3,2,1,0:T(8,128)(2,1)} %get-tuple-element.25), calls=%async_computation.1 | async-start | bytes 1048576 | tf_op jit(solution)/shard_map/all_to_all | solution.py:347
  42.9 1.7 %weight_part.1 = f32[2,32,128]{2,1,0:T(8,128)S(1)} custom-call(s32[34]{0:T(128)S(1)} %pad_add_fusion.place_ref, bf16[16,2,128,128]{3,2,1,0:T(8,128)(2,1)S(1)} %all-to-all-done.g_ref, f32[16,64,256]{2,1,0:T(8,128)S(1)} %get-tuple-element.26.states_ref, bf16[192,128]{1,0:T(8,128)(2,1)S(1)} %pad_maximum_fusion.4.left_g_ref, ...), custom_call_target="tpu_custom_call" | custom-call | flops 20132659200 | bytes 2097152 | tf_op jit(solution)/shard_map/weight_part/pallas_call | solution.py:367
  44.6 2.7 %collective-permute-start.3 = (f32[32,128]{1,0:T(8,128)S(1)}, f32[32,128]{1,0:T(8,128)S(1)}, u32[]{:S(2)}, u32[]{:S(2)}) collective-permute-start(f32[32,128]{1,0:T(8,128)S(1)} %slice_bitcast_fusion), channel_id=1, source_target_pairs={{0,8},{1,9},{2,10},{3,11},{4,12},{5,13},{6,14},{7,15},{8,0},{9,1},... | collective-permute-start | bytes 49160 | tf_op jit(solution)/shard_map/ppermute | solution.py:380
  47.3 5.4 %collective-permute-done.3 = f32[32,128]{1,0:T(8,128)S(1)} collective-permute-done((f32[32,128]{1,0:T(8,128)S(1)}, f32[32,128]{1,0:T(8,128)S(1)}, u32[]{:S(2)}, u32[]{:S(2)}) %collective-permute-start.3) | collective-permute-done | bytes 16416 | tf_op jit(solution)/shard_map/ppermute | solution.py:380
  52.6 0.6 %fusion.13 = f32[32,128]{1,0:T(8,128)} fusion(f32[32,128]{1,0:T(8,128)S(1)} %collective-permute-done.3, f32[2,32,128]{2,1,0:T(8,128)S(1)} %weight_part.1), kind=kLoop, calls=%fused_computation.39 | loop fusion | flops 4096 | bytes 49152 | tf_op jit(solution)/shard_map/add | solution.py:381
  53.2 0.0 all-to-all-done.1.parts_ref
  53.2 0.9 %join.1 = bf16[128,2048]{1,0:T(8,128)(2,1)} custom-call(bf16[8,2,128,128]{3,2,1,0:T(8,128)(2,1)S(1)} %all-to-all-done.1.parts_ref), custom_call_target="tpu_custom_call" | custom-call | tf_op jit(solution)/shard_map/join/pallas_call | solution.py:356
  (14 shorter events, 0.3 us)
Async XLA Ops:
  0.6 14.4 %copy-start = (f32[2048]{0:T(1024)S(1)}, f32[2048]{0:T(1024)}, u32[]{:S(2)}) copy-start(f32[2048]{0:T(1024)} %param.14) | copy-start | bytes 24580
  3.5 8.3 %collective-permute-start = (bf16[4,2,128,128]{3,2,1,0:T(8,128)(2,1)}, bf16[4,2,128,128]{3,2,1,0:T(8,128)(2,1)S(1)}, u32[]{:S(2)}, u32[]{:S(2)}) collective-permute-start(bf16[4,2,128,128]{3,2,1,0:T(8,128)(2,1)} %get-tuple-element.15), channel_id=1, source_target_pairs={{0,4},{1,5},{2,6},{3,7},{4,0},{5,1},{6,2},{7,3},{8,12},{9,13},{10,... | collective-permute-start | bytes 786440 | tf_op jit(solution)/shard_map/ppermute | solution.py:249
  3.6 7.0 %copy-start.1 = (bf16[128,2048]{1,0:T(8,128)(2,1)S(1)}, bf16[128,2048]{1,0:T(8,128)(2,1)}, u32[]{:S(2)}) copy-start(bf16[128,2048]{1,0:T(8,128)(2,1)} %x_ref.1) | copy-start | bytes 1572868
  3.6 31.2 %all-to-all-start = ((bf16[16,2,128,128]{3,2,1,0:T(8,128)(2,1)}), bf16[16,2,128,128]{3,2,1,0:T(8,128)(2,1)S(1)}, u32[]{:S(2)}, u32[]{:S(2)}) async-start(bf16[16,2,128,128]{3,2,1,0:T(8,128)(2,1)} %get-tuple-element.17), calls=%async_computation | async-start | bytes 2097152 | tf_op jit(solution)/shard_map/all_to_all | solution.py:317
  10.8 1.1 %copy-start.5 = (f32[32]{0:T(128)S(1)}, f32[32]{0:T(128)}, u32[]{:S(2)}) copy-start(f32[32]{0:T(128)} %param.13) | copy-start | bytes 388
  10.8 1.1 %copy-start.6 = (f32[32]{0:T(128)S(1)}, f32[32]{0:T(128)}, u32[]{:S(2)}) copy-start(f32[32]{0:T(128)} %param.12) | copy-start | bytes 388
  12.4 1.0 %copy-start.3 = (f32[32,2048]{1,0:T(8,128)S(1)}, f32[32,2048]{1,0:T(8,128)}, u32[]{:S(2)}) copy-start(f32[32,2048]{1,0:T(8,128)} %param.11) | copy-start | bytes 786436
  13.4 1.8 %copy-start.2 = (f32[128,64]{1,0:T(8,128)S(1)}, f32[128,64]{1,0:T(8,128)}, u32[]{:S(2)}) copy-start(f32[128,64]{1,0:T(8,128)} %constant.97.clone) | copy-start | bytes 98308
  13.4 13.3 %collective-permute-start.1 = (bf16[2,2,2,128,128]{4,3,2,1,0:T(8,128)(2,1)S(1)}, bf16[2,2,2,128,128]{4,3,2,1,0:T(8,128)(2,1)S(1)}, u32[]{:S(2)}, u32[]{:S(2)}) collective-permute-start(bf16[2,2,2,128,128]{4,3,2,1,0:T(8,128)(2,1)S(1)} %get-tuple-element.30), channel_id=1, source_target_pairs={{0,2},{1,3},{2,0},{3,1},{4,6},{5,7},{6,4},{7,5},{8,10},{9,11},{10,... | collective-permute-start | bytes 786440 | tf_op jit(solution)/shard_map/ppermute | solution.py:249
  15.6 0.8 %copy-start.4 = (f32[64,128]{1,0:T(8,128)S(1)}, f32[64,128]{1,0:T(8,128)}, u32[]{:S(2)}) copy-start(f32[64,128]{1,0:T(8,128)} %constant.98.clone) | copy-start | bytes 98308
  26.8 1.6 %collective-permute-start.2 = (bf16[1,4,2,128,128]{4,3,2,1,0:T(8,128)(2,1)S(1)}, bf16[1,4,2,128,128]{4,3,2,1,0:T(8,128)(2,1)S(1)}, u32[]{:S(2)}, u32[]{:S(2)}) collective-permute-start(bf16[1,4,2,128,128]{4,3,2,1,0:T(8,128)(2,1)S(1)} %get-tuple-element.29), channel_id=1, source_target_pairs={{0,1},{1,0},{2,3},{3,2},{4,5},{5,4},{6,7},{7,6},{8,9},{9,8},{10,11... | collective-permute-start | bytes 786440 | tf_op jit(solution)/shard_map/ppermute | solution.py:249
  26.9 0.7 %copy-start.7 = (s32[32]{0:T(128)S(1)}, s32[32]{0:T(128)}, u32[]{:S(2)}) copy-start(s32[32]{0:T(128)} %param.15) | copy-start | bytes 388
  38.1 15.1 %all-to-all-start.1 = ((bf16[8,2,128,128]{3,2,1,0:T(8,128)(2,1)}), bf16[8,2,128,128]{3,2,1,0:T(8,128)(2,1)S(1)}, u32[]{:S(2)}, u32[]{:S(2)}) async-start(bf16[8,2,128,128]{3,2,1,0:T(8,128)(2,1)} %get-tuple-element.25), calls=%async_computation.1 | async-start | bytes 1048576 | tf_op jit(solution)/shard_map/all_to_all | solution.py:347
  44.6 8.0 %collective-permute-start.3 = (f32[32,128]{1,0:T(8,128)S(1)}, f32[32,128]{1,0:T(8,128)S(1)}, u32[]{:S(2)}, u32[]{:S(2)}) collective-permute-start(f32[32,128]{1,0:T(8,128)S(1)} %slice_bitcast_fusion), channel_id=1, source_target_pairs={{0,8},{1,9},{2,10},{3,11},{4,12},{5,13},{6,14},{7,15},{8,0},{9,1},... | collective-permute-start | bytes 49160 | tf_op jit(solution)/shard_map/ppermute | solution.py:380

commit v9 on v7

--- a/solution.py
+++ b/solution.py
@@ -71,11 +71,10 @@
     gain_ref,
     left_g_ref,
     back_ref,
-    spectrum_ref,
+    taps_ref,
     step_ref,
     y_ref,
     states_ref,
-    slot_of,
     sums,
     states,
     high,
@@ -90,35 +89,36 @@
     n_own = n_src // 2
     own_base = place_ref[0] * n_own
     far_base = n_own - own_base
-    for slot in range(n_spans):
-        slot_of[place_ref[2 + slot]] = slot
     weight = weight_ref[...]
-    taps = jnp.dot(spectrum_ref[...], weight, precision=HIGHEST, preferred_element_type=F32)
-    taps_real, taps_imag = taps[:rows], taps[rows:]
+    taps_real, taps_imag = taps_ref[:rows], taps_ref[rows:]
     left = left_g_ref[...]
-    for source in range(n_own):
-        for part in range(2):
-            far = twice(side_by_side(g_ref, far_base + source, part))
-            sums[2 * (far_base + source) + part] = jnp.dot(
-                left[2 * rows :], far, preferred_element_type=F32
-            )
-            near = twice(side_by_side(g_ref, own_base + source, part))
-            of_g = jnp.dot(left, near, preferred_element_type=F32)
-            sums[2 * (own_base + source) + part] = of_g[2 * rows :]
-            g_real, g_imag = of_g[:rows], of_g[rows : 2 * rows]
-            y_real = halves(taps_real * g_real + taps_imag * g_imag)
-            y_imag = halves(taps_real * g_imag - taps_imag * g_real)
-            slot = 2 * source + part
-            high[slot, :rows] = y_real[0]
-            high[slot, rows:] = y_imag[0]
-            low[slot, :rows] = y_real[1]
-            low[slot, rows:] = y_imag[1]
+    def spread(slot, of_g):
+        sums[2 * own_base + slot] = of_g[2 * rows :]
+        g_real, g_imag = of_g[:rows], of_g[rows : 2 * rows]
+        y_real = halves(taps_real * g_real + taps_imag * g_imag)
+        y_imag = halves(taps_real * g_imag - taps_imag * g_real)
+        high[slot, :rows] = y_real[0]
+        high[slot, rows:] = y_imag[0]
+        low[slot, :rows] = y_real[1]
+        low[slot, rows:] = y_imag[1]
+
+    waiting = []
+    for slot in range(2 * n_own):
+        source, part = slot // 2, slot % 2
+        near = twice(side_by_side(g_ref, own_base + source, part))
+        waiting.append((slot, jnp.dot(left, near, preferred_element_type=F32)))
+        far = twice(side_by_side(g_ref, far_base + source, part))
+        sums[2 * far_base + slot] = jnp.dot(left[2 * rows :], far, preferred_element_type=F32)
+        if len(waiting) > 1:
+            spread(*waiting.pop(0))
+    for item in waiting:
+        spread(*item)
     step_real = jnp.broadcast_to(step_ref[0], (n_basis, lanes))
     step_imag = jnp.broadcast_to(step_ref[1], (n_basis, lanes))
     state_real = jnp.zeros((n_basis, lanes), F32)
     state_imag = jnp.zeros((n_basis, lanes), F32)
     for span in range(n_spans - 1, -1, -1):
-        slot = slot_of[span]
+        slot = place_ref[2 + span]
         states[slot, :n_basis] = state_real
         states[slot, n_basis:] = state_imag
         if span:
@@ -128,27 +128,33 @@
     gain = gain_ref[...]
     both_weight = twice(weight)
     leaving = []
-    for source in range(n_own):
-        for part in range(2):
-            slot = 2 * source + part
-            state = states[2 * own_base + slot]
-            states_ref[slot] = state
-            far = halves(both_weight * state)
-            both_high = jnp.concatenate([high[slot], far[0]], 0)
-            both_low = jnp.concatenate([low[slot], far[1]], 0)
-            by_high = jnp.dot(back_ref[...], both_high, preferred_element_type=F32)
-            value = (
-                (by_high[:rows] + by_high[rows:])
-                + jnp.dot(back_ref[:rows], both_low, preferred_element_type=F32)
-                + gain * side_by_side(g_ref, own_base + source, part).astype(F32)
-            ).astype(BF16)
-            at = slice(part * rows, (part + 1) * rows)
-            result[source, 0, at, :] = value[:, :width]
-            result[source, 1, at, :] = value[:, width:]
-        leaving.append(
-            pltpu.make_async_copy(result.at[source], y_ref.at[source], sems.at[source])
-        )
-        leaving[-1].start()
+    def finish(slot, by_high, by_low):
+        source, part = slot // 2, slot % 2
+        own = side_by_side(g_ref, own_base + source, part).astype(F32)
+        value = ((by_high[:rows] + by_high[rows:]) + by_low + gain * own).astype(BF16)
+        at = slice(part * rows, (part + 1) * rows)
+        result[source, 0, at, :] = value[:, :width]
+        result[source, 1, at, :] = value[:, width:]
+        if part:
+            leaving.append(
+                pltpu.make_async_copy(result.at[source], y_ref.at[source], sems.at[source])
+            )
+            leaving[-1].start()
+
+    waiting = []
+    for slot in range(2 * n_own):
+        state = states[2 * own_base + slot]
+        states_ref[slot] = state
+        far = halves(both_weight * state)
+        both_high = jnp.concatenate([high[slot], far[0]], 0)
+        both_low = jnp.concatenate([low[slot], far[1]], 0)
+        by_high = jnp.dot(back_ref[...], both_high, preferred_element_type=F32)
+        by_low = jnp.dot(back_ref[:rows], both_low, preferred_element_type=F32)
+        waiting.append((slot, by_high, by_low))
+        if len(waiting) > 1:
+            finish(*waiting.pop(0))
+    for item in waiting:
+        finish(*item)
     for move in leaving:
         move.wait()
 
@@ -220,20 +226,20 @@
         move.wait()
 
 
-def join_kernel(parts_ref, value_ref, sems):
-    n_own, groups, _, own = parts_ref.shape
-    moves = []
-    for source in range(n_own):
-        for group in range(groups):
-            at = (group * n_own + source) * own
-            moves.append(
-                pltpu.make_async_copy(
-                    parts_ref.at[source, group], value_ref.at[:, at : at + own], sems.at[source, group]
-                )
-            )
-    for move in moves:
-        move.start()
-    for move in moves:
+def join_kernel(parts_ref, value_ref, held, sems):
+    n_own, groups, rows_dev, own = parts_ref.shape
+    chunks = sems.shape[0]
+    rows = rows_dev // chunks
+    leaving = []
+    for chunk in range(chunks):
+        at = pl.ds(chunk * rows, rows)
+        for source in range(n_own):
+            for group in range(groups):
+                column = (group * n_own + source) * own
+                held[at, column : column + own] = parts_ref[source, group, at]
+        leaving.append(pltpu.make_async_copy(held.at[at], value_ref.at[at], sems.at[chunk]))
+        leaving[-1].start()
+    for move in leaving:
         move.wait()
 
 
@@ -290,8 +296,13 @@
         x_parts.append(widened(part))
     weight = own_blocks(filter_weight)
     gain = own_blocks(skip_gain[None, :])
-    place = jnp.concatenate([jnp.stack([half, rank]).astype(jnp.int32), span_of_slot])
+    slots = jnp.arange(2 * devices, dtype=jnp.int32)
+    slot_of_span = jnp.sum(
+        jnp.where(span_of_slot[None, :] == slots[:, None], slots[None, :], 0), 1, dtype=jnp.int32
+    )
+    place = jnp.concatenate([jnp.stack([half, rank]).astype(jnp.int32), slot_of_span])
     n_spans = 2 * devices
+    taps = jnp.dot(spectrum, weight, precision=HIGHEST, preferred_element_type=F32)
     smem = pl.BlockSpec(memory_space=pltpu.SMEM)
     vmem = pl.BlockSpec(memory_space=pltpu.VMEM)
     params = pltpu.CompilerParams(vmem_limit_bytes=24 * 2**20)
@@ -304,7 +315,6 @@
         in_specs=[smem] + [vmem] * 7,
         out_specs=(anywhere, vmem),
         scratch_shapes=[
-            pltpu.SMEM((n_spans,), jnp.int32),
             pltpu.VMEM((n_spans, 2 * n_basis, lanes), F32),
             pltpu.VMEM((n_spans, 2 * n_basis, lanes), F32),
             pltpu.VMEM((devices, 2 * rows, lanes), BF16),
@@ -315,7 +325,7 @@
         compiler_params=params,
         cost_estimate=pl.CostEstimate(flops=4*10**10, bytes_accessed=2**20, transcendentals=0),
         name="input_part",
-    )(place, g, weight, gain, left_g, back, spectrum, step)
+    )(place, g, weight, gain, left_g, back, taps, step)
     y = lax.all_to_all(
         y[..., :own],
         "seq",
@@ -328,9 +338,12 @@
         input_grad = pl.pallas_call(
             join_kernel,
             out_shape=jax.ShapeDtypeStruct((rows_dev, channels), BF16),
-            in_specs=[anywhere],
+            in_specs=[vmem],
             out_specs=anywhere,
-            scratch_shapes=[pltpu.SemaphoreType.DMA((n_own, 2))],
+            scratch_shapes=[
+                pltpu.VMEM((rows_dev, channels), BF16),
+                pltpu.SemaphoreType.DMA((4,)),
+            ],
             compiler_params=small,
             name="join",
         )(y)

time: 54.4 us -> 54.2 us (level)
  transfers between devices with their start and end apart: 10 -> 10, of which waited for: 2 -> 2; matrix products, arithmetic and copies ran while one was open for 10% -> 11% of each run, Pallas kernels for 9% -> 9%
where the time goes in v9:
time: 54.2 us; the launch traced here: 53.7 us
  starting transfers between devices  20.7 us (38%)
  waiting for transfers between devices  16.4 us (30%)
  Pallas kernels  7.74 us (14%)
  local copies, waits for them, and re-layouts  6.04 us (11%)
  other arithmetic  1.27 us (2%)
  between operations  1.03 us (2%)
    all_to_all x1, waiting for transfers between devices, on_device(): g = widened(lax.all_to_all(blocks, 'seq', 0, 0, tiled=True))  11 us
    ppermute x7, starting transfers between devices, on_device(): part = lax.ppermute(part, 'seq', [(i, i ^ offset) for i in range(devices)])  6.53 us
    all_to_all x1, starting transfers between devices, on_device(): g = widened(lax.all_to_all(blocks, 'seq', 0, 0, tiled=True))  6.44 us
    ppermute x1, waiting for transfers between devices, on_device(): lax.ppermute(wgrad[1], 'seq', [(i, i ^ n_own) for i in range(devices)])  5.35 us
    all_to_all x1, starting transfers between devices, on_device(): lax.all_to_all(y[..., :own], 'seq', 0, 0, tiled=True, axis_index_groups=[...  4.37 us
    unnamed x27, local copies, waits for them, and re-layouts  4.14 us
    ppermute x1, starting transfers between devices, on_device(): lax.ppermute(wgrad[1], 'seq', [(i, i ^ n_own) for i in range(devices)])  3.36 us
    pallas_call x1, Pallas kernels, on_device(): pl.pallas_call(input_kernel, out_shape=(jax.ShapeDtypeStruct((n_own, 2, r...  3.17 us
  transfers between devices with their start and end apart: 10, of which 2 were waited for; matrix products, arithmetic and copies ran while one was open for 11% of the time, Pallas kernels for 9%

profile of v9, /device:TPU:8, one launch (start us, length us, event | category | flops | bytes accessed | tf_op | source)
XLA Modules:
  0.0 53.7 jit_solution(16957434295131135889)
XLA Ops:
  0.6 0.0 copy-start
  0.6 2.0 %split.1 = bf16[16,2,128,128]{3,2,1,0:T(8,128)(2,1)} custom-call(bf16[128,2048]{1,0:T(8,128)(2,1)} %value_ref.1), custom_call_target="tpu_custom_call" | custom-call | tf_op jit(solution)/shard_map/split/pallas_call | solution.py:269
  2.7 0.0 copy-start.1
  2.7 6.4 %all-to-all-start = ((bf16[16,2,128,128]{3,2,1,0:T(8,128)(2,1)}), bf16[16,2,128,128]{3,2,1,0:T(8,128)(2,1)S(1)}, u32[]{:S(2)}, u32[]{:S(2)}) async-start(bf16[16,2,128,128]{3,2,1,0:T(8,128)(2,1)} %split.1), calls=%async_computation | async-start | bytes 2097152 | tf_op jit(solution)/shard_map/all_to_all | solution.py:286
  9.1 0.0 copy-start.2
  9.2 0.0 copy-start.5
  9.2 0.0 copy-start.6
  9.2 0.6 %copy-done.5 = f32[32]{0:T(128)S(1)} copy-done((f32[32]{0:T(128)S(1)}, f32[32]{0:T(128)}, u32[]{:S(2)}) %copy-start.5) | copy-done | bytes 152
  9.9 0.0 copy-done.6
  9.9 0.1 fusion.5
  10.0 0.0 copy-done.2
  10.0 0.2 fusion.10
  10.2 0.0 copy-done.1
  10.3 0.1 copy.61
  10.4 1.1 %constant_dynamic-slice_fusion = (bf16[128,2,1,128]{3,2,1,0:T(2,128)(2,1)S(1)}, bf16[128,2,1,128]{3,2,1,0:T(2,128)(2,1)S(1)}, bf16[128,2,1,128]{3,2,1,0:T(2,128)...) fusion(bf16[128,2,8,128]{3,2,1,0:T(8,128)(2,1)S(1)} %bitcast.77, ...), kind=kLoop, calls=%fused_computation.39 | loop fusion | bytes 1048608 | tf_op jit(solution)/shard_map/jit(dynamic_index_in_dim)/dynamic_slice | solution.py:292
  11.5 0.2 collective-permute-start
  11.8 1.5 %collective-permute-start.1 = (bf16[2,128,128]{2,1,0:T(8,128)(2,1)S(1)}, bf16[2,128,128]{2,1,0:T(8,128)(2,1)S(1)}, u32[]{:S(2)}, u32[]{:S(2)}) collective-permute-start(bf16[2,128,128]{2,1,0:T(8,128)(2,1)S(1)} %bitcast.86), channel_id=1, source_target_pairs={{0,2},{1,3},{2,0},{3,1},{4,6},{5,7},{6,4},{7,5},{8,10},{9,11},{10,... | collective-permute-start | bytes 196616 | tf_op jit(solution)/shard_map/ppermute | solution.py:295
  13.3 0.3 collective-permute-start.2
  13.6 0.4 collective-permute-start.3
  14.1 0.6 %copy.74 = bf16[128,2,1,128]{3,0,1,2:T(8,128)(2,1)} copy(bf16[128,2,1,128]{3,2,1,0:T(2,128)(2,1)S(1)} %get-tuple-element.12) | data formatting | bytes 131072
  14.7 0.0 copy-start.3
  14.7 1.4 %collective-permute-start.4 = (bf16[2,128,128]{2,1,0:T(8,128)(2,1)}, bf16[2,128,128]{2,1,0:T(8,128)(2,1)S(1)}, u32[]{:S(2)}, u32[]{:S(2)}) collective-permute-start(bf16[2,128,128]{2,1,0:T(8,128)(2,1)} %bitcast.67), channel_id=1, source_target_pairs={{0,5},{1,4},{2,7},{3,6},{4,1},{5,0},{6,3},{7,2},{8,13},{9,12},{10,... | collective-permute-start | bytes 196616 | tf_op jit(solution)/shard_map/ppermute | solution.py:295
  16.1 0.2 slice_reduce_fusion
  16.3 0.1 copy.40.step_ref
  16.4 0.1 fusion.13
  16.5 0.1 rev.8
  16.6 0.1 rev.9
  16.7 0.1 copy.39
  16.7 0.1 copy.38
  16.8 0.1 copy.49.spectrum_ref
  16.9 0.0 copy-done.3
  17.1 0.6 %copy.72 = bf16[128,2,1,128]{3,0,1,2:T(8,128)(2,1)} copy(bf16[128,2,1,128]{3,2,1,0:T(2,128)(2,1)S(1)} %get-tuple-element.10) | data formatting | bytes 131072
  17.7 0.6 %copy.73 = bf16[128,2,1,128]{3,0,1,2:T(8,128)(2,1)} copy(bf16[128,2,1,128]{3,2,1,0:T(2,128)(2,1)S(1)} %get-tuple-element.11) | data formatting | bytes 131072
  18.4 0.0 copy-done
  18.4 0.0 copy-start.7
  18.4 0.6 %copy-done.7 = s32[32]{0:T(128)S(1)} copy-done((s32[32]{0:T(128)S(1)}, s32[32]{0:T(128)}, u32[]{:S(2)}) %copy-start.7) | copy-done | bytes 152
  19.0 0.1 select_reduce_fusion
  19.2 0.1 pad_maximum_fusion.5.left_x_ref
  19.3 0.0 copy-start.4
  19.3 0.1 pad_maximum_fusion.4.left_g_ref
  19.4 0.7 %copy-done.4 = f32[64,128]{1,0:T(8,128)S(1)} copy-done((f32[64,128]{1,0:T(8,128)S(1)}, f32[64,128]{1,0:T(8,128)}, u32[]{:S(2)}) %copy-start.4) | copy-done | bytes 32792
  20.1 0.1 reduce-precision_convert_fusion.2
  20.2 0.3 fusion.12.taps_ref
  20.5 0.1 pad_add_fusion.place_ref
  20.6 0.0 collective-permute-done.refs_1_
  20.6 1.5 %collective-permute-start.5 = (bf16[2,128,128]{2,1,0:T(8,128)(2,1)}, bf16[2,128,128]{2,1,0:T(8,128)(2,1)S(1)}, u32[]{:S(2)}, u32[]{:S(2)}) collective-permute-start(bf16[2,128,128]{2,1,0:T(8,128)(2,1)} %bitcast.66), channel_id=1, source_target_pairs={{0,6},{1,7},{2,4},{3,5},{4,2},{5,3},{6,0},{7,1},{8,14},{9,15},{10,... | collective-permute-start | bytes 196616 | tf_op jit(solution)/shard_map/ppermute | solution.py:295
  22.0 0.0 collective-permute-done.1.refs_2_
  22.0 1.1 %collective-permute-start.6 = (bf16[2,128,128]{2,1,0:T(8,128)(2,1)}, bf16[2,128,128]{2,1,0:T(8,128)(2,1)S(1)}, u32[]{:S(2)}, u32[]{:S(2)}) collective-permute-start(bf16[2,128,128]{2,1,0:T(8,128)(2,1)} %bitcast.65), channel_id=1, source_target_pairs={{0,7},{1,6},{2,5},{3,4},{4,3},{5,2},{6,1},{7,0},{8,15},{9,14},{10,... | collective-permute-start | bytes 196616 | tf_op jit(solution)/shard_map/ppermute | solution.py:295
  23.2 11.0 %all-to-all-done.g_ref = bf16[16,2,128,128]{3,2,1,0:T(8,128)(2,1)S(1)} async-done(((bf16[16,2,128,128]{3,2,1,0:T(8,128)(2,1)}), bf16[16,2,128,128]{3,2,1,0:T(8,128)(2,1)S(1)}, u32[]{:S(2)}, u32[]{:S(2)}) %all-to-all-start) | async-done | bytes 1048608 | tf_op jit(solution)/shard_map/all_to_all | solution.py:286
  34.2 3.2 %input_part.1 = (bf16[8,2,128,128]{3,2,1,0:T(8,128)(2,1)}, f32[16,64,256]{2,1,0:T(8,128)S(1)}) custom-call(s32[34]{0:T(128)S(1)} %pad_add_fusion.place_ref, bf16[16,2,128,128]{3,2,1,0:T(8,128)(2,1)S(1)} %all-to-all-done.g_ref, f32[32,256]{1,0:T(8,128)S(1)} %bitcast.76, f32[1,256]{1,0:T(1,128)S(1)} %fusion.8.gain_ref, ...), custom_call_target="tpu_custom_call" | custom-call | flops 40000000000 | bytes 1048576 | tf_op jit(solution)/shard_map/input_part/pallas_call | solution.py:309
  37.4 4.4 %all-to-all-start.1 = ((bf16[8,2,128,128]{3,2,1,0:T(8,128)(2,1)}), bf16[8,2,128,128]{3,2,1,0:T(8,128)(2,1)S(1)}, u32[]{:S(2)}, u32[]{:S(2)}) async-start(bf16[8,2,128,128]{3,2,1,0:T(8,128)(2,1)} %get-tuple-element.7), calls=%async_computation.1 | async-start | bytes 1048576 | tf_op jit(solution)/shard_map/all_to_all | solution.py:329
  41.8 0.0 collective-permute-done.2.refs_3_
  41.8 0.0 collective-permute-done.3.refs_4_
  41.8 0.0 collective-permute-done.4.refs_5_
  41.8 0.0 collective-permute-done.5.refs_6_
  41.8 0.0 collective-permute-done.6.refs_7_
  41.8 1.7 %weight_part.1 = f32[2,32,128]{2,1,0:T(8,128)S(1)} custom-call(s32[34]{0:T(128)S(1)} %pad_add_fusion.place_ref, bf16[16,2,128,128]{3,2,1,0:T(8,128)(2,1)S(1)} %all-to-all-done.g_ref, f32[16,64,256]{2,1,0:T(8,128)S(1)} %get-tuple-element.8.states_ref, bf16[192,128]{1,0:T(8,128)(2,1)S(1)} %pad_maximum_fusion.4.left_g_ref, ...), custom_call_target="tpu_custom_call" | custom-call | flops 20132659200 | bytes 2097152 | tf_op jit(solution)/shard_map/weight_part/pallas_call | solution.py:352
  43.5 3.4 %collective-permute-start.7 = (f32[32,128]{1,0:T(8,128)S(1)}, f32[32,128]{1,0:T(8,128)S(1)}, u32[]{:S(2)}, u32[]{:S(2)}) collective-permute-start(f32[32,128]{1,0:T(8,128)S(1)} %slice_bitcast_fusion), channel_id=1, source_target_pairs={{0,8},{1,9},{2,10},{3,11},{4,12},{5,13},{6,14},{7,15},{8,0},{9,1},... | collective-permute-start | bytes 49160 | tf_op jit(solution)/shard_map/ppermute | solution.py:365
  46.9 5.3 %collective-permute-done.7 = f32[32,128]{1,0:T(8,128)S(1)} collective-permute-done((f32[32,128]{1,0:T(8,128)S(1)}, f32[32,128]{1,0:T(8,128)S(1)}, u32[]{:S(2)}, u32[]{:S(2)}) %collective-permute-start.7) | collective-permute-done | bytes 16416 | tf_op jit(solution)/shard_map/ppermute | solution.py:365
  52.2 0.6 %fusion.7 = f32[32,128]{1,0:T(8,128)} fusion(f32[32,128]{1,0:T(8,128)S(1)} %collective-permute-done.7, f32[2,32,128]{2,1,0:T(8,128)S(1)} %weight_part.1), kind=kLoop, calls=%fused_computation.32 | loop fusion | flops 4096 | bytes 49152 | tf_op jit(solution)/shard_map/add | solution.py:366
  52.8 0.0 all-to-all-done.1.parts_ref
  52.8 0.8 %join.1 = bf16[128,2048]{1,0:T(8,128)(2,1)} custom-call(bf16[8,2,128,128]{3,2,1,0:T(8,128)(2,1)S(1)} %all-to-all-done.1.parts_ref), custom_call_target="tpu_custom_call" | custom-call | tf_op jit(solution)/shard_map/join/pallas_call | solution.py:338
  (16 shorter events, 0.2 us)
Async XLA Ops:
  0.6 17.8 %copy-start = (f32[2048]{0:T(1024)S(1)}, f32[2048]{0:T(1024)}, u32[]{:S(2)}) copy-start(f32[2048]{0:T(1024)} %param.14) | copy-start | bytes 24580
  2.7 7.6 %copy-start.1 = (bf16[128,2048]{1,0:T(8,128)(2,1)S(1)}, bf16[128,2048]{1,0:T(8,128)(2,1)}, u32[]{:S(2)}) copy-start(bf16[128,2048]{1,0:T(8,128)(2,1)} %param.9) | copy-start | bytes 1572868
  2.7 31.5 %all-to-all-start = ((bf16[16,2,128,128]{3,2,1,0:T(8,128)(2,1)}), bf16[16,2,128,128]{3,2,1,0:T(8,128)(2,1)S(1)}, u32[]{:S(2)}, u32[]{:S(2)}) async-start(bf16[16,2,128,128]{3,2,1,0:T(8,128)(2,1)} %split.1), calls=%async_computation | async-start | bytes 2097152 | tf_op jit(solution)/shard_map/all_to_all | solution.py:286
  9.1 0.9 %copy-start.2 = (f32[128,64]{1,0:T(8,128)S(1)}, f32[128,64]{1,0:T(8,128)}, u32[]{:S(2)}) copy-start(f32[128,64]{1,0:T(8,128)} %constant.72.clone) | copy-start | bytes 98308
  9.2 0.7 %copy-start.5 = (f32[32]{0:T(128)S(1)}, f32[32]{0:T(128)}, u32[]{:S(2)}) copy-start(f32[32]{0:T(128)} %param.13) | copy-start | bytes 388
  9.2 0.7 %copy-start.6 = (f32[32]{0:T(128)S(1)}, f32[32]{0:T(128)}, u32[]{:S(2)}) copy-start(f32[32]{0:T(128)} %param.12) | copy-start | bytes 388
  11.5 9.0 %collective-permute-start = (bf16[2,128,128]{2,1,0:T(8,128)(2,1)S(1)}, bf16[2,128,128]{2,1,0:T(8,128)(2,1)S(1)}, u32[]{:S(2)}, u32[]{:S(2)}) collective-permute-start(bf16[2,128,128]{2,1,0:T(8,128)(2,1)S(1)} %bitcast.87), channel_id=1, source_target_pairs={{0,1},{1,0},{2,3},{3,2},{4,5},{5,4},{6,7},{7,6},{8,9},{9,8},{10,11... | collective-permute-start | bytes 196616 | tf_op jit(solution)/shard_map/ppermute | solution.py:295
  11.8 10.3 %collective-permute-start.1 = (bf16[2,128,128]{2,1,0:T(8,128)(2,1)S(1)}, bf16[2,128,128]{2,1,0:T(8,128)(2,1)S(1)}, u32[]{:S(2)}, u32[]{:S(2)}) collective-permute-start(bf16[2,128,128]{2,1,0:T(8,128)(2,1)S(1)} %bitcast.86), channel_id=1, source_target_pairs={{0,2},{1,3},{2,0},{3,1},{4,6},{5,7},{6,4},{7,5},{8,10},{9,11},{10,... | collective-permute-start | bytes 196616 | tf_op jit(solution)/shard_map/ppermute | solution.py:295
  13.3 28.4 %collective-permute-start.2 = (bf16[2,128,128]{2,1,0:T(8,128)(2,1)S(1)}, bf16[2,128,128]{2,1,0:T(8,128)(2,1)S(1)}, u32[]{:S(2)}, u32[]{:S(2)}) collective-permute-start(bf16[2,128,128]{2,1,0:T(8,128)(2,1)S(1)} %bitcast.84), channel_id=1, source_target_pairs={{0,3},{1,2},{2,1},{3,0},{4,7},{5,6},{6,5},{7,4},{8,11},{9,10},{10,... | collective-permute-start | bytes 196616 | tf_op jit(solution)/shard_map/ppermute | solution.py:295
  13.6 28.1 %collective-permute-start.3 = (bf16[2,128,128]{2,1,0:T(8,128)(2,1)S(1)}, bf16[2,128,128]{2,1,0:T(8,128)(2,1)S(1)}, u32[]{:S(2)}, u32[]{:S(2)}) collective-permute-start(bf16[2,128,128]{2,1,0:T(8,128)(2,1)S(1)} %bitcast.85), channel_id=1, source_target_pairs={{0,4},{1,5},{2,6},{3,7},{4,0},{5,1},{6,2},{7,3},{8,12},{9,13},{10,... | collective-permute-start | bytes 196616 | tf_op jit(solution)/shard_map/ppermute | solution.py:295
  14.7 2.3 %copy-start.3 = (f32[32,2048]{1,0:T(8,128)S(1)}, f32[32,2048]{1,0:T(8,128)}, u32[]{:S(2)}) copy-start(f32[32,2048]{1,0:T(8,128)} %param.11) | copy-start | bytes 786436
  14.7 27.1 %collective-permute-start.4 = (bf16[2,128,128]{2,1,0:T(8,128)(2,1)}, bf16[2,128,128]{2,1,0:T(8,128)(2,1)S(1)}, u32[]{:S(2)}, u32[]{:S(2)}) collective-permute-start(bf16[2,128,128]{2,1,0:T(8,128)(2,1)} %bitcast.67), channel_id=1, source_target_pairs={{0,5},{1,4},{2,7},{3,6},{4,1},{5,0},{6,3},{7,2},{8,13},{9,12},{10,... | collective-permute-start | bytes 196616 | tf_op jit(solution)/shard_map/ppermute | solution.py:295
  18.4 0.7 %copy-start.7 = (s32[32]{0:T(128)S(1)}, s32[32]{0:T(128)}, u32[]{:S(2)}) copy-start(s32[32]{0:T(128)} %param.15) | copy-start | bytes 388
  19.3 0.8 %copy-start.4 = (f32[64,128]{1,0:T(8,128)S(1)}, f32[64,128]{1,0:T(8,128)}, u32[]{:S(2)}) copy-start(f32[64,128]{1,0:T(8,128)} %constant.73.clone) | copy-start | bytes 98308
  20.6 21.2 %collective-permute-start.5 = (bf16[2,128,128]{2,1,0:T(8,128)(2,1)}, bf16[2,128,128]{2,1,0:T(8,128)(2,1)S(1)}, u32[]{:S(2)}, u32[]{:S(2)}) collective-permute-start(bf16[2,128,128]{2,1,0:T(8,128)(2,1)} %bitcast.66), channel_id=1, source_target_pairs={{0,6},{1,7},{2,4},{3,5},{4,2},{5,3},{6,0},{7,1},{8,14},{9,15},{10,... | collective-permute-start | bytes 196616 | tf_op jit(solution)/shard_map/ppermute | solution.py:295
  22.0 19.8 %collective-permute-start.6 = (bf16[2,128,128]{2,1,0:T(8,128)(2,1)}, bf16[2,128,128]{2,1,0:T(8,128)(2,1)S(1)}, u32[]{:S(2)}, u32[]{:S(2)}) collective-permute-start(bf16[2,128,128]{2,1,0:T(8,128)(2,1)} %bitcast.65), channel_id=1, source_target_pairs={{0,7},{1,6},{2,5},{3,4},{4,3},{5,2},{6,1},{7,0},{8,15},{9,14},{10,... | collective-permute-start | bytes 196616 | tf_op jit(solution)/shard_map/ppermute | solution.py:295
  37.4 15.5 %all-to-all-start.1 = ((bf16[8,2,128,128]{3,2,1,0:T(8,128)(2,1)}), bf16[8,2,128,128]{3,2,1,0:T(8,128)(2,1)S(1)}, u32[]{:S(2)}, u32[]{:S(2)}) async-start(bf16[8,2,128,128]{3,2,1,0:T(8,128)(2,1)} %get-tuple-element.7), calls=%async_computation.1 | async-start | bytes 1048576 | tf_op jit(solution)/shard_map/all_to_all | solution.py:329
  43.5 8.7 %collective-permute-start.7 = (f32[32,128]{1,0:T(8,128)S(1)}, f32[32,128]{1,0:T(8,128)S(1)}, u32[]{:S(2)}, u32[]{:S(2)}) collective-permute-start(f32[32,128]{1,0:T(8,128)S(1)} %slice_bitcast_fusion), channel_id=1, source_target_pairs={{0,8},{1,9},{2,10},{3,11},{4,12},{5,13},{6,14},{7,15},{8,0},{9,1},... | collective-permute-start | bytes 49160 | tf_op jit(solution)/shard_map/ppermute | solution.py:365

commit v10 on v9

--- a/solution.py
+++ b/solution.py
@@ -45,13 +45,17 @@
     back = jnp.concatenate(
         [inverse, power_real[:, :0:-1].T, -power_imag[:, :0:-1].T], 1
     )
-    back = jnp.concatenate(table_halves(back), 0)
+    back_high, back_low = table_halves(back)
+    back = jnp.concatenate([back_high, back_low], 0)
+    far = jnp.concatenate([back_high[:, 2 * rows :]] * 2 + [back_low[:, 2 * rows :]], 1)
     basis_spectrum = jnp.dot(
         forward, power_real[:, :rows].T, precision=HIGHEST, preferred_element_type=F32
     )
-    later_inputs, basis_spectrum = lax.optimization_barrier((inputs, basis_spectrum))
     step = jnp.stack([power_real[:, rows], power_imag[:, rows]], 0)[:, :, None]
-    return (left_g, left_x, back, basis_spectrum, step), later_inputs
+    later_inputs, left_g, back, far, basis_spectrum = lax.optimization_barrier(
+        (inputs, left_g, back, far, basis_spectrum)
+    )
+    return (left_g, left_x, back, far, basis_spectrum, step), later_inputs
 
 
 def side_by_side(ref, source, part):
@@ -71,6 +75,7 @@
     gain_ref,
     left_g_ref,
     back_ref,
+    far_ref,
     taps_ref,
     step_ref,
     y_ref,
@@ -79,6 +84,7 @@
     states,
     high,
     low,
+    nears,
     result,
     sems,
 ):
@@ -117,21 +123,40 @@
     step_imag = jnp.broadcast_to(step_ref[1], (n_basis, lanes))
     state_real = jnp.zeros((n_basis, lanes), F32)
     state_imag = jnp.zeros((n_basis, lanes), F32)
-    for span in range(n_spans - 1, -1, -1):
+    gain = gain_ref[...]
+    both_weight = twice(weight)
+    leaving = []
+
+    def descend(span, state_real, state_imag):
         slot = place_ref[2 + span]
         states[slot, :n_basis] = state_real
         states[slot, n_basis:] = state_imag
-        if span:
-            next_real = sums[slot, :n_basis] + step_real * state_real - step_imag * state_imag
-            state_imag = sums[slot, n_basis:] + step_real * state_imag + step_imag * state_real
-            state_real = next_real
-    gain = gain_ref[...]
-    both_weight = twice(weight)
-    leaving = []
-    def finish(slot, by_high, by_low):
+        if not span:
+            return state_real, state_imag
+        return (
+            sums[slot, :n_basis] + step_real * state_real - step_imag * state_imag,
+            sums[slot, n_basis:] + step_real * state_imag + step_imag * state_real,
+        )
+
+    def keep(slot, by_high, by_low):
+        own = side_by_side(g_ref, own_base + slot // 2, slot % 2).astype(F32)
+        nears[slot] = (by_high[:rows] + by_high[rows:]) + by_low + gain * own
+
+    waiting = []
+    for slot in range(2 * n_own):
+        by_high = jnp.dot(back_ref[:, : 2 * rows], high[slot], preferred_element_type=F32)
+        by_low = jnp.dot(back_ref[:rows, : 2 * rows], low[slot], preferred_element_type=F32)
+        waiting.append((slot, by_high, by_low))
+        for span in range(n_spans - 1 - 2 * slot, n_spans - 3 - 2 * slot, -1):
+            state_real, state_imag = descend(span, state_real, state_imag)
+        if len(waiting) > 1:
+            keep(*waiting.pop(0))
+    for item in waiting:
+        keep(*item)
+
+    def finish(slot, far):
         source, part = slot // 2, slot % 2
-        own = side_by_side(g_ref, own_base + source, part).astype(F32)
-        value = ((by_high[:rows] + by_high[rows:]) + by_low + gain * own).astype(BF16)
+        value = (nears[slot] + far).astype(BF16)
         at = slice(part * rows, (part + 1) * rows)
         result[source, 0, at, :] = value[:, :width]
         result[source, 1, at, :] = value[:, width:]
@@ -145,12 +170,13 @@
     for slot in range(2 * n_own):
         state = states[2 * own_base + slot]
         states_ref[slot] = state
-        far = halves(both_weight * state)
-        both_high = jnp.concatenate([high[slot], far[0]], 0)
-        both_low = jnp.concatenate([low[slot], far[1]], 0)
-        by_high = jnp.dot(back_ref[...], both_high, preferred_element_type=F32)
-        by_low = jnp.dot(back_ref[:rows], both_low, preferred_element_type=F32)
-        waiting.append((slot, by_high, by_low))
+        far_high, far_low = halves(both_weight * state)
+        far = jnp.dot(
+            far_ref[...],
+            jnp.concatenate([far_high, far_low, far_high], 0),
+            preferred_element_type=F32,
+        )
+        waiting.append((slot, far))
         if len(waiting) > 1:
             finish(*waiting.pop(0))
     for item in waiting:
@@ -285,7 +311,7 @@
         blocks = jnp.concatenate([blocks, blocks], 0)
     g = widened(lax.all_to_all(blocks, "seq", 0, 0, tiled=True))
     made, later_inputs = tables(rows, filter_rates, filter_freqs, inputs)
-    left_g, left_x, back, spectrum, step = made
+    left_g, left_x, back, far, spectrum, step = made
     x_blocks = later_inputs.reshape(rows_dev, 2, n_own, own)
     x_parts = []
     for offset in range(n_own):
@@ -312,20 +338,21 @@
             jax.ShapeDtypeStruct((n_own, 2, rows_dev, width), BF16),
             jax.ShapeDtypeStruct((devices, 2 * n_basis, lanes), F32),
         ),
-        in_specs=[smem] + [vmem] * 7,
+        in_specs=[smem] + [vmem] * 8,
         out_specs=(anywhere, vmem),
         scratch_shapes=[
             pltpu.VMEM((n_spans, 2 * n_basis, lanes), F32),
             pltpu.VMEM((n_spans, 2 * n_basis, lanes), F32),
             pltpu.VMEM((devices, 2 * rows, lanes), BF16),
             pltpu.VMEM((devices, 2 * rows, lanes), BF16),
+            pltpu.VMEM((devices, rows, lanes), F32),
             pltpu.VMEM((n_own, 2, rows_dev, width), BF16),
             pltpu.SemaphoreType.DMA((n_own,)),
         ],
         compiler_params=params,
         cost_estimate=pl.CostEstimate(flops=4*10**10, bytes_accessed=2**20, transcendentals=0),
         name="input_part",
-    )(place, g, weight, gain, left_g, back, taps, step)
+    )(place, g, weight, gain, left_g, back, far, taps, step)
     y = lax.all_to_all(
         y[..., :own],
         "seq",

time: 54.2 us -> 53.8 us (level)
  local copies, waits for them, and re-layouts: 6.04 us -> 6.66 us
  waiting for transfers between devices: 16.4 us -> 15.8 us
    unnamed x27, local copies, waits for them, and re-layouts: 4.14 us -> 4.77 us
    all_to_all x1, waiting for transfers between devices: 11 us -> 10.4 us  [on_device(): g = widened(lax.all_to_all(blocks, 'seq', 0, 0, tiled=True))]
  transfers between devices with their start and end apart: 10 -> 10, of which waited for: 2 -> 2; matrix products, arithmetic and copies ran while one was open for 11% -> 12% of each run, Pallas kernels for 9% -> 9%
where the time goes in v10:
time: 53.8 us; the launch traced here: 53.4 us
  starting transfers between devices  20.5 us (38%)
  waiting for transfers between devices  15.8 us (29%)
  Pallas kernels  7.62 us (14%)
  local copies, waits for them, and re-layouts  6.66 us (12%)
  other arithmetic  1.35 us (3%)
  between operations  0.99 us (2%)
    all_to_all x1, waiting for transfers between devices, on_device(): g = widened(lax.all_to_all(blocks, 'seq', 0, 0, tiled=True))  10.4 us
    ppermute x7, starting transfers between devices, on_device(): part = lax.ppermute(part, 'seq', [(i, i ^ offset) for i in range(devices)])  6.46 us
    all_to_all x1, starting transfers between devices, on_device(): g = widened(lax.all_to_all(blocks, 'seq', 0, 0, tiled=True))  6.31 us
    ppermute x1, waiting for transfers between devices, on_device(): lax.ppermute(wgrad[1], 'seq', [(i, i ^ n_own) for i in range(devices)])  5.35 us
    unnamed x27, local copies, waits for them, and re-layouts  4.77 us
    all_to_all x1, starting transfers between devices, on_device(): lax.all_to_all(y[..., :own], 'seq', 0, 0, tiled=True, axis_index_groups=[...  4.27 us
    ppermute x1, starting transfers between devices, on_device(): lax.ppermute(wgrad[1], 'seq', [(i, i ^ n_own) for i in range(devices)])  3.46 us
    pallas_call x1, Pallas kernels, on_device(): pl.pallas_call(input_kernel, out_shape=(jax.ShapeDtypeStruct((n_own, 2, r...  3.05 us
  transfers between devices with their start and end apart: 10, of which 2 were waited for; matrix products, arithmetic and copies ran while one was open for 12% of the time, Pallas kernels for 9%

profile of v10, /device:TPU:8, one launch (start us, length us, event | category | flops | bytes accessed | tf_op | source)
XLA Modules:
  0.0 53.4 jit_solution(11505265721786918031)
XLA Ops:
  0.6 0.0 copy-start
  0.6 2.0 %split.1 = bf16[16,2,128,128]{3,2,1,0:T(8,128)(2,1)} custom-call(bf16[128,2048]{1,0:T(8,128)(2,1)} %value_ref.1), custom_call_target="tpu_custom_call" | custom-call | tf_op jit(solution)/shard_map/split/pallas_call | solution.py:295
  2.7 6.3 %all-to-all-start = ((bf16[16,2,128,128]{3,2,1,0:T(8,128)(2,1)}), bf16[16,2,128,128]{3,2,1,0:T(8,128)(2,1)S(1)}, u32[]{:S(2)}, u32[]{:S(2)}) async-start(bf16[16,2,128,128]{3,2,1,0:T(8,128)(2,1)} %split.1), calls=%async_computation | async-start | bytes 2097152 | tf_op jit(solution)/shard_map/all_to_all | solution.py:312
  9.0 0.0 copy-start.5
  9.0 0.0 copy-start.6
  9.0 0.6 %copy-done.5 = f32[32]{0:T(128)S(1)} copy-done((f32[32]{0:T(128)S(1)}, f32[32]{0:T(128)}, u32[]{:S(2)}) %copy-start.5) | copy-done | bytes 152
  9.7 0.0 copy-done.6
  9.7 0.1 fusion.5
  9.8 0.1 fusion.13
  9.9 0.1 rev.9
  10.0 0.1 rev.8
  10.0 0.0 copy-start.2
  10.0 0.1 copy.39
  10.1 0.0 copy-start.4
  10.1 0.0 copy-start.1
  10.1 0.1 copy.38
  10.2 0.7 %copy-done.4 = f32[64,128]{1,0:T(8,128)S(1)} copy-done((f32[64,128]{1,0:T(8,128)S(1)}, f32[64,128]{1,0:T(8,128)}, u32[]{:S(2)}) %copy-start.4) | copy-done | bytes 32792
  10.9 0.1 reduce-precision_convert_fusion.2
  11.0 0.1 pad_maximum_fusion.6.far_ref
  11.1 0.0 copy-done.2
  11.1 0.1 pad_maximum_fusion.4.left_g_ref
  11.3 0.2 fusion.10
  11.5 0.0 copy-done.1
  11.5 0.1 copy.61
  11.6 1.1 %constant_dynamic-slice_fusion = (bf16[128,2,1,128]{3,2,1,0:T(2,128)(2,1)S(1)}, bf16[128,2,1,128]{3,2,1,0:T(2,128)(2,1)S(1)}, bf16[128,2,1,128]{3,2,1,0:T(2,128)...) fusion(bf16[128,2,8,128]{3,2,1,0:T(8,128)(2,1)S(1)} %bitcast.77, ...), kind=kLoop, calls=%fused_computation.40 | loop fusion | bytes 1048608 | tf_op jit(solution)/shard_map/jit(dynamic_index_in_dim)/dynamic_slice | solution.py:318
  12.8 0.2 collective-permute-start
  13.0 1.5 %collective-permute-start.1 = (bf16[2,128,128]{2,1,0:T(8,128)(2,1)S(1)}, bf16[2,128,128]{2,1,0:T(8,128)(2,1)S(1)}, u32[]{:S(2)}, u32[]{:S(2)}) collective-permute-start(bf16[2,128,128]{2,1,0:T(8,128)(2,1)S(1)} %bitcast.85), channel_id=1, source_target_pairs={{0,2},{1,3},{2,0},{3,1},{4,6},{5,7},{6,4},{7,5},{8,10},{9,11},{10,... | collective-permute-start | bytes 196616 | tf_op jit(solution)/shard_map/ppermute | solution.py:321
  14.6 0.3 collective-permute-start.2
  14.9 0.0 copy-start.3
  14.9 0.6 %copy.75 = bf16[128,2,1,128]{3,0,1,2:T(8,128)(2,1)} copy(bf16[128,2,1,128]{3,2,1,0:T(2,128)(2,1)S(1)} %get-tuple-element.19) | data formatting | bytes 131072
  15.5 0.4 collective-permute-start.3
  15.9 0.6 %copy.74 = bf16[128,2,1,128]{3,0,1,2:T(8,128)(2,1)} copy(bf16[128,2,1,128]{3,2,1,0:T(2,128)(2,1)S(1)} %get-tuple-element.18) | data formatting | bytes 131072
  16.5 1.4 %collective-permute-start.4 = (bf16[2,128,128]{2,1,0:T(8,128)(2,1)}, bf16[2,128,128]{2,1,0:T(8,128)(2,1)S(1)}, u32[]{:S(2)}, u32[]{:S(2)}) collective-permute-start(bf16[2,128,128]{2,1,0:T(8,128)(2,1)} %bitcast.67), channel_id=1, source_target_pairs={{0,5},{1,4},{2,7},{3,6},{4,1},{5,0},{6,3},{7,2},{8,13},{9,12},{10,... | collective-permute-start | bytes 196616 | tf_op jit(solution)/shard_map/ppermute | solution.py:321
  17.9 0.2 slice_reduce_fusion
  18.1 0.1 copy.40.step_ref
  18.2 0.1 copy.49.spectrum_ref
  18.3 0.0 copy-done.3
  18.4 0.6 %copy.72 = bf16[128,2,1,128]{3,0,1,2:T(8,128)(2,1)} copy(bf16[128,2,1,128]{3,2,1,0:T(2,128)(2,1)S(1)} %get-tuple-element.16) | data formatting | bytes 131072
  19.1 0.6 %copy.73 = bf16[128,2,1,128]{3,0,1,2:T(8,128)(2,1)} copy(bf16[128,2,1,128]{3,2,1,0:T(2,128)(2,1)S(1)} %get-tuple-element.17) | data formatting | bytes 131072
  19.8 0.0 copy-done
  19.8 0.0 copy-start.7
  19.8 0.6 %copy-done.7 = s32[32]{0:T(128)S(1)} copy-done((s32[32]{0:T(128)S(1)}, s32[32]{0:T(128)}, u32[]{:S(2)}) %copy-start.7) | copy-done | bytes 152
  20.4 0.1 select_reduce_fusion
  20.5 0.1 pad_maximum_fusion.5.left_x_ref
  20.6 0.3 fusion.12.taps_ref
  20.9 0.1 pad_add_fusion.place_ref
  21.0 0.0 collective-permute-done.refs_1_
  21.0 1.5 %collective-permute-start.5 = (bf16[2,128,128]{2,1,0:T(8,128)(2,1)}, bf16[2,128,128]{2,1,0:T(8,128)(2,1)S(1)}, u32[]{:S(2)}, u32[]{:S(2)}) collective-permute-start(bf16[2,128,128]{2,1,0:T(8,128)(2,1)} %bitcast.66), channel_id=1, source_target_pairs={{0,6},{1,7},{2,4},{3,5},{4,2},{5,3},{6,0},{7,1},{8,14},{9,15},{10,... | collective-permute-start | bytes 196616 | tf_op jit(solution)/shard_map/ppermute | solution.py:321
  22.5 0.0 collective-permute-done.1.refs_2_
  22.5 1.1 %collective-permute-start.6 = (bf16[2,128,128]{2,1,0:T(8,128)(2,1)}, bf16[2,128,128]{2,1,0:T(8,128)(2,1)S(1)}, u32[]{:S(2)}, u32[]{:S(2)}) collective-permute-start(bf16[2,128,128]{2,1,0:T(8,128)(2,1)} %bitcast.65), channel_id=1, source_target_pairs={{0,7},{1,6},{2,5},{3,4},{4,3},{5,2},{6,1},{7,0},{8,15},{9,14},{10,... | collective-permute-start | bytes 196616 | tf_op jit(solution)/shard_map/ppermute | solution.py:321
  23.6 10.4 %all-to-all-done.g_ref = bf16[16,2,128,128]{3,2,1,0:T(8,128)(2,1)S(1)} async-done(((bf16[16,2,128,128]{3,2,1,0:T(8,128)(2,1)}), bf16[16,2,128,128]{3,2,1,0:T(8,128)(2,1)S(1)}, u32[]{:S(2)}, u32[]{:S(2)}) %all-to-all-start) | async-done | bytes 1048608 | tf_op jit(solution)/shard_map/all_to_all | solution.py:312
  34.1 3.1 %input_part.1 = (bf16[8,2,128,128]{3,2,1,0:T(8,128)(2,1)}, f32[16,64,256]{2,1,0:T(8,128)S(1)}) custom-call(s32[34]{0:T(128)S(1)} %pad_add_fusion.place_ref, bf16[16,2,128,128]{3,2,1,0:T(8,128)(2,1)S(1)} %all-to-all-done.g_ref, f32[32,256]{1,0:T(8,128)S(1)} %bitcast.76, f32[1,256]{1,0:T(1,128)S(1)} %fusion.8.gain_ref, ...), custom_call_target="tpu_custom_call" | custom-call | flops 40000000000 | bytes 1048576 | tf_op jit(solution)/shard_map/input_part/pallas_call | solution.py:335
  37.1 4.3 %all-to-all-start.1 = ((bf16[8,2,128,128]{3,2,1,0:T(8,128)(2,1)}), bf16[8,2,128,128]{3,2,1,0:T(8,128)(2,1)S(1)}, u32[]{:S(2)}, u32[]{:S(2)}) async-start(bf16[8,2,128,128]{3,2,1,0:T(8,128)(2,1)} %get-tuple-element.13), calls=%async_computation.1 | async-start | bytes 1048576 | tf_op jit(solution)/shard_map/all_to_all | solution.py:356
  41.4 0.0 collective-permute-done.2.refs_3_
  41.4 0.0 collective-permute-done.3.refs_4_
  41.4 0.0 collective-permute-done.4.refs_5_
  41.4 0.0 collective-permute-done.5.refs_6_
  41.4 0.0 collective-permute-done.6.refs_7_
  41.4 1.7 %weight_part.1 = f32[2,32,128]{2,1,0:T(8,128)S(1)} custom-call(s32[34]{0:T(128)S(1)} %pad_add_fusion.place_ref, bf16[16,2,128,128]{3,2,1,0:T(8,128)(2,1)S(1)} %all-to-all-done.g_ref, f32[16,64,256]{2,1,0:T(8,128)S(1)} %get-tuple-element.14.states_ref, bf16[192,128]{1,0:T(8,128)(2,1)S(1)} %pad_maximum_fusion.4.left_g_ref, ...), custom_call_target="tpu_custom_call" | custom-call | flops 20132659200 | bytes 2097152 | tf_op jit(solution)/shard_map/weight_part/pallas_call | solution.py:379
  43.2 3.5 %collective-permute-start.7 = (f32[32,128]{1,0:T(8,128)S(1)}, f32[32,128]{1,0:T(8,128)S(1)}, u32[]{:S(2)}, u32[]{:S(2)}) collective-permute-start(f32[32,128]{1,0:T(8,128)S(1)} %slice_bitcast_fusion), channel_id=1, source_target_pairs={{0,8},{1,9},{2,10},{3,11},{4,12},{5,13},{6,14},{7,15},{8,0},{9,1},... | collective-permute-start | bytes 49160 | tf_op jit(solution)/shard_map/ppermute | solution.py:392
  46.6 5.3 %collective-permute-done.7 = f32[32,128]{1,0:T(8,128)S(1)} collective-permute-done((f32[32,128]{1,0:T(8,128)S(1)}, f32[32,128]{1,0:T(8,128)S(1)}, u32[]{:S(2)}, u32[]{:S(2)}) %collective-permute-start.7) | collective-permute-done | bytes 16416 | tf_op jit(solution)/shard_map/ppermute | solution.py:392
  52.0 0.6 %fusion.7 = f32[32,128]{1,0:T(8,128)} fusion(f32[32,128]{1,0:T(8,128)S(1)} %collective-permute-done.7, f32[2,32,128]{2,1,0:T(8,128)S(1)} %weight_part.1), kind=kLoop, calls=%fused_computation.33 | loop fusion | flops 4096 | bytes 49152 | tf_op jit(solution)/shard_map/add | solution.py:393
  52.6 0.0 all-to-all-done.1.parts_ref
  52.6 0.8 %join.1 = bf16[128,2048]{1,0:T(8,128)(2,1)} custom-call(bf16[8,2,128,128]{3,2,1,0:T(8,128)(2,1)S(1)} %all-to-all-done.1.parts_ref), custom_call_target="tpu_custom_call" | custom-call | tf_op jit(solution)/shard_map/join/pallas_call | solution.py:365
  (17 shorter events, 0.2 us)
Async XLA Ops:
  0.6 19.1 %copy-start = (f32[2048]{0:T(1024)S(1)}, f32[2048]{0:T(1024)}, u32[]{:S(2)}) copy-start(f32[2048]{0:T(1024)} %param.14) | copy-start | bytes 24580
  2.7 31.4 %all-to-all-start = ((bf16[16,2,128,128]{3,2,1,0:T(8,128)(2,1)}), bf16[16,2,128,128]{3,2,1,0:T(8,128)(2,1)S(1)}, u32[]{:S(2)}, u32[]{:S(2)}) async-start(bf16[16,2,128,128]{3,2,1,0:T(8,128)(2,1)} %split.1), calls=%async_computation | async-start | bytes 2097152 | tf_op jit(solution)/shard_map/all_to_all | solution.py:312
  9.0 0.7 %copy-start.5 = (f32[32]{0:T(128)S(1)}, f32[32]{0:T(128)}, u32[]{:S(2)}) copy-start(f32[32]{0:T(128)} %param.13) | copy-start | bytes 388
  9.0 0.7 %copy-start.6 = (f32[32]{0:T(128)S(1)}, f32[32]{0:T(128)}, u32[]{:S(2)}) copy-start(f32[32]{0:T(128)} %param.12) | copy-start | bytes 388
  10.0 1.1 %copy-start.2 = (f32[128,64]{1,0:T(8,128)S(1)}, f32[128,64]{1,0:T(8,128)}, u32[]{:S(2)}) copy-start(f32[128,64]{1,0:T(8,128)} %constant.72.clone) | copy-start | bytes 98308
  10.1 0.8 %copy-start.4 = (f32[64,128]{1,0:T(8,128)S(1)}, f32[64,128]{1,0:T(8,128)}, u32[]{:S(2)}) copy-start(f32[64,128]{1,0:T(8,128)} %constant.73.clone) | copy-start | bytes 98308
  10.1 1.3 %copy-start.1 = (bf16[128,2048]{1,0:T(8,128)(2,1)S(1)}, bf16[128,2048]{1,0:T(8,128)(2,1)}, u32[]{:S(2)}) copy-start(bf16[128,2048]{1,0:T(8,128)(2,1)} %param.9) | copy-start | bytes 1572868
  12.8 8.3 %collective-permute-start = (bf16[2,128,128]{2,1,0:T(8,128)(2,1)S(1)}, bf16[2,128,128]{2,1,0:T(8,128)(2,1)S(1)}, u32[]{:S(2)}, u32[]{:S(2)}) collective-permute-start(bf16[2,128,128]{2,1,0:T(8,128)(2,1)S(1)} %bitcast.86), channel_id=1, source_target_pairs={{0,1},{1,0},{2,3},{3,2},{4,5},{5,4},{6,7},{7,6},{8,9},{9,8},{10,11... | collective-permute-start | bytes 196616 | tf_op jit(solution)/shard_map/ppermute | solution.py:321
  13.0 9.5 %collective-permute-start.1 = (bf16[2,128,128]{2,1,0:T(8,128)(2,1)S(1)}, bf16[2,128,128]{2,1,0:T(8,128)(2,1)S(1)}, u32[]{:S(2)}, u32[]{:S(2)}) collective-permute-start(bf16[2,128,128]{2,1,0:T(8,128)(2,1)S(1)} %bitcast.85), channel_id=1, source_target_pairs={{0,2},{1,3},{2,0},{3,1},{4,6},{5,7},{6,4},{7,5},{8,10},{9,11},{10,... | collective-permute-start | bytes 196616 | tf_op jit(solution)/shard_map/ppermute | solution.py:321
  14.6 26.8 %collective-permute-start.2 = (bf16[2,128,128]{2,1,0:T(8,128)(2,1)S(1)}, bf16[2,128,128]{2,1,0:T(8,128)(2,1)S(1)}, u32[]{:S(2)}, u32[]{:S(2)}) collective-permute-start(bf16[2,128,128]{2,1,0:T(8,128)(2,1)S(1)} %bitcast.84), channel_id=1, source_target_pairs={{0,3},{1,2},{2,1},{3,0},{4,7},{5,6},{6,5},{7,4},{8,11},{9,10},{10,... | collective-permute-start | bytes 196616 | tf_op jit(solution)/shard_map/ppermute | solution.py:321
  14.9 3.5 %copy-start.3 = (f32[32,2048]{1,0:T(8,128)S(1)}, f32[32,2048]{1,0:T(8,128)}, u32[]{:S(2)}) copy-start(f32[32,2048]{1,0:T(8,128)} %param.11) | copy-start | bytes 786436
  15.5 25.9 %collective-permute-start.3 = (bf16[2,128,128]{2,1,0:T(8,128)(2,1)}, bf16[2,128,128]{2,1,0:T(8,128)(2,1)S(1)}, u32[]{:S(2)}, u32[]{:S(2)}) collective-permute-start(bf16[2,128,128]{2,1,0:T(8,128)(2,1)} %bitcast.68), channel_id=1, source_target_pairs={{0,4},{1,5},{2,6},{3,7},{4,0},{5,1},{6,2},{7,3},{8,12},{9,13},{10,... | collective-permute-start | bytes 196616 | tf_op jit(solution)/shard_map/ppermute | solution.py:321
  16.5 24.9 %collective-permute-start.4 = (bf16[2,128,128]{2,1,0:T(8,128)(2,1)}, bf16[2,128,128]{2,1,0:T(8,128)(2,1)S(1)}, u32[]{:S(2)}, u32[]{:S(2)}) collective-permute-start(bf16[2,128,128]{2,1,0:T(8,128)(2,1)} %bitcast.67), channel_id=1, source_target_pairs={{0,5},{1,4},{2,7},{3,6},{4,1},{5,0},{6,3},{7,2},{8,13},{9,12},{10,... | collective-permute-start | bytes 196616 | tf_op jit(solution)/shard_map/ppermute | solution.py:321
  19.8 0.7 %copy-start.7 = (s32[32]{0:T(128)S(1)}, s32[32]{0:T(128)}, u32[]{:S(2)}) copy-start(s32[32]{0:T(128)} %param.15) | copy-start | bytes 388
  21.0 20.4 %collective-permute-start.5 = (bf16[2,128,128]{2,1,0:T(8,128)(2,1)}, bf16[2,128,128]{2,1,0:T(8,128)(2,1)S(1)}, u32[]{:S(2)}, u32[]{:S(2)}) collective-permute-start(bf16[2,128,128]{2,1,0:T(8,128)(2,1)} %bitcast.66), channel_id=1, source_target_pairs={{0,6},{1,7},{2,4},{3,5},{4,2},{5,3},{6,0},{7,1},{8,14},{9,15},{10,... | collective-permute-start | bytes 196616 | tf_op jit(solution)/shard_map/ppermute | solution.py:321
  22.5 18.9 %collective-permute-start.6 = (bf16[2,128,128]{2,1,0:T(8,128)(2,1)}, bf16[2,128,128]{2,1,0:T(8,128)(2,1)S(1)}, u32[]{:S(2)}, u32[]{:S(2)}) collective-permute-start(bf16[2,128,128]{2,1,0:T(8,128)(2,1)} %bitcast.65), channel_id=1, source_target_pairs={{0,7},{1,6},{2,5},{3,4},{4,3},{5,2},{6,1},{7,0},{8,15},{9,14},{10,... | collective-permute-start | bytes 196616 | tf_op jit(solution)/shard_map/ppermute | solution.py:321
  37.1 15.4 %all-to-all-start.1 = ((bf16[8,2,128,128]{3,2,1,0:T(8,128)(2,1)}), bf16[8,2,128,128]{3,2,1,0:T(8,128)(2,1)S(1)}, u32[]{:S(2)}, u32[]{:S(2)}) async-start(bf16[8,2,128,128]{3,2,1,0:T(8,128)(2,1)} %get-tuple-element.13), calls=%async_computation.1 | async-start | bytes 1048576 | tf_op jit(solution)/shard_map/all_to_all | solution.py:356
  43.2 8.8 %collective-permute-start.7 = (f32[32,128]{1,0:T(8,128)S(1)}, f32[32,128]{1,0:T(8,128)S(1)}, u32[]{:S(2)}, u32[]{:S(2)}) collective-permute-start(f32[32,128]{1,0:T(8,128)S(1)} %slice_bitcast_fusion), channel_id=1, source_target_pairs={{0,8},{1,9},{2,10},{3,11},{4,12},{5,13},{6,14},{7,15},{8,0},{9,1},... | collective-permute-start | bytes 49160 | tf_op jit(solution)/shard_map/ppermute | solution.py:392
